TPU v7x, 32 devices: a whole 2x2x4 slice. The times are simulated.
32 devices in a mesh: seq: 16 (over z, y, x), head: 2 (over core).
Axes of the slice: x: 2, y: 2, z: 4, core: 2. Of those that a mesh axis runs over, the one named last changes fastest.
Arguments:
- block_in: bfloat16 [8192, 768], P(('seq', 'head')), may hold values from -6 to 6
- grad_out: bfloat16 [8192, 768], P(('seq', 'head')), may hold values from -6 to 6
- lengths: int32 [2], replicated, may hold values from 1024 to 4096, as said below
- norm_gain: float32 [768], replicated, may hold values from 0.25 to 1.75
- w_in: bfloat16 [768, 3352], replicated, may hold values from -0.21875 to 0.21875
- conv_w: float32 [4, 1792], replicated, may hold values from -3 to 3
- conv_b: float32 [1792], replicated, may hold values from -0.5 to 0.5
- dt_bias: float32 [24], replicated, may hold values from -6 to -3.5
- a_log: float32 [24], replicated, may hold values from -10.5 to 1.4
- d_skip: float32 [24], replicated, may hold values from 0.5 to 2
- gate_gain: float32 [1536], replicated, may hold values from 0.25 to 1.75
- w_out: bfloat16 [1536, 768], replicated, may hold values from -0.15625 to 0.15625
Outputs:
- block_out: bfloat16 [8192, 768], P(('seq', 'head'))
- grad_in: float32 [8192, 768], P(('seq', 'head'))
- grad_norm_gain: float32 [768], replicated
- grad_w_in: float32 [768, 3352], replicated
- grad_conv_w: float32 [4, 1792], replicated
- grad_conv_b: float32 [1792], replicated
- grad_dt_bias: float32 [24], replicated
- grad_a_log: float32 [24], replicated
- grad_d_skip: float32 [24], replicated
- grad_gate_gain: float32 [1536], replicated
- grad_w_out: float32 [1536, 768], replicated
Inputs may be any that keep to these rules, and one draw needn't show every extreme that they name: lengths[s] counts the valid slots at the start of sequence s, the rest being padding; at least one sequence is valid in all 4096 slots.
All inputs are finite; a program needn't handle non-finite values.
Results may differ from a plain program's by a relative error of at most 0.012.
The roundings to bfloat16 on the way count: a program that leaves them out, or rounds other values in their place, can miss the bound.
Values may be sent and summed in bfloat16 or wider, within the bound.
A program may use at most 320 MiB of HBM per device.

v0:
```python
from functools import partial

import jax
import jax.numpy as jnp
from jax import lax
from jax.sharding import PartitionSpec as P

INNER = 1536
HEADS = 24
HEAD_DIM = 64
STATE = 128
CONV = 4
BLOCK = 256
SEQS = 2


eps_norm = 1e-05
best = lax.Precision.HIGHEST


def passed_along(value, axis, steps):
    count = lax.axis_size(axis)
    initial, last = (max(0, -steps), min(count, count - steps))
    return lax.ppermute(value, axis, [(source, source + steps) for source in range(initial, last)])


def entering(part, axis, combine, identity, reverse):
    count = lax.axis_size(axis)
    place = lax.axis_index(axis)
    ahead = count - 1 - place if reverse else place
    gathered = jax.tree.map(lambda a: lax.all_gather(a, axis), part)
    state = jax.tree.map(lambda a, e: jnp.zeros_like(a) + jnp.asarray(e, a.dtype), part, identity)

    def one(turn, state):
        source = count - 1 - turn if reverse else turn
        return combine(
            state, jax.tree.map(lambda a: lax.dynamic_index_in_dim(a, source, 0, False), gathered)
        )

    return lax.fori_loop(0, ahead, one, state)


def inverse_rms(values):
    return lax.rsqrt(jnp.mean(values * values, axis=-1, keepdims=True) + eps_norm)


def norm_backward(values, scaling, gain_vec, gradient):
    weighted = gradient * gain_vec
    average = jnp.mean(weighted * values, axis=-1, keepdims=True)
    grad_values = scaling * weighted - values * (scaling * scaling * scaling) * average
    grad_gain = jnp.sum(gradient * values * scaling, axis=0)
    return (grad_values, grad_gain)


def causal_conv(edge_rows, fresh_rows, weights, offset):
    length = fresh_rows.shape[0]
    joined = jnp.concatenate([edge_rows, fresh_rows], axis=0)
    running = offset + joined[0:length] * weights[0]
    for position in range(1, CONV):
        running = running + joined[position : position + length] * weights[position]
    return running


def prepare(
    x_raw,
    bc_raw,
    dt_raw,
    edge_x,
    edge_bc,
    conv_x,
    conv_bc,
    bias_x,
    bias_bc,
    dt_shift,
    a_log_part,
    valid_mask,
):
    keep_mask = valid_mask[:, None]
    x_flat = jax.nn.silu(causal_conv(edge_x, x_raw, conv_x, bias_x)) * keep_mask
    act_bc = jax.nn.silu(causal_conv(edge_bc, bc_raw, conv_bc, bias_bc))
    dt_rows = jax.nn.softplus(dt_raw + dt_shift) * keep_mask
    rates = -jnp.exp(a_log_part)
    x_heads = x_flat.reshape(x_flat.shape[0], -1, HEAD_DIM)
    return (x_heads, act_bc[:, :STATE], act_bc[:, STATE:], dt_rows, rates)


def block_step(rates, carry_state, inputs):
    x_heads, b_rows, c_rows, dt_rows = inputs
    block_len = dt_rows.shape[0]
    cumulative = jnp.cumsum(dt_rows, axis=0) * rates
    indices = jnp.arange(block_len)
    causal = (indices[:, None] >= indices[None, :])[:, :, None]
    spread = cumulative[:, None, :] - cumulative[None, :, :]
    decays = jnp.where(causal, jnp.exp(jnp.where(causal, spread, 0.0)), 0.0)
    scores = jnp.dot(c_rows, b_rows.T, precision=best)
    weight = decays * scores[:, :, None] * dt_rows[None, :, :]
    inner_part = jnp.einsum("tuh,uhp->thp", weight, x_heads, precision=best)
    carried = jnp.exp(cumulative)[:, :, None] * jnp.einsum(
        "tn,hpn->thp", c_rows, carry_state, precision=best
    )
    to_end = jnp.exp(cumulative[-1:] - cumulative) * dt_rows
    fresh_state = jnp.einsum("uh,uhp,un->hpn", to_end, x_heads, b_rows, precision=best)
    carry_state = jnp.exp(cumulative[-1])[:, None, None] * carry_state + fresh_state
    return (carry_state, inner_part + carried)


def mixer(
    valid_mask,
    x_raw,
    bc_raw,
    dt_raw,
    edge_x,
    edge_bc,
    conv_x,
    conv_bc,
    bias_x,
    bias_bc,
    dt_shift,
    a_log_part,
    skip_part,
    incoming,
):
    x_heads, b_rows, c_rows, dt_rows, rates = prepare(
        x_raw,
        bc_raw,
        dt_raw,
        edge_x,
        edge_bc,
        conv_x,
        conv_bc,
        bias_x,
        bias_bc,
        dt_shift,
        a_log_part,
        valid_mask,
    )
    blocks_count = x_heads.shape[0] // BLOCK

    def blocks(values):
        return values.reshape((blocks_count, BLOCK) + values.shape[1:])

    final_state, outputs = lax.scan(
        partial(block_step, rates),
        incoming,
        (blocks(x_heads), blocks(b_rows), blocks(c_rows), blocks(dt_rows)),
    )
    mixed_rows = outputs.reshape(x_heads.shape) + x_heads * skip_part[:, None]
    return (mixed_rows.reshape(x_heads.shape[0], -1), final_state)


def chain(earlier, later):
    return (earlier[0] * later[0], later[0][..., None, None] * earlier[1] + later[1])


def place_into(piece, full_len, start):
    full_shape = piece.shape[:-1] + (full_len,)
    return lax.dynamic_update_slice_in_dim(
        jnp.zeros(full_shape, jnp.float32), piece, start, piece.ndim - 1
    )


def local(
    block_in,
    grad_out,
    lengths,
    norm_gain,
    w_in,
    conv_w,
    conv_b,
    dt_bias,
    a_log,
    d_skip,
    gate_gain,
    w_out,
):
    tokens = block_in.shape[0]
    groups = lax.axis_size("head")
    group_idx = lax.axis_index("head")
    cycle_len = lax.axis_size("seq")
    cycle_idx = lax.axis_index("seq")
    per_seq = cycle_len // SEQS
    heads_here = HEADS // groups
    width_here = heads_here * HEAD_DIM
    local_len = tokens * groups
    cycle_place = cycle_idx // SEQS
    seq_id = cycle_idx % SEQS
    seq_onehot = jnp.arange(SEQS) == seq_id
    seq_valid = jnp.sum(jnp.where(seq_onehot, lengths, 0))
    is_start = cycle_place == 0
    is_last = cycle_place == per_seq - 1
    first_slot = cycle_place * local_len
    valid_heads = (first_slot + jnp.arange(local_len) < seq_valid).astype(jnp.float32)
    valid_tokens = (first_slot + group_idx * tokens + jnp.arange(tokens) < seq_valid).astype(
        jnp.float32
    )
    source = block_in.astype(jnp.float32)
    in_scale = inverse_rms(source)
    normed = (source * in_scale * norm_gain).astype(jnp.bfloat16)
    projected = jnp.dot(normed, w_in, preferred_element_type=jnp.float32).astype(jnp.bfloat16)
    gate_in = projected[:, :INNER].astype(jnp.float32)
    x_part = projected[:, INNER : 2 * INNER].reshape(tokens, groups, width_here)
    bc_part = jnp.broadcast_to(
        projected[:, None, 2 * INNER : 2 * INNER + 2 * STATE], (tokens, groups, 2 * STATE)
    )
    dt_part = projected[:, 2 * INNER + 2 * STATE :].reshape(tokens, groups, heads_here)
    x_raw, bc_raw, dt_raw = (
        lax.all_to_all(x_part, "head", split_axis=1, concat_axis=0, tiled=True),
        lax.all_to_all(bc_part, "head", split_axis=1, concat_axis=0, tiled=True),
        lax.all_to_all(dt_part, "head", split_axis=1, concat_axis=0, tiled=True),
    )
    x_raw = x_raw.reshape(local_len, width_here)
    bc_raw = bc_raw.reshape(local_len, 2 * STATE)
    dt_raw = dt_raw.reshape(local_len, heads_here).astype(jnp.float32)
    tail = local_len - CONV + 1
    edge_x, edge_bc = passed_along((x_raw[tail:], bc_raw[tail:]), "seq", SEQS)
    edge_keep = jnp.where(is_start, 0.0, 1.0)
    edge_x = edge_x.astype(jnp.float32) * edge_keep
    edge_bc = edge_bc.astype(jnp.float32) * edge_keep
    x_raw = x_raw.astype(jnp.float32)
    bc_raw = bc_raw.astype(jnp.float32)
    conv_x = lax.dynamic_slice_in_dim(conv_w, group_idx * width_here, width_here, 1)
    conv_bc = conv_w[:, INNER:]
    bias_x = lax.dynamic_slice_in_dim(conv_b, group_idx * width_here, width_here, 0)
    bias_bc = conv_b[INNER:]
    dt_shift = lax.dynamic_slice_in_dim(dt_bias, group_idx * heads_here, heads_here, 0)
    a_log_part = lax.dynamic_slice_in_dim(a_log, group_idx * heads_here, heads_here, 0)
    skip_part = lax.dynamic_slice_in_dim(d_skip, group_idx * heads_here, heads_here, 0)
    x_heads, b_rows, c_rows, dt_rows, rates = prepare(
        x_raw,
        bc_raw,
        dt_raw,
        edge_x,
        edge_bc,
        conv_x,
        conv_bc,
        bias_x,
        bias_bc,
        dt_shift,
        a_log_part,
        valid_heads,
    )
    cumulative = jnp.cumsum(dt_rows, axis=0) * rates
    decay_all = jnp.exp(cumulative[-1])
    to_end = jnp.exp(cumulative[-1:] - cumulative) * dt_rows
    own_state = jnp.einsum("uh,uhp,un->hpn", to_end, x_heads, b_rows, precision=best)
    slot_mask = seq_onehot.astype(jnp.float32)
    identity = (
        jnp.ones((SEQS, heads_here), jnp.float32),
        jnp.zeros((SEQS, heads_here, HEAD_DIM, STATE), jnp.float32),
    )

    def slotted(decay_vec, piece_state):
        decay_slots = jnp.where(seq_onehot[:, None], decay_vec[None, :], 1.0)
        state_slots = slot_mask[:, None, None, None] * piece_state[None]
        return (decay_slots, state_slots)

    arrived_all = entering(
        slotted(jnp.where(is_start, 0.0, decay_all), own_state), "seq", chain, identity, False
    )[1]
    arrived = lax.dynamic_index_in_dim(arrived_all, seq_id, 0, keepdims=False)
    incoming = jnp.where(is_start, 0.0, arrived)
    (mixed_heads, final_state), pull_back = jax.vjp(
        partial(mixer, valid_heads),
        x_raw,
        bc_raw,
        dt_raw,
        edge_x,
        edge_bc,
        conv_x,
        conv_bc,
        bias_x,
        bias_bc,
        dt_shift,
        a_log_part,
        skip_part,
        incoming,
    )
    mixed_send = mixed_heads.astype(jnp.bfloat16).reshape(local_len, 1, width_here)
    mixed_tok = (
        lax.all_to_all(mixed_send, "head", split_axis=0, concat_axis=1, tiled=True)
        .reshape(tokens, INNER)
        .astype(jnp.float32)
    )
    gate_sigmoid = jax.nn.sigmoid(gate_in)
    gate_act = gate_in * gate_sigmoid
    gated = mixed_tok * gate_act
    gate_scale = inverse_rms(gated)
    gnormed = (gated * gate_scale * gate_gain).astype(jnp.bfloat16)
    branch = jnp.dot(gnormed, w_out, preferred_element_type=jnp.float32)
    valid_col = valid_tokens[:, None]
    block_out = (source + valid_col * branch).astype(jnp.bfloat16)
    grad_rows = grad_out.astype(jnp.float32)
    d_branch = (grad_rows * valid_col).astype(jnp.bfloat16)
    grad_w_out = jnp.einsum("ti,td->id", gnormed, d_branch, preferred_element_type=jnp.float32)
    d_gnormed = jnp.einsum("td,id->ti", d_branch, w_out, preferred_element_type=jnp.float32)
    d_gated, grad_gate = norm_backward(gated, gate_scale, gate_gain, d_gnormed)
    d_mixed = (d_gated * gate_act).astype(jnp.bfloat16)
    d_gate_in = d_gated * mixed_tok * gate_sigmoid * (1.0 + gate_in * (1.0 - gate_sigmoid))
    d_heads = lax.all_to_all(
        d_mixed.reshape(tokens, groups, width_here), "head", split_axis=1, concat_axis=0, tiled=True
    )
    d_heads = d_heads.reshape(local_len, width_here).astype(jnp.float32)
    weighted = d_heads.reshape(local_len, heads_here, HEAD_DIM) * jnp.exp(cumulative)[:, :, None]
    own_grad = jnp.einsum("thp,tn->hpn", weighted, c_rows, precision=best)
    behind_all = entering(
        slotted(jnp.where(is_last, 0.0, decay_all), own_grad), "seq", chain, identity, True
    )[1]
    behind = lax.dynamic_index_in_dim(behind_all, seq_id, 0, keepdims=False)
    from_right = jnp.where(is_last, 0.0, behind)
    grads = pull_back((d_heads, from_right))
    back_x, back_bc = passed_along((grads[3] * edge_keep, grads[4] * edge_keep), "seq", -SEQS)
    dx_heads = jnp.concatenate([grads[0][:tail], grads[0][tail:] + back_x], axis=0)
    dbc_heads = jnp.concatenate([grads[1][:tail], grads[1][tail:] + back_bc], axis=0)
    rec_x, rec_bc, rec_dt = (
        lax.all_to_all(
            dx_heads.reshape(local_len, 1, width_here),
            "head",
            split_axis=0,
            concat_axis=1,
            tiled=True,
        ),
        lax.all_to_all(
            dbc_heads.reshape(local_len, 1, 2 * STATE),
            "head",
            split_axis=0,
            concat_axis=1,
            tiled=True,
        ),
        lax.all_to_all(
            grads[2].reshape(local_len, 1, heads_here),
            "head",
            split_axis=0,
            concat_axis=1,
            tiled=True,
        ),
    )
    d_projected = jnp.concatenate(
        [
            d_gate_in,
            rec_x.reshape(tokens, INNER),
            jnp.sum(rec_bc, axis=1),
            rec_dt.reshape(tokens, HEADS),
        ],
        axis=1,
    ).astype(jnp.bfloat16)
    grad_w_in = jnp.einsum("td,tp->dp", normed, d_projected, preferred_element_type=jnp.float32)
    d_normed = jnp.einsum("tp,dp->td", d_projected, w_in, preferred_element_type=jnp.float32)
    d_source, grad_norm = norm_backward(source, in_scale, norm_gain, d_normed)
    grad_in = grad_rows + d_source
    grad_conv = jnp.concatenate(
        [place_into(grads[5], INNER, group_idx * width_here), grads[6]], axis=1
    )
    grad_bias = jnp.concatenate(
        [place_into(grads[7], INNER, group_idx * width_here), grads[8]], axis=0
    )
    grad_dt = place_into(grads[9], HEADS, group_idx * heads_here)
    grad_alog = place_into(grads[10], HEADS, group_idx * heads_here)
    grad_skip = place_into(grads[11], HEADS, group_idx * heads_here)
    (
        grad_norm,
        grad_w_in,
        grad_conv,
        grad_bias,
        grad_dt,
        grad_alog,
        grad_skip,
        grad_gate,
        grad_w_out,
    ) = lax.psum(
        (
            grad_norm,
            grad_w_in,
            grad_conv,
            grad_bias,
            grad_dt,
            grad_alog,
            grad_skip,
            grad_gate,
            grad_w_out,
        ),
        ("seq", "head"),
    )
    return (
        block_out,
        grad_in,
        grad_norm,
        grad_w_in,
        grad_conv,
        grad_bias,
        grad_dt,
        grad_alog,
        grad_skip,
        grad_gate,
        grad_w_out,
    )


def solution(mesh):
    placed = (
        P(("seq", "head"), None),
        P(("seq", "head"), None),
        P(),
        P(),
        P(),
        P(),
        P(),
        P(),
        P(),
        P(),
        P(),
        P(),
    )
    return jax.shard_map(
        local,
        mesh=mesh,
        in_specs=placed,
        out_specs=(
            P(("seq", "head"), None),
            P(("seq", "head"), None),
            P(),
            P(),
            P(),
            P(),
            P(),
            P(),
            P(),
            P(),
            P(),
        ),
        check_vma=False,
    )
```

profile of v0, /device:TPU:0, one launch (start us, length us, event | category | flops | bytes accessed | tf_op | source)
XLA Modules:
  0.0 1019.1 jit_solution(1937852641391881275)
XLA Ops:
  9.1 4.2 convolution_convert_fusion
  15.8 5.6 all_to_all.103
  22.0 5.5 collective-permute-start
  70.4 37.2 %all_gather.16 = f32[16,2,12]{2,1,0:T(2,128)S(1)} all-gather(f32[1,2,12]{2,1,0:T(2,128)S(1)} %get-tuple-element.2016), channel_id=1, replica_groups=mesh['seq'=16,'head'=2] {'seq'}, dimensions={0}, use_global_device_ids=true | all-gather | bytes 1632 | tf_op jit(solution)/shard_map/all_gather | solution.py:31
  118.3 102.5 %all-gather.3.cloned.1.call-done = f32[16,2,12,64,128]{4,3,2,1,0:T(8,128)} async-done(((f32[1,2,12,64,128]{4,3,2,1,0:T(8,128)}), f32[16,2,12,64,128]{4,3,2,1,0:T(8,128)}) %all-gather.3.cloned.1.call-update) | async-done | bytes 12582928 | tf_op jit(solution)/shard_map/all_gather | solution.py:31
  224.6 80.5 %while.105 = (s32[]{:T(128)}, f32[12,64,128]{2,1,0:T(8,128)S(1)}, f32[2,256,12,64]{1,0,3,2:T(2,128)}, f32[2,256,12]{1,2,0:T(8,128)S(1)}, f32[2,256,256,12]{2,1,3...) while((s32[]{:T(128)}, f32[12,64,128]{2,1,0:T(8,128)S(1)}, ...), condition=%wide.region_9.10_spmd.clone.clone, body=%wide.region_6.9_spmd.clone.clone.sunk | while | flops 1317872640 | bytes 61413468 | solution.py:142
  235.0 3.8 fusion.240
  239.6 16.7 %dynamic_update_slice.270 = f32[2,256,12,64]{1,0,3,2:T(2,128)} dynamic-update-slice(f32[2,256,12,64]{1,0,3,2:T(2,128)} %get-tuple-element.2536, f32[1,256,12,64]{1,0,3,2:T(1,128)S(1)} %copy.345, s32[]{:T(128)S(6)} %copy.400, s32[]{:T(128)} %constant.277.clone.1..sunk.2, s32[]{:T(128)} %constant.277.clone.1..sunk.2, s32[]{:T(128)} %constant.277.clone.1..sunk.2) | dynamic-update-slice | bytes 1572868 | tf_op jit(solution)/shard_map/jvp()/while/body/jit(dynamic_update_index_in_dim)/dynamic_update_slice | solution.py:142
  256.3 6.3 multiply_dynamic-update-slice_fusion.3
  279.8 16.7 %dynamic_update_slice.270 = f32[2,256,12,64]{1,0,3,2:T(2,128)} dynamic-update-slice(f32[2,256,12,64]{1,0,3,2:T(2,128)} %get-tuple-element.2536, f32[1,256,12,64]{1,0,3,2:T(1,128)S(1)} %copy.345, s32[]{:T(128)S(6)} %copy.400, s32[]{:T(128)} %constant.277.clone.1..sunk.2, s32[]{:T(128)} %constant.277.clone.1..sunk.2, s32[]{:T(128)} %constant.277.clone.1..sunk.2) | dynamic-update-slice | bytes 1572868 | tf_op jit(solution)/shard_map/jvp()/while/body/jit(dynamic_update_index_in_dim)/dynamic_update_slice | solution.py:142
  296.6 6.3 multiply_dynamic-update-slice_fusion.3
  317.8 5.8 all_to_all.104
  340.3 5.4 all_to_all.105
  359.6 58.6 %all_gather.18 = f32[16,2,12]{2,1,0:T(2,128)S(1)} all-gather(f32[1,2,12]{2,1,0:T(2,128)S(1)} %copy-done.141), channel_id=1, replica_groups=mesh['seq'=16,'head'=2] {'seq'}, dimensions={0}, use_global_device_ids=true | all-gather | bytes 1632 | tf_op jit(solution)/shard_map/all_gather | solution.py:31
  421.2 4.5 fusion.160
  425.7 103.9 %all-gather.5.cloned.1.call-done = f32[16,2,12,64,128]{4,3,2,1,0:T(8,128)} async-done(((f32[1,2,12,64,128]{4,3,2,1,0:T(8,128)}), f32[16,2,12,64,128]{4,3,2,1,0:T(8,128)}) %all-gather.5.cloned.1.call-update) | async-done | bytes 12582928 | tf_op jit(solution)/shard_map/all_gather | solution.py:31
  529.6 20.4 %while.104 = (s32[]{:T(128)}, f32[2,12,64,128]{3,2,1,0:T(8,128)S(1)}, s32[]{:T(128)}, f32[16,2,12]{2,1,0:T(2,128)S(1)}, f32[16,2,12,64,128]{4,3,2,1,0:T(8,128)},...) while((s32[]{:T(128)}, f32[2,12,64,128]{3,2,1,0:T(8,128)S(1)}, s32[]{:T(128)}, ...), condition=%wide.region_13.14_spmd, body=%wide.region_12.13_spmd.sunk | while | flops 393222 | bytes 2359739 | solution.py:40
  554.0 121.2 %while.106 = (s32[]{:T(128)}, f32[12]{0:T(128)}, f32[12,64,128]{2,1,0:T(8,128)S(1)}, f32[2,256,12,64]{1,0,3,2:T(2,128)}, f32[2,256,128]{2,1,0:T(8,128)}, /*index...) while((s32[]{:T(128)}, f32[12]{0:T(128)}, ...), condition=%wide.region_25.26_spmd.clone.clone, body=%wide.region_14.25_spmd.clone.clone.sunk | while | flops 2628298752 | bytes 62654428 | solution.py:142
  555.8 9.5 fusion.254
  584.2 4.0 fusion.262
  589.0 16.7 %dynamic_update_slice.275 = f32[2,256,12,64]{1,0,3,2:T(2,128)} dynamic-update-slice(f32[2,256,12,64]{1,0,3,2:T(2,128)} %get-tuple-element.2656, f32[1,256,12,64]{1,0,3,2:T(1,128)S(1)} %copy.348, s32[]{:T(128)S(6)} %sub.279, s32[]{:T(128)} %constant.277.clone.1..sunk.3, s32[]{:T(128)} %constant.277.clone.1..sunk.3, s32[]{:T(128)} %constant.277.clone.1..sunk.3) | dynamic-update-slice | bytes 1572868 | tf_op jit(solution)/shard_map/transpose(jvp())/while/body/jit(dynamic_update_index_in_dim)/dynamic_update_slice | solution.py:142
  616.3 9.5 fusion.254
  644.5 4.0 fusion.262
  649.3 16.7 %dynamic_update_slice.275 = f32[2,256,12,64]{1,0,3,2:T(2,128)} dynamic-update-slice(f32[2,256,12,64]{1,0,3,2:T(2,128)} %get-tuple-element.2656, f32[1,256,12,64]{1,0,3,2:T(1,128)S(1)} %copy.348, s32[]{:T(128)S(6)} %sub.279, s32[]{:T(128)} %constant.277.clone.1..sunk.3, s32[]{:T(128)} %constant.277.clone.1..sunk.3, s32[]{:T(128)} %constant.277.clone.1..sunk.3) | dynamic-update-slice | bytes 1572868 | tf_op jit(solution)/shard_map/transpose(jvp())/while/body/jit(dynamic_update_index_in_dim)/dynamic_update_slice | solution.py:142
  687.1 6.1 multiply_reduce_fusion.3
  711.1 4.2 all_to_all.107
  720.4 5.2 all_to_all.108
  733.0 6.8 fusion.156
  745.8 5.9 fusion.148
  751.7 45.2 %all-reduce.20 = (f32[768]{0:T(1024)}, f32[4,1792]{1,0:T(4,128)}, f32[1792]{0:T(1024)}, f32[24]{0:T(128)}, f32[24]{0:T(128)}, /*index=5*/f32[24]{0:T(128)}, f32[1536]{0:T(1024)}) all-reduce(f32[768]{0:T(1024)S(1)} %get-tuple-element.1806, f32[4,1792]{1,0:T(4,128)S(1)} %pad_maximum_fusion.5, ...), channel_id=1, replica_groups=mesh['seq'=16,'head'=2] {'seq','head'}, use_global_device_ids=true, to_apply=%region_29.30 | all-reduce | flops 11336 | bytes 90688 | tf_op jit(solution)/shard_map/psum | solution.py:369
  799.2 201.9 %all-reduce.24.cloned.1.call-done = (f32[768,3352]{0,1:T(8,128)}, f32[1536,768]{1,0:T(8,128)}) async-done(((f32[768,3352]{0,1:T(8,128)}, f32[1536,768]{1,0:T(8,128)}), (f32[768,3352]{0,1:T(8,128)}, f32[1536,768]{1,0:T(8,128)})) %all-reduce.24.cloned.1.call-update) | async-done | bytes 15015952 | tf_op jit(solution)/shard_map/psum | solution.py:369
  1001.1 8.8 copy.483
  (738 shorter events, 273.9 us)
Async XLA Ops:
  7.2 326.1 %copy-start = (bf16[1536,768]{1,0:T(8,128)(2,1)S(1)}, bf16[1536,768]{1,0:T(8,128)(2,1)}, u32[]{:S(2)}) copy-start(bf16[1536,768]{1,0:T(8,128)(2,1)} %param.31) | copy-start | bytes 7077892
  14.6 12.8 %slice-start = ((bf16[256,3352]{0,1:T(8,128)(2,1)}), bf16[256,256]{0,1:T(8,128)(2,1)S(1)}, s32[]{:S(2)}) async-start(bf16[256,3352]{0,1:T(8,128)(2,1)} %copy-done.40), calls=%async_computation.11 | async-start | bytes 262144 | tf_op jit(solution)/shard_map/slice | solution.py:203
  15.8 16.0 %slice-start.1 = ((bf16[256,3352]{0,1:T(8,128)(2,1)}), bf16[256,24]{0,1:T(8,128)(2,1)S(1)}, s32[]{:S(2)}) async-start(bf16[256,3352]{0,1:T(8,128)(2,1)} %copy-done.40), calls=%async_computation.12 | async-start | bytes 24576 | tf_op jit(solution)/shard_map/slice | solution.py:205
  15.8 25.3 %copy-start.149 = (s32[2]{0:T(128)S(1)}, s32[2]{0:T(128)}, u32[]{:S(2)}) copy-start(s32[2]{0:T(128)} %param.22) | copy-start | bytes 28
  21.4 31.6 %copy-start.28 = (bf16[256,2,768]{2,0,1:T(8,128)(2,1)}, bf16[256,2,768]{2,0,1:T(8,128)(2,1)S(1)}, u32[]{:S(2)}) copy-start(bf16[256,2,768]{2,0,1:T(8,128)(2,1)S(1)} %all_to_all.103) | copy-start | bytes 2359300
  22.0 36.4 %collective-permute-start = (bf16[3,768]{1,0:T(4,128)(2,1)}, bf16[3,768]{1,0:T(4,128)(2,1)}, u32[]{:S(2)}, u32[]{:S(2)}) collective-permute-start(bf16[3,768]{1,0:T(4,128)(2,1)} %slice.198), channel_id=1, source_target_pairs={{0,4},{2,6},{4,8},{6,10},{8,12},{10,14},{12,16},{14,18},{16,20},{1... | collective-permute-start | bytes 13832 | tf_op jit(solution)/shard_map/ppermute | solution.py:24
  28.3 5.0 all-to-all-start.2
  33.3 19.7 %copy-start.46 = (bf16[256,2,256]{2,0,1:T(8,128)(2,1)}, bf16[256,2,256]{2,0,1:T(8,128)(2,1)S(1)}, u32[]{:S(2)}) copy-start(bf16[256,2,256]{2,0,1:T(8,128)(2,1)S(1)} %all-to-all-done.2) | copy-start | bytes 786436
  33.3 8.5 all-to-all-start
  36.5 184.3 %all-gather.3.cloned.1.call-start = ((), (), s32[]{:S(2)}) async-start(), calls=%async_computation.8 | async-start | bytes 13369344 | tf_op jit(solution)/shard_map/all_gather | solution.py:31
  37.2 17.7 %collective-permute-start.1 = (bf16[3,256]{1,0:T(4,128)(2,1)}, bf16[3,256]{1,0:T(4,128)(2,1)}, u32[]{:S(2)}, u32[]{:S(2)}) collective-permute-start(bf16[3,256]{1,0:T(4,128)(2,1)} %slice.204), channel_id=1, source_target_pairs={{0,4},{2,6},{4,8},{6,10},{8,12},{10,14},{12,16},{14,18},{16,20},{1... | collective-permute-start | bytes 4616 | tf_op jit(solution)/shard_map/ppermute | solution.py:24
  41.7 69.1 %copy-start.77 = (bf16[256,2,12]{0,2,1:T(8,128)(2,1)}, bf16[256,2,12]{0,2,1:T(8,128)(2,1)S(1)}, u32[]{:S(2)}) copy-start(bf16[256,2,12]{0,2,1:T(8,128)(2,1)S(1)} %all-to-all-done) | copy-start | bytes 36868
  41.7 11.2 %copy-start.71 = (f32[2,256,1,12]{1,3,0,2:T(8,128)}, f32[2,256,1,12]{1,3,0,2:T(8,128)S(1)}, u32[]{:S(2)}) copy-start(f32[2,256,1,12]{1,3,0,2:T(8,128)S(1)} %convert_bitcast_fusion.3) | copy-start | bytes 73732
  42.5 16.7 %copy-start.91 = (f32[512]{0:T(512)}, f32[512]{0:T(512)S(1)}, u32[]{:S(2)}) copy-start(f32[512]{0:T(512)S(1)} %fusion.181) | copy-start | bytes 6148
  43.2 9.7 copy-start.121
  58.4 53.2 %copy-start.35 = (f32[512,256]{1,0:T(8,128)}, f32[512,256]{1,0:T(8,128)S(1)}, u32[]{:S(2)}) copy-start(f32[512,256]{1,0:T(8,128)S(1)} %get-tuple-element.1976) | copy-start | bytes 1572868
  67.8 39.9 %copy-start.147 = (f32[24]{0:T(128)S(1)}, f32[24]{0:T(128)}, u32[]{:S(2)}) copy-start(f32[24]{0:T(128)} %param.28) | copy-start | bytes 292
  67.8 43.1 %copy-start.122 = (f32[12]{0:T(128)S(1)}, f32[12]{0:T(128)}, u32[]{:S(2)}) copy-start(f32[12]{0:T(128)} %copy-done.121) | copy-start | bytes 148
  68.9 460.7 %all-gather.5.cloned.1.call-start = ((), (), s32[]{:S(2)}) async-start(), calls=%async_computation.9 | async-start | bytes 13369344 | tf_op jit(solution)/shard_map/all_gather | solution.py:31
  333.3 87.9 %copy-start.98 = (f32[256]{0:T(256)}, f32[256]{0:T(256)S(1)}, u32[]{:S(2)}) copy-start(f32[256]{0:T(256)S(1)} %get-tuple-element.2014) | copy-start | bytes 3076
  358.9 642.3 %all-reduce.24.cloned.1.call-start = ((), (), s32[]{:S(2)}) async-start(), calls=%async_computation.10 | async-start | bytes 30031872 | tf_op jit(solution)/shard_map/psum | solution.py:369
  555.8 9.5 copy-start.1
  555.8 9.5 copy-start.21
  555.8 10.2 %copy-start.11 = (f32[2,256,128]{2,1,0:T(8,128)S(1)}, f32[2,256,128]{2,1,0:T(8,128)}, u32[]{:S(2)}) copy-start(f32[2,256,128]{2,1,0:T(8,128)} %get-tuple-element.2697) | copy-start | bytes 786436 | tf_op jit(solution)/shard_map/transpose(jvp())/while
  616.3 9.5 copy-start.1
  616.3 9.5 copy-start.21
  616.3 10.2 %copy-start.11 = (f32[2,256,128]{2,1,0:T(8,128)S(1)}, f32[2,256,128]{2,1,0:T(8,128)}, u32[]{:S(2)}) copy-start(f32[2,256,128]{2,1,0:T(8,128)} %get-tuple-element.2697) | copy-start | bytes 786436 | tf_op jit(solution)/shard_map/transpose(jvp())/while
  680.0 29.8 %collective-permute-start.3 = (f32[3,256]{1,0:T(4,128)}, f32[3,256]{1,0:T(4,128)}, u32[]{:S(2)}, u32[]{:S(2)}) collective-permute-start(f32[3,256]{1,0:T(4,128)} %add_multiply_fusion.1), channel_id=1, source_target_pairs={{4,0},{6,2},{8,4},{10,6},{12,8},{14,10},{16,12},{18,14},{20,16},{2... | collective-permute-start | bytes 9224 | tf_op jit(solution)/shard_map/ppermute | solution.py:24
  706.3 9.8 collective-permute-start.2
  745.8 51.1 %copy-start.43 = (bf16[256,768]{1,0:T(8,128)(2,1)S(1)}, bf16[256,768]{1,0:T(8,128)(2,1)}, u32[]{:S(2)}) copy-start(bf16[256,768]{1,0:T(8,128)(2,1)} %param.21) | copy-start | bytes 1179652
  745.8 51.1 %copy-start.135 = (f32[256]{0:T(256)S(1)}, f32[256]{0:T(256)}, u32[]{:S(2)}) copy-start(f32[256]{0:T(256)} %get-tuple-element.2011) | copy-start | bytes 3076
  1001.1 8.8 copy-start.34
  (179 other events, 671.6 us)
Sparse Core Ops, SparseCore 0:
  69.0 151.7 all-gather.2
  359.0 170.5 all-gather.4
  740.0 261.1 all-reduce.23
where the time goes:
time: 1030 us; the launch traced here: 1020 us
  waiting for transfers between devices  409 us (40%)
  local copies, waits for them, and re-layouts  185 us (18%)
  blocking collectives  171 us (17%)
  other arithmetic  118 us (11%)
  matrix products  99.5 us (10%)
  starting transfers between devices  18.3 us (2%)
  between operations  15.6 us (2%)
    all_gather x2, waiting for transfers between devices, entering(): gathered = jax.tree.map(lambda a: lax.all_gather(a, axis), part)  206 us
    psum x1, waiting for transfers between devices, local(): lax.psum((grad_norm, grad_w_in, grad_conv, grad_bias, grad_dt, grad_alog,...  202 us
    all_gather x2, blocking collectives, entering(): gathered = jax.tree.map(lambda a: lax.all_gather(a, axis), part)  95.8 us
    dynamic_update_slice x18, local copies, waits for them, and re-layouts, mixer(): lax.scan(partial(block_step, rates), incoming, (blocks(x_heads), blocks(b...  71.9 us
    psum x1, blocking collectives, local(): lax.psum((grad_norm, grad_w_in, grad_conv, grad_bias, grad_dt, grad_alog,...  45.2 us
    dot_general x6, matrix products, block_step(): inner_part = jnp.einsum('tuh,uhp->thp', weight, x_heads, precision=best)  34.4 us
    unnamed x229, local copies, waits for them, and re-layouts  32.9 us
  transfers between devices with their start and end apart: 9, of which 4 were waited for; matrix products, arithmetic and copies ran while one was open for 8% of the time, Pallas kernels for 0%

commit v1 on v0

v1 whole, which is shorter than its diff:
```python
from functools import partial

import jax
import jax.numpy as jnp
from jax import lax
from jax.experimental import pallas as pl
from jax.experimental.pallas import tpu as pltpu
from jax.sharding import PartitionSpec as P

D = 768
INNER = 1536
HEADS = 24
HEAD_DIM = 64
STATE = 128
CONV = 4
SEQS = 2
XBC = INNER + 2 * STATE
PROJ = 2 * INNER + 2 * STATE + HEADS
PAIRS = HEADS // 2
EPS = 1e-05
LOG2E = 1.4426950408889634

f32 = jnp.float32
bf16 = jnp.bfloat16
MESH = pl.DeviceIdType.MESH
VMEM = pl.BlockSpec(memory_space=pltpu.VMEM)
SMEM = pl.BlockSpec(memory_space=pltpu.SMEM)
NN = ((1,), (0,))
NT = ((1,), (1,))
TN = ((0,), (0,))


def dot(a, b, dims=NN):
    return lax.dot_general(a, b, (dims, ((), ())), preferred_element_type=f32)


def split_dot(a, pick, terms=3):
    total = None
    for _ in range(terms):
        part = a.astype(bf16)
        a = a - part.astype(f32)
        term = dot(part, pick)
        total = term if total is None else total + term
    return total


def split_dot_left(pick, a, terms=3):
    total = None
    for _ in range(terms):
        part = a.astype(bf16)
        a = a - part.astype(f32)
        term = dot(pick, part)
        total = term if total is None else total + term
    return total


def iota(shape, dim):
    return lax.broadcasted_iota(jnp.int32, shape, dim)


def one_hot(cond):
    return jnp.where(cond, 1.0, 0.0).astype(bf16)


def sigmoid(v):
    return 1.0 / (1.0 + jnp.exp(-v))


def lanes(start, size):
    return pl.ds(pl.multiple_of(start, 128), size)


def valid_rows(lengths_ref, per_row, rows, width):
    place = lax.axis_index("seq")
    first = (place // SEQS) * (rows * lax.axis_size("head")) + lax.axis_index("head") * rows
    limit = lengths_ref[place % SEQS]
    return jnp.where(iota((rows, width), 0) + first < limit, 1.0, 0.0)


def call(body, outs, args, scratch=(), smem=(), vmem=56 << 20, cost=None, **params):
    return pl.pallas_call(
        body,
        out_shape=[jax.ShapeDtypeStruct(s, d) for s, d in outs],
        in_specs=[SMEM if i in smem else VMEM for i in range(len(args))],
        out_specs=[VMEM] * len(outs),
        scratch_shapes=list(scratch),
        compiler_params=pltpu.CompilerParams(vmem_limit_bytes=vmem, **params),
    )(*args)


def front_kernel(
    lengths_ref,
    blk,
    edge,
    gain,
    w_in,
    conv_w,
    conv_b,
    heads_ref,
    normed_out,
    gate_out,
    pad_out,
    run_out,
    x_out,
    xd_out,
    xde_out,
    b_out,
    c_out,
    head_out,
    cumt_out,
    cumb_out,
    rows_out,
    state_out,
):
    rows = blk.shape[0]

    def norm(v):
        v = v.astype(f32)
        scale = lax.rsqrt(jnp.mean(v * v, axis=-1, keepdims=True) + EPS)
        return (v * scale * gain[...]).astype(bf16)

    normed = norm(blk[...])
    normed_out[...] = normed
    gate_out[...] = dot(normed, w_in[:INNER, :], NT).astype(bf16)
    ahead = norm(edge[...])
    pad_out[0:16, :] = dot(ahead, w_in[INNER : INNER + XBC, :], NT).astype(bf16).astype(f32)
    pad_out[16 : 16 + rows, :] = dot(normed, w_in[INNER : INNER + XBC, :], NT).astype(bf16).astype(f32)
    keep = valid_rows(lengths_ref, None, rows, 128)
    head_out[3] = jnp.zeros((rows, 128), f32)
    head_out[3, :, 0:HEADS] = dot(normed, w_in[INNER + XBC :, :], NT).astype(bf16).astype(f32)
    lane = iota((rows, 128), 1)
    shifted = head_out[3] + heads_ref[0:1, :]
    soft = jnp.maximum(shifted, 0.0) + jnp.log1p(jnp.exp(-jnp.abs(shifted)))
    dt = jnp.where(lane < HEADS, soft * keep, 0.0)
    rates = -jnp.exp(heads_ref[1:2, :])
    below = one_hot(iota((rows, rows), 0) >= iota((rows, rows), 1))
    cum = split_dot_left(below, dt) * rates
    cum2 = cum * LOG2E
    head_out[0] = dt
    head_out[1] = cum
    head_out[2] = sigmoid(shifted) * keep
    head_out[3] = cum2
    cumt_out[...] = cum2.T
    pick_lane = iota((128, 256), 1)
    pick_head = iota((128, 256), 0)

    def spread(i, carry):
        cumb_out[:, lanes(i * 256, 256)] = split_dot(
            head_out[3], one_hot((pick_lane >> 7) + 2 * i == pick_head)
        )
        return carry

    lax.fori_loop(0, PAIRS, spread, 0)

    def convolve(i):
        cols = lanes(i * 256, 256)
        running = conv_b[:, cols] + pad_out[13 : 13 + rows, cols] * conv_w[0:1, cols]
        for tap in range(1, CONV):
            running = running + pad_out[13 + tap : 13 + tap + rows, cols] * conv_w[tap : tap + 1, cols]
        run_out[:, cols] = running
        return running * sigmoid(running)

    act = convolve(INNER // 256)
    b_out[...] = act[:, :STATE].astype(bf16)
    c_out[...] = act[:, STATE:].astype(bf16)
    keep2 = valid_rows(lengths_ref, None, rows, 256)

    def channels(i, carry):
        cols = lanes(i * 256, 256)
        pick = one_hot((pick_lane >> 6) + 4 * i == pick_head)
        x = convolve(i) * keep2
        x_out[:, cols] = x
        xd = x * split_dot(head_out[0], pick)
        xd_out[:, cols] = xd.astype(bf16)
        wide = split_dot(head_out[3], pick)
        last = wide[rows - 1 : rows, :]
        xde_out[:, cols] = (xd * jnp.exp2(last - wide)).astype(bf16)
        rows_out[0:8, cols] = jnp.broadcast_to(jnp.exp2(last), (8, 256))
        rows_out[8:16, cols] = split_dot(jnp.broadcast_to(heads_ref[2:3, :], (8, 128)), pick)
        return carry

    lax.fori_loop(0, INNER // 256, channels, 0)
    state_out[...] = dot(b_out[...], xde_out[...], TN)


def front(lengths, blk, edge, gain, w_in, conv_w, conv_b, heads):
    t = blk.shape[0]
    outs = [
        ((t, D), bf16),
        ((t, INNER), bf16),
        ((t + 16, XBC), f32),
        ((t, XBC), f32),
        ((t, INNER), f32),
        ((t, INNER), bf16),
        ((t, INNER), bf16),
        ((t, STATE), bf16),
        ((t, STATE), bf16),
        ((4, t, 128), f32),
        ((128, t), f32),
        ((t, HEADS * 128), f32),
        ((16, INNER), f32),
        ((STATE, INNER), f32),
    ]
    return call(front_kernel, outs, (lengths, blk, edge, gain, w_in, conv_w, conv_b, heads), smem=(0,))


def exchange_kernel(reverse, state, decay, out, sib_state, sib_decay, mine, total, got, got_decay, back, back_got, ssem, rsem):
    half = INNER // 2
    chips = lax.axis_size("seq") // SEQS
    rows = STATE // chips
    place = lax.axis_index("seq")
    core = lax.axis_index("head")
    chip = place // SEQS
    which = place % SEQS
    sibling = (place, 1 - core)
    rank = 1 - core if reverse else core
    barrier = pltpu.get_barrier_semaphore()
    pl.semaphore_signal(barrier, inc=1, device_id=sibling, device_id_type=MESH)

    def peer(k):
        return (lax.rem(chip + k, chips) * SEQS + which, core)

    for k in range(1, chips):
        pl.semaphore_signal(barrier, inc=1, device_id=peer(k), device_id_type=MESH)
    pl.semaphore_wait(barrier, chips)
    own_cols = lanes(core * half, half)
    sib_cols = lanes((1 - core) * half, half)

    def copy(src, dst, n, to):
        return pltpu.make_async_remote_copy(
            src_ref=src, dst_ref=dst, send_sem=ssem.at[n], recv_sem=rsem.at[n], device_id=to, device_id_type=MESH
        )

    first = [
        copy(state.at[:, sib_cols], sib_state, 0, sibling),
        copy(decay.at[:, sib_cols], sib_decay, 1, sibling),
    ]
    for c in first:
        c.start()
    for c in first:
        c.wait()
    own = state[:, own_cols]
    own_decay = decay[0:1, own_cols]
    other = sib_state[...]
    other_decay = sib_decay[0:1, :]
    later = rank == 1
    late_decay = jnp.where(later, own_decay, other_decay)
    early_decay = jnp.where(later, other_decay, own_decay)
    early = jnp.where(later, other, own)
    late = jnp.where(later, own, other)
    mine[...] = (late_decay * early + late).astype(bf16)
    total[...] = jnp.broadcast_to(own_decay * other_decay, total.shape)
    second = []
    for k in range(1, chips):
        to = lax.rem(chip + k, chips)
        piece = pl.ds(pl.multiple_of(to * rows, rows), rows)
        second.append(copy(mine.at[piece], got.at[k], 2 * k, peer(k)))
        second.append(copy(total, got_decay.at[k], 2 * k + 1, peer(k)))
    for c in second:
        c.start()
    got[0] = mine[pl.ds(pl.multiple_of(chip * rows, rows), rows), :]
    got_decay[0] = total[...]
    for c in second:
        c.wait()

    def scan(i, carry):
        source = chips - 1 - i if reverse else i
        slot = lax.rem(chip - source + chips, chips)
        to = lax.rem(source - chip + chips, chips)
        back[pl.ds(to, 1)] = carry.astype(bf16)[None]
        return got_decay[pl.ds(slot, 1)][0, 0:1, :] * carry + got[pl.ds(slot, 1)][0].astype(f32)

    lax.fori_loop(0, chips, scan, jnp.zeros((rows, half), f32))
    third = []
    here = pl.ds(pl.multiple_of(chip * rows, rows), rows)
    base = 2 * chips
    for k in range(1, chips):
        third.append(copy(back.at[k], back_got.at[here], base + k, peer(k)))
    for c in third:
        c.start()
    back_got[here, :] = back[0]
    for c in third:
        c.wait()
    enter = back_got[...].astype(f32)
    second_enter = early_decay * enter + early
    for_own = jnp.where(later, second_enter, enter).astype(bf16)
    for_sib = jnp.where(later, enter, second_enter).astype(bf16)
    out[:, own_cols] = for_own
    mine[...] = for_sib
    last = copy(mine, out.at[:, own_cols], base, sibling)
    last.start()
    last.wait()


def exchange(state, decay, reverse):
    half = INNER // 2
    chips = lax.axis_size("seq") // SEQS
    rows = STATE // chips
    n = 3 * chips
    scratch = [
        pltpu.VMEM((STATE, half), f32),
        pltpu.VMEM((8, half), f32),
        pltpu.VMEM((STATE, half), bf16),
        pltpu.VMEM((8, half), f32),
        pltpu.VMEM((chips, rows, half), bf16),
        pltpu.VMEM((chips, 8, half), f32),
        pltpu.VMEM((chips, rows, half), bf16),
        pltpu.VMEM((STATE, half), bf16),
        pltpu.SemaphoreType.DMA((n,)),
        pltpu.SemaphoreType.DMA((n,)),
    ]
    return call(
        partial(exchange_kernel, reverse),
        [((STATE, INNER), bf16)],
        (state, decay),
        scratch,
        collective_id=1 if reverse else 0,
        has_side_effects=True,
    )[0]


def exchange_plain(state, decay, reverse):
    groups = lax.axis_size("head")
    count = lax.axis_size("seq") * groups
    place = lax.axis_index("seq")
    states = lax.all_gather(state.astype(bf16), ("seq", "head"), axis=0)
    decays = lax.all_gather(decay[0:1], ("seq", "head"), axis=0)
    blocks = count // SEQS
    block = place // SEQS * groups + lax.axis_index("head")

    def one(i, carry):
        source = blocks - 1 - i if reverse else i
        index = (source // groups * SEQS + place % SEQS) * groups + source % groups
        new = lax.dynamic_index_in_dim(decays, index, 0, False) * carry
        return new + lax.dynamic_index_in_dim(states, index, 0, False).astype(f32)

    ahead = blocks - 1 - block if reverse else block
    return lax.fori_loop(0, ahead, one, jnp.zeros(state.shape, f32)).astype(bf16)


def middle_kernel(
    lengths_ref,
    blk,
    gout,
    normed,
    gate,
    x_in,
    xd_in,
    b_in,
    c_in,
    cumt,
    cumb,
    rows_in,
    enter,
    gain,
    w_out,
    y_out,
    block_out,
    dy_out,
    dye_out,
    dgate_out,
    ggain_out,
    adj_out,
    grads_out,
    scores,
    mixed,
    gated_s,
    gn_s,
    scale_s,
    dgn_s,
    db_s,
):
    rows = blk.shape[0]
    causal = iota((rows, rows), 0) >= iota((rows, rows), 1)
    scores[...] = jnp.where(causal, dot(c_in[...], b_in[...], NT), 0.0)
    lane = iota((rows, 128), 1)
    left = one_hot(iota((1, 128), 1) < HEAD_DIM)
    right = one_hot(iota((1, 128), 1) >= HEAD_DIM)

    def pair(i, carry):
        cols = lanes(i * 128, 128)
        c0 = cumb[:, lanes(i * 256, 128)]
        c1 = cumb[:, lanes(i * 256 + 128, 128)]
        xd = xd_in[:, cols]
        y = None
        for cc, part, mask in ((c0, 0, left), (c1, 1, right)):
            row = cumt[pl.ds(2 * i + part, 1), :]
            decay = jnp.exp2(jnp.minimum(jnp.concatenate([cc] * (rows // 128), axis=1) - row, 0.0))
            term = dot((decay * scores[...]).astype(bf16), xd * mask)
            y = term if y is None else y + term
        grow = jnp.exp2(jnp.where(lane < HEAD_DIM, c0, c1))
        y = y + grow * dot(c_in[...], enter[:, cols])
        y_out[:, cols] = y
        mixed[:, cols] = (y + rows_in[8:9, cols] * x_in[:, cols]).astype(bf16).astype(f32)
        return carry

    lax.fori_loop(0, PAIRS, pair, 0)
    step = 32

    def gating(i, carry):
        r = pl.ds(pl.multiple_of(i * step, step), step)
        g = gate[r, :].astype(f32)
        gated = mixed[r, :] * g * sigmoid(g)
        scale = lax.rsqrt(jnp.mean(gated * gated, axis=-1, keepdims=True) + EPS)
        gated_s[r, :] = gated
        scale_s[r, :] = jnp.broadcast_to(scale, (step, 128))
        gn_s[r, :] = (gated * scale * gain[...]).astype(bf16)
        return carry

    lax.fori_loop(0, rows // step, gating, 0)
    keep = valid_rows(lengths_ref, None, rows, D)
    db_s[...] = (gout[...].astype(f32) * keep).astype(bf16)
    dgn_s[...] = dot(db_s[...], w_out[...], NT)
    block_out[...] = (blk[...].astype(f32) + keep * dot(gn_s[...], w_out[...])).astype(bf16)
    ggain_out[...] = jnp.zeros_like(ggain_out)

    def ungating(i, carry):
        r = pl.ds(pl.multiple_of(i * step, step), step)
        g = gate[r, :].astype(f32)
        sg = sigmoid(g)
        gated = gated_s[r, :]
        scale = scale_s[r, 0:1]
        dgn = dgn_s[r, :]
        ggain_out[...] += jnp.sum((dgn * gated * scale).reshape(step // 8, 8, INNER), axis=0)
        weighted = dgn * gain[...]
        average = jnp.mean(weighted * gated, axis=-1, keepdims=True)
        d_gated = scale * weighted - gated * (scale * scale * scale) * average
        dy_out[r, :] = (d_gated * g * sg).astype(bf16)
        dgate_out[r, :] = (d_gated * mixed[r, :] * sg * (1.0 + g * (1.0 - sg))).astype(bf16)
        return carry

    lax.fori_loop(0, rows // step, ungating, 0)

    def weigh(i, carry):
        cols = lanes(i * 128, 128)
        grow = jnp.exp2(jnp.where(lane < HEAD_DIM, cumb[:, lanes(i * 256, 128)], cumb[:, lanes(i * 256 + 128, 128)]))
        dye_out[:, cols] = (dy_out[:, cols].astype(f32) * grow).astype(bf16)
        return carry

    lax.fori_loop(0, PAIRS, weigh, 0)
    adj_out[...] = dot(c_in[...], dye_out[...], TN)
    grads_out[:INNER, :] = dot(dgate_out[...], normed[...], TN).astype(bf16)
    grads_out[INNER:, :] = dot(gn_s[...], db_s[...], TN).astype(bf16)


def middle(lengths, blk, gout, normed, gate, x, xd, b, c, cumt, cumb, rows_in, enter, gain, w_out):
    t = blk.shape[0]
    outs = [
        ((t, INNER), f32),
        ((t, D), bf16),
        ((t, INNER), bf16),
        ((t, INNER), bf16),
        ((t, INNER), bf16),
        ((8, INNER), f32),
        ((STATE, INNER), f32),
        ((2 * INNER, D), bf16),
    ]
    scratch = [
        pltpu.VMEM((t, t), f32),
        pltpu.VMEM((t, INNER), f32),
        pltpu.VMEM((t, INNER), f32),
        pltpu.VMEM((t, INNER), bf16),
        pltpu.VMEM((t, 128), f32),
        pltpu.VMEM((t, INNER), f32),
        pltpu.VMEM((t, D), bf16),
    ]
    args = (lengths, blk, gout, normed, gate, x, xd, b, c, cumt, cumb, rows_in, enter, gain, w_out)
    return call(middle_kernel, outs, args, scratch, smem=(0,))


def back_kernel(
    lengths_ref,
    y_in,
    dy_in,
    dye_in,
    x_in,
    xd_in,
    xde_in,
    b_in,
    c_in,
    run_in,
    cumt,
    cumb,
    head_in,
    rows_in,
    heads_ref,
    enter,
    own,
    leave,
    drun_out,
    dz_out,
    small_out,
    scores,
    dscores,
    skip_s,
    q_s,
    ry_s,
):
    rows = y_in.shape[0]
    causal = iota((rows, rows), 1) >= iota((rows, rows), 0)
    scores[...] = jnp.where(causal, dot(b_in[...], c_in[...], NT), 0.0)
    dscores[...] = jnp.zeros_like(dscores)
    q_s[...] = jnp.zeros_like(q_s)
    ry_s[...] = jnp.zeros_like(ry_s)
    lane = iota((rows, 128), 1)
    keep = valid_rows(lengths_ref, None, rows, 128)
    left = one_hot(iota((1, 128), 1) < HEAD_DIM)
    right = one_hot(iota((1, 128), 1) >= HEAD_DIM)
    pick_lane = iota((128, 128), 0)
    pick_head = iota((128, 128), 1)

    def dsilu(cols):
        running = run_in[:, cols]
        sg = sigmoid(running)
        return sg * (1.0 + running * (1.0 - sg))

    def pair(i, carry):
        cols = lanes(i * 128, 128)
        c0 = cumb[:, lanes(i * 256, 128)]
        c1 = cumb[:, lanes(i * 256 + 128, 128)]
        xd = xd_in[:, cols]
        dy = dy_in[:, cols]
        v = None
        for cc, part, mask in ((c0, 0, left), (c1, 1, right)):
            row = cumt[pl.ds(2 * i + part, 1), :]
            decay = jnp.exp2(jnp.minimum(row - jnp.concatenate([cc] * (rows // 128), axis=1), 0.0))
            masked = dy * mask
            term = dot((decay * scores[...]).astype(bf16), masked)
            v = term if v is None else v + term
            dscores[...] += decay * dot(xd, masked, NT)
        c01 = jnp.where(lane < HEAD_DIM, c0, c1)
        v = v + jnp.exp2(c01[rows - 1 : rows, :] - c01) * dot(b_in[...], leave[:, cols])
        pick = one_hot((pick_lane >> 6) + 2 * i == pick_head)
        dtw = split_dot(head_in[0], one_hot((pick_head >> 6) + 2 * i == pick_lane))
        x = x_in[:, cols]
        dyf = dy.astype(f32)
        q_s[...] += split_dot(x * v, pick)
        ry_s[...] += split_dot(dyf * y_in[:, cols], pick)
        skip_s[:, cols] = jnp.sum((dyf * x).reshape(rows // 8, 8, 128), axis=0)
        dx = dtw * v + rows_in[8:9, cols] * dyf
        drun_out[:, cols] = dx * keep * dsilu(cols)
        return carry

    lax.fori_loop(0, PAIRS, pair, 0)
    dsc = jnp.where(causal, dscores[...], 0.0).astype(bf16)
    d_b = dot(dsc, c_in[...]) + dot(xde_in[...], leave[...], NT)
    d_c = dot(dsc, b_in[...], TN) + dot(dye_in[...], enter[...], NT)
    drun_out[:, INNER : INNER + STATE] = d_b * dsilu(slice(INNER, INNER + STATE))
    drun_out[:, INNER + STATE :] = d_c * dsilu(slice(INNER + STATE, XBC))
    full_pick = one_hot((iota((INNER, 128), 0) >> 6) == iota((INNER, 128), 1))
    out_state = rows_in[0:1, :] * enter[...].astype(f32) + own[...]
    d_last = split_dot(
        jnp.sum((leave[...].astype(f32) * out_state).reshape(STATE // 8, 8, INNER), axis=0), full_pick
    )
    d_last = jnp.sum(d_last, axis=0, keepdims=True)
    dt = head_in[0]
    q = q_s[...]
    d_cum = ry_s[...] - dt * q + jnp.where(iota((rows, 128), 0) == rows - 1, d_last, 0.0)
    rates = -jnp.exp(heads_ref[1:2, :])
    above = one_hot(iota((rows, rows), 0) <= iota((rows, rows), 1))
    d_dt = q + split_dot_left(above, d_cum * rates)
    dz = d_dt * head_in[2]
    dz_out[...] = dz
    small_out[0:1, :] = jnp.sum(dz, axis=0, keepdims=True)
    small_out[1:2, :] = jnp.sum(d_cum * head_in[1], axis=0, keepdims=True)
    small_out[2:3, :] = jnp.sum(split_dot(skip_s[...], full_pick), axis=0, keepdims=True)
    small_out[3:8, :] = jnp.zeros((5, 128), f32)


def back(lengths, y, dy, dye, x, xd, xde, b, c, run, cumt, cumb, head, rows_in, heads, enter, own, leave):
    t = y.shape[0]
    outs = [((t, XBC), f32), ((t, 128), f32), ((8, 128), f32)]
    scratch = [
        pltpu.VMEM((t, t), f32),
        pltpu.VMEM((t, t), f32),
        pltpu.VMEM((8, INNER), f32),
        pltpu.VMEM((t, 128), f32),
        pltpu.VMEM((t, 128), f32),
    ]
    args = (lengths, y, dy, dye, x, xd, xde, b, c, run, cumt, cumb, head, rows_in, heads, enter, own, leave)
    return call(back_kernel, outs, args, scratch, smem=(0,))


VEC_ROW = XBC + 128
REST_ROWS = 2048


def last_kernel(
    blk,
    gout,
    normed,
    gain,
    w_in,
    conv_w,
    pad_in,
    drun_in,
    edge,
    dz_in,
    dgate,
    ggain,
    small_in,
    gin_out,
    grads_out,
    ext,
    dproj,
    vec,
    sums,
):
    rows = blk.shape[0]
    ext[0:rows, :] = drun_in[...]
    ext[rows : rows + 8, :] = edge[...]
    vec[...] = jnp.zeros_like(vec)

    def channels(i, carry):
        cols = lanes(i * 128, 128)
        drun = ext[0:rows, cols]
        total = drun * conv_w[CONV - 1 : CONV, cols]
        for tap in range(CONV - 1):
            ahead = CONV - 1 - tap
            total = total + ext[ahead : ahead + rows, cols] * conv_w[tap : tap + 1, cols]
        dproj[:, cols] = total.astype(bf16)
        for tap in range(CONV):
            sums[tap : tap + 1, cols] = jnp.sum(
                drun * pad_in[13 + tap : 13 + tap + rows, cols], axis=0, keepdims=True
            )
        sums[CONV : CONV + 1, cols] = jnp.sum(drun, axis=0, keepdims=True)
        return carry

    lax.fori_loop(0, XBC // 128, channels, 0)
    for v in range(CONV + 1):
        for part in range(3):
            width = min(D, XBC - part * D)
            vec[3 * v + part : 3 * v + part + 1, 0:width] = sums[v : v + 1, part * D : part * D + width]
    dz = dz_in[...].astype(bf16)
    d_normed = dot(dgate[...], w_in[:INNER, :])
    d_normed = d_normed + dot(dproj[...], w_in[INNER : INNER + XBC, :])
    d_normed = d_normed + dot(dz[:, :HEADS], w_in[INNER + XBC :, :])
    src = blk[...].astype(f32)
    scale = lax.rsqrt(jnp.mean(src * src, axis=-1, keepdims=True) + EPS)
    vec[15:16, :] = jnp.sum(d_normed * src * scale, axis=0, keepdims=True)
    gate_gain = jnp.sum(ggain[...], axis=0, keepdims=True)
    vec[16:17, :] = gate_gain[:, :D]
    vec[17:18, :] = gate_gain[:, D:]
    vec[18:21, 0:128] = small_in[0:3, :]
    weighted = d_normed * gain[...]
    average = jnp.mean(weighted * src, axis=-1, keepdims=True)
    gin_out[...] = gout[...].astype(f32) + scale * weighted - src * (scale * scale * scale) * average
    grads_out[:XBC, :] = dot(dproj[...], normed[...], TN).astype(bf16)
    grads_out[XBC:VEC_ROW, :] = dot(dz, normed[...], TN).astype(bf16)
    grads_out[VEC_ROW : VEC_ROW + 32, :] = vec[...].astype(bf16)
    grads_out[VEC_ROW + 32 :, :] = jnp.zeros((REST_ROWS - VEC_ROW - 32, D), bf16)


def last(blk, gout, normed, gain, w_in, conv_w, pad, drun, edge, dz, dgate, ggain, small):
    t = blk.shape[0]
    outs = [((t, D), f32), ((REST_ROWS, D), bf16)]
    scratch = [pltpu.VMEM((t + 8, XBC), f32), pltpu.VMEM((t, XBC), bf16), pltpu.VMEM((32, D), f32), pltpu.VMEM((8, XBC), f32)]
    args = (blk, gout, normed, gain, w_in, conv_w, pad, drun, edge, dz, dgate, ggain, small)
    return call(last_kernel, outs, args, scratch)


ORDERS = (("x", "y", "z1", "z2"), ("y", "x", "z1", "z2"), ("z1", "z2", "x", "y"))
STAGES = 9


def sum_kernel(waves, *refs):
    n = len(waves)
    count = 1 + max(array for array, _, _ in waves)
    ins = [refs[array].at[start : start + rows] for array, start, rows in waves]
    outs = [refs[count + array].at[start : start + rows] for array, start, rows in waves]
    acc, got = refs[2 * count : 2 * count + n], refs[2 * count + n : 2 * count + 2 * n]
    ssem, rsem = refs[2 * count + 2 * n :]
    place = lax.axis_index("seq")
    core = lax.axis_index("head")
    bits = {"c": core, "x": place % 2, "y": place // 2 % 2, "z1": place // 4 % 2, "z2": place // 8}
    steps = {"x": 1, "y": 2, "z1": 4, "z2": 8}

    def partner(d):
        if d == "c":
            return (place, 1 - core)
        return (place + steps[d] * (1 - 2 * bits[d]), core)

    barrier = pltpu.get_barrier_semaphore()
    for d in bits:
        pl.semaphore_signal(barrier, inc=1, device_id=partner(d), device_id_type=MESH)
    pl.semaphore_wait(barrier, len(bits))

    def stream(w, s):
        rows = waves[w][2]
        cols = slice(s * 256, (s + 1) * 256)
        order = ("c",) + ORDERS[s]
        index = w * 3 + s
        keeps, sends = [], []
        off, size = 0, rows
        for d in order[:4]:
            size //= 2
            keeps.append(off + bits[d] * size)
            sends.append(off + (1 - bits[d]) * size)
            off = keeps[-1]
        unit = rows // 16
        base = core * (rows // 2)
        sizes = [rows // 2, rows // 4, rows // 8, unit, unit]
        slots = [0, rows // 2, rows // 2 + rows // 4, rows - 2 * unit, rows - unit]

        def at(start, size):
            return pl.ds(pl.multiple_of(start, 16), size)

        def copy(stage):
            if stage < 5:
                d = order[stage]
                where = sends[stage] if stage < 4 else off
                size = sizes[stage]
                src = ins[w].at[at(where, size), cols] if stage == 0 else acc[w].at[at(where - base, size), cols]
                dst = got[w].at[slice(slots[stage], slots[stage] + size), cols]
            else:
                level = 8 - stage
                d = order[level]
                rows_here = at(keeps[level], sizes[level])
                src = outs[w].at[rows_here, cols]
                dst = outs[w].at[rows_here, cols]
            return pltpu.make_async_remote_copy(
                src_ref=src,
                dst_ref=dst,
                send_sem=ssem.at[index, stage],
                recv_sem=rsem.at[index, stage],
                device_id=partner(d),
                device_id_type=MESH,
            )

        def add(stage):
            where = keeps[stage] if stage < 4 else off
            size = sizes[stage]

            @pl.loop(0, size // unit)
            def _(i):
                here = at(where + i * unit, unit)
                local = at(where - base + i * unit, unit)
                term = got[w][slice(slots[stage], slots[stage] + size), cols] if size == unit else got[w][at(slots[stage] + i * unit, unit), cols]
                if stage == 0:
                    acc[w][local, cols] = ins[w][here, cols] + term
                elif stage < 4:
                    acc[w][local, cols] = acc[w][local, cols] + term
                else:
                    outs[w][here, cols] = acc[w][local, cols] + term

        return copy, add

    streams = {(w, s): stream(w, s) for w in range(n) for s in range(3)}
    for tick in range(STAGES + n):
        for w in range(n):
            stage = tick - w
            for s in range(3):
                copy, add = streams[w, s]
                if 0 < stage <= STAGES:
                    copy(stage - 1).wait()
                    if stage - 1 < 5:
                        add(stage - 1)
                if 0 <= stage < STAGES:
                    copy(stage).start()


def sum_over_devices(*arrays):
    waves = [(k, start, a.shape[0] // 2) for k, a in enumerate(arrays) for start in (0, a.shape[0] // 2)]
    n = len(waves)
    scratch = [pltpu.VMEM((r // 2, D), bf16) for _, _, r in waves] + [pltpu.VMEM((r, D), bf16) for _, _, r in waves]
    scratch += [pltpu.SemaphoreType.DMA((n * 3, STAGES)), pltpu.SemaphoreType.DMA((n * 3, STAGES))]
    return call(
        partial(sum_kernel, waves),
        [(a.shape, bf16) for a in arrays],
        arrays,
        scratch,
        collective_id=2,
        has_side_effects=True,
    )


def shifted(value, ahead):
    groups = lax.axis_size("head")
    count = lax.axis_size("seq") * groups
    moves = []
    for source in range(count):
        piece, half = source // groups, source % groups
        half += ahead
        if half == groups:
            half, piece = 0, piece + SEQS
        elif half < 0:
            half, piece = groups - 1, piece - SEQS
        if 0 <= piece * groups + half < count:
            moves.append((source, piece * groups + half))
    return lax.ppermute(value, ("seq", "head"), moves)


def local(block_in, grad_out, lengths, norm_gain, w_in, conv_w, conv_b, dt_bias, a_log, d_skip, gate_gain, w_out):
    fast = lax.axis_size("seq") == 16 and lax.axis_size("head") == 2
    swap = exchange if fast else exchange_plain
    total = sum_over_devices if fast else lambda *a: lax.psum(a, ("seq", "head"))
    w_in = w_in.T
    heads = jnp.pad(jnp.stack([dt_bias, a_log, d_skip]), ((0, 5), (0, 128 - HEADS)))
    gain = norm_gain.reshape(1, D)
    edge = shifted(block_in[-16:], 1)
    (normed, gate, pad, run, x, xd, xde, b, c, head, cumt, cumb, rows, own) = front(
        lengths, block_in, edge, gain, w_in, conv_w, conv_b.reshape(1, XBC), heads
    )
    enter = swap(own, rows[0:8], False)
    (y, block_out, dy, dye, dgate, ggain, adj, grads_a) = middle(
        lengths, block_in, grad_out, normed, gate, x, xd, b, c, cumt, cumb, rows, enter, gate_gain.reshape(1, INNER), w_out
    )
    leave = swap(adj, rows[0:8], True)
    drun, dz, small = back(
        lengths, y, dy, dye, x, xd, xde, b, c, run, cumt, cumb, head, rows, heads, enter, own, leave
    )
    edge_back = shifted(drun[0:8], -1)
    grad_in, grads_b = last(
        block_in, grad_out, normed, gain, w_in, conv_w, pad, drun, edge_back, dz, dgate, ggain, small
    )
    grads_a, grads_b = total(grads_a, grads_b)
    grad_w_in = jnp.concatenate([grads_a[:INNER], grads_b[: PROJ - INNER]], axis=0).astype(f32).T
    grad_w_out = grads_a[INNER:].astype(f32)
    vec = grads_b[VEC_ROW : VEC_ROW + 32].astype(f32)
    grad_conv = vec[0:12].reshape(CONV, 3 * D)[:, :XBC]
    grad_bias = vec[12:15].reshape(3 * D)[:XBC]
    grad_norm = vec[15]
    grad_gate = vec[16:18].reshape(INNER)
    grad_dt = vec[18, :HEADS]
    grad_alog = vec[19, :HEADS]
    grad_skip = vec[20, :HEADS]
    return (
        block_out,
        grad_in,
        grad_norm,
        grad_w_in,
        grad_conv,
        grad_bias,
        grad_dt,
        grad_alog,
        grad_skip,
        grad_gate,
        grad_w_out,
    )


def solution(mesh):
    rows = P(("seq", "head"), None)
    return jax.shard_map(
        local,
        mesh=mesh,
        in_specs=(rows, rows) + (P(),) * 10,
        out_specs=(rows, rows) + (P(),) * 9,
        check_vma=False,
    )
```

time: 1030 us -> 227 us (0.22); the launches traced: 1020 us -> 227 us
  waiting for transfers between devices: 409 us -> 1.66 us
  Pallas kernels: 0 us -> 196 us
  local copies, waits for them, and re-layouts: 185 us -> 13 us
  blocking collectives: 171 us -> 0 us
  other arithmetic: 118 us -> 12 us
  matrix products: 99.5 us -> 0 us
  between operations: 15.6 us -> 0.71 us
  starting transfers between devices: 18.3 us -> 3.81 us
    all_gather x2 -> x0, waiting for transfers between devices: 206 us -> none  [entering(): gathered = jax.tree.map(lambda a: lax.all_gather(a, axis), part)]
    psum x1 -> x0, waiting for transfers between devices: 202 us -> none  [local(): lax.psum((grad_norm, grad_w_in, grad_conv, grad_bias, grad_dt, grad_alog,...]
    pallas_call x0 -> x7, Pallas kernels: none -> 196 us  [call(): pl.pallas_call(body, out_shape=[jax.ShapeDtypeStruct(s, d) for s, d in ou...]
    dot_general x32 -> x0, matrix products: 99.5 us -> none  [the longest x6 34.4 us: block_step(): inner_part = jnp.einsum('tuh,uhp->thp', weight, x_heads, precision=best)]
    all_gather x2 -> x0, blocking collectives: 95.8 us -> none  [entering(): gathered = jax.tree.map(lambda a: lax.all_gather(a, axis), part)]
    dynamic_update_slice x21 -> x0, local copies, waits for them, and re-layouts: 72.7 us -> none  [the longest x18 71.9 us: mixer(): lax.scan(partial(block_step, rates), incoming, (blocks(x_heads), blocks(b...]
    psum x1 -> x0, blocking collectives: 45.2 us -> none  [local(): lax.psum((grad_norm, grad_w_in, grad_conv, grad_bias, grad_dt, grad_alog,...]
    unnamed x229 -> x4, local copies, waits for them, and re-layouts: 32.9 us -> 1.23 us
  transfers between devices with their start and end apart: 9 -> 2, of which waited for: 4 -> 1; matrix products, arithmetic and copies ran while one was open for 8% -> 2% of each run, Pallas kernels for 0% -> 0%
where the time goes in v1:
time: 227 us
  Pallas kernels  196 us (86%)
  local copies, waits for them, and re-layouts  13 us (6%)
  other arithmetic  12 us (5%)
  starting transfers between devices  3.81 us (2%)
    pallas_call x7, Pallas kernels, call(): pl.pallas_call(body, out_shape=[jax.ShapeDtypeStruct(s, d) for s, d in ou...  196 us
    convert_element_type x1, other arithmetic, local(): grad_w_out = grads_a[INNER:].astype(f32)  5.06 us
    transpose x1, other arithmetic, local(): jnp.concatenate([grads_a[:INNER], grads_b[:PROJ - INNER]], axis=0)  4.83 us
  transfers between devices with their start and end apart: 2, of which 1 were waited for; matrix products, arithmetic and copies ran while one was open for 2% of the time, Pallas kernels for 0%

profile of v1, /device:TPU:0, one launch (start us, length us, event | category | flops | bytes accessed | tf_op | source)
XLA Modules:
  0.0 226.8 jit_solution(12299253334446866227)
XLA Ops:
  0.6 0.7 slice.49
  1.4 2.3 %collective-permute-start = (bf16[16,768]{1,0:T(8,128)(2,1)S(1)}, bf16[16,768]{1,0:T(8,128)(2,1)S(1)}, u32[]{:S(2)}, u32[]{:S(2)}) collective-permute-start(bf16[16,768]{1,0:T(8,128)(2,1)S(1)} %slice.49), channel_id=1, source_target_pairs={{0,1},{1,4},{2,3},{3,6},{4,5},{5,8},{6,7},{7,10},{8,9},{9,12},{10,... | collective-permute-start | bytes 73736 | tf_op jit(solution)/shard_map/ppermute | solution.py:790
  3.7 1.3 select_maximum_fusion.heads_ref
  5.0 1.3 reshape.40.gain
  6.3 1.3 reshape.42.gain
  7.6 1.3 reshape.41.conv_b
  8.9 0.0 collective-permute-done.edge
  8.9 0.0 copy-start.1
  8.9 0.6 copy-done.1
  9.5 16.8 %shard_map.203 = (bf16[256,768]{1,0:T(8,128)(2,1)}, bf16[256,1536]{1,0:T(8,128)(2,1)}, f32[272,1792]{1,0:T(8,128)}, f32[256,1792]{1,0:T(8,128)}, f32[256,1536]{1...) custom-call(s32[2]{0:T(128)} %lengths_ref.5, ...), custom_call_target="tpu_custom_call" | custom-call | tf_op jit(solution)/shard_map/pallas_call | solution.py:81
  26.3 1.4 slice.50.decay
  27.7 26.3 %shard_map.204.enter = bf16[128,1536]{1,0:T(8,128)(2,1)} custom-call(f32[128,1536]{1,0:T(8,128)} %get-tuple-element.49.state.own, f32[8,1536]{1,0:T(8,128)} %slice.50.decay), custom_call_target="tpu_custom_call" | custom-call | tf_op jit(solution)/shard_map/pallas_call | solution.py:81
  54.0 16.8 %shard_map.205 = (f32[256,1536]{1,0:T(8,128)}, bf16[256,768]{1,0:T(8,128)(2,1)}, bf16[256,1536]{1,0:T(8,128)(2,1)}, bf16[256,1536]{1,0:T(8,128)(2,1)}, bf16[256,...) custom-call(s32[2]{0:T(128)} %lengths_ref.5, bf16[256,768]{1,0:T(8,128)(2,1)} %blk.5, ...), custom_call_target="tpu_custom_call" | custom-call | tf_op jit(solution)/shard_map/pallas_call | solution.py:81
  70.8 23.7 %shard_map.206.leave = bf16[128,1536]{1,0:T(8,128)(2,1)} custom-call(f32[128,1536]{1,0:T(8,128)} %get-tuple-element.58.state, f32[8,1536]{1,0:T(8,128)} %slice.50.decay), custom_call_target="tpu_custom_call" | custom-call | tf_op jit(solution)/shard_map/pallas_call | solution.py:81
  94.5 14.6 %shard_map.207 = (f32[256,1792]{1,0:T(8,128)}, f32[256,128]{1,0:T(8,128)}, f32[8,128]{1,0:T(8,128)}) custom-call(s32[2]{0:T(128)} %lengths_ref.5, f32[256,1536]{1,0:T(8,128)} %get-tuple-element.52.y_in, bf16[256,1536]{1,0:T(8,128)(2,1)} %get-tuple-element.53.dy_in, bf16[256,1536]{1,0:T(8,128)(2,1)} %get-tuple-element.54.dye_in, ...), custom_call_target="tpu_custom_call" | custom-call | tf_op jit(solution)/shard_map/pallas_call | solution.py:81
  109.1 0.8 slice.51
  109.9 1.5 collective-permute-start.1
  111.4 1.7 collective-permute-done.1.edge
  113.1 0.0 copy-start
  113.1 0.6 copy-done
  113.7 10.5 %shard_map.208 = (f32[256,768]{1,0:T(8,128)}, bf16[2048,768]{1,0:T(8,128)(2,1)}) custom-call(bf16[256,768]{1,0:T(8,128)(2,1)} %blk.5, bf16[256,768]{1,0:T(8,128)(2,1)} %gout.3, bf16[256,768]{1,0:T(8,128)(2,1)} %get-tuple-element.40.normed, f32[1,768]{1,0:T(1,128)} %reshape.40.gain, bf16[3352,768]{1,0:T(8,128)(2,1)} %bitcast.13, f32[4,1792]{1,0:T(4,128)} %conv_w.3, ...), custom_call_target="tpu_custom_call" | custom-call | tf_op jit(solution)/shard_map/pallas_call | solution.py:81
  124.1 87.0 %shard_map.209 = (bf16[3072,768]{1,0:T(8,128)(2,1)}, bf16[2048,768]{1,0:T(8,128)(2,1)}) custom-call(bf16[3072,768]{1,0:T(8,128)(2,1)} %get-tuple-element.65.refs_0_, bf16[2048,768]{1,0:T(8,128)(2,1)} %get-tuple-element.66.refs_1_), custom_call_target="tpu_custom_call" | custom-call | tf_op jit(solution)/shard_map/pallas_call | solution.py:81
  211.2 0.8 slice_convert_fusion.1
  212.0 2.0 slice.55
  213.9 0.5 slice_bitcast_fusion
  214.5 0.6 slice_reduce_fusion
  215.1 0.6 reshape.45
  215.7 0.6 slice.67
  216.3 0.6 slice.69
  216.9 5.1 %slice_convert_fusion = (f32[1536,768]{1,0:T(8,128)}, bf16[1536,768]{1,0:T(8,128)(2,1)S(1)}) fusion(bf16[3072,768]{1,0:T(8,128)(2,1)} %get-tuple-element.68), kind=kLoop, calls=%fused_computation.1 | loop fusion | flops 1179648 | bytes 11796480 | tf_op jit(solution)/shard_map/convert_element_type | solution.py:818
  222.0 4.8 %convert_bitcast_fusion = f32[768,3352]{0,1:T(8,128)} fusion(bf16[1816,768]{1,0:T(8,128)(2,1)S(1)} %slice.55, bf16[1536,768]{1,0:T(8,128)(2,1)S(1)} %get-tuple-element.70), kind=kLoop, calls=%fused_computation | loop fusion | flops 10297344 | bytes 15446016 | tf_op jit(solution)/shard_map/transpose | solution.py:817
  (5 shorter events, 0.0 us)
Async XLA Ops:
  1.4 7.5 %collective-permute-start = (bf16[16,768]{1,0:T(8,128)(2,1)S(1)}, bf16[16,768]{1,0:T(8,128)(2,1)S(1)}, u32[]{:S(2)}, u32[]{:S(2)}) collective-permute-start(bf16[16,768]{1,0:T(8,128)(2,1)S(1)} %slice.49), channel_id=1, source_target_pairs={{0,1},{1,4},{2,3},{3,6},{4,5},{5,8},{6,7},{7,10},{8,9},{9,12},{10,... | collective-permute-start | bytes 73736 | tf_op jit(solution)/shard_map/ppermute | solution.py:790
  8.9 0.6 copy-start.1
  109.9 3.1 %collective-permute-start.1 = (f32[8,1792]{1,0:T(8,128)S(1)}, f32[8,1792]{1,0:T(8,128)S(1)}, u32[]{:S(2)}, u32[]{:S(2)}) collective-permute-start(f32[8,1792]{1,0:T(8,128)S(1)} %slice.51), channel_id=1, source_target_pairs={{1,0},{3,2},{4,1},{5,4},{6,3},{7,6},{8,5},{9,8},{10,7},{11,10},{12... | collective-permute-start | bytes 172040 | tf_op jit(solution)/shard_map/ppermute | solution.py:790
  113.1 0.6 copy-start

commit v2 on v1

--- a/solution.py
+++ b/solution.py
@@ -70,7 +70,7 @@
     return pl.ds(pl.multiple_of(start, 128), size)
 
 
-def valid_rows(lengths_ref, per_row, rows, width):
+def valid_rows(lengths_ref, rows, width):
     place = lax.axis_index("seq")
     first = (place // SEQS) * (rows * lax.axis_size("head")) + lax.axis_index("head") * rows
     limit = lengths_ref[place % SEQS]
@@ -86,6 +86,12 @@
         scratch_shapes=list(scratch),
         compiler_params=pltpu.CompilerParams(vmem_limit_bytes=vmem, **params),
     )(*args)
+
+
+VEC_ROW = XBC + 128
+REST_ROWS = 2048
+FIRST_ROWS = 2 * INNER
+WAVES = 4
 
 
 def front_kernel(
@@ -125,7 +131,7 @@
     ahead = norm(edge[...])
     pad_out[0:16, :] = dot(ahead, w_in[INNER : INNER + XBC, :], NT).astype(bf16).astype(f32)
     pad_out[16 : 16 + rows, :] = dot(normed, w_in[INNER : INNER + XBC, :], NT).astype(bf16).astype(f32)
-    keep = valid_rows(lengths_ref, None, rows, 128)
+    keep = valid_rows(lengths_ref, rows, 128)
     head_out[3] = jnp.zeros((rows, 128), f32)
     head_out[3, :, 0:HEADS] = dot(normed, w_in[INNER + XBC :, :], NT).astype(bf16).astype(f32)
     lane = iota((rows, 128), 1)
@@ -163,7 +169,7 @@
     act = convolve(INNER // 256)
     b_out[...] = act[:, :STATE].astype(bf16)
     c_out[...] = act[:, STATE:].astype(bf16)
-    keep2 = valid_rows(lengths_ref, None, rows, 256)
+    keep2 = valid_rows(lengths_ref, rows, 256)
 
     def channels(i, carry):
         cols = lanes(i * 256, 256)
@@ -202,121 +208,6 @@
         ((STATE, INNER), f32),
     ]
     return call(front_kernel, outs, (lengths, blk, edge, gain, w_in, conv_w, conv_b, heads), smem=(0,))
-
-
-def exchange_kernel(reverse, state, decay, out, sib_state, sib_decay, mine, total, got, got_decay, back, back_got, ssem, rsem):
-    half = INNER // 2
-    chips = lax.axis_size("seq") // SEQS
-    rows = STATE // chips
-    place = lax.axis_index("seq")
-    core = lax.axis_index("head")
-    chip = place // SEQS
-    which = place % SEQS
-    sibling = (place, 1 - core)
-    rank = 1 - core if reverse else core
-    barrier = pltpu.get_barrier_semaphore()
-    pl.semaphore_signal(barrier, inc=1, device_id=sibling, device_id_type=MESH)
-
-    def peer(k):
-        return (lax.rem(chip + k, chips) * SEQS + which, core)
-
-    for k in range(1, chips):
-        pl.semaphore_signal(barrier, inc=1, device_id=peer(k), device_id_type=MESH)
-    pl.semaphore_wait(barrier, chips)
-    own_cols = lanes(core * half, half)
-    sib_cols = lanes((1 - core) * half, half)
-
-    def copy(src, dst, n, to):
-        return pltpu.make_async_remote_copy(
-            src_ref=src, dst_ref=dst, send_sem=ssem.at[n], recv_sem=rsem.at[n], device_id=to, device_id_type=MESH
-        )
-
-    first = [
-        copy(state.at[:, sib_cols], sib_state, 0, sibling),
-        copy(decay.at[:, sib_cols], sib_decay, 1, sibling),
-    ]
-    for c in first:
-        c.start()
-    for c in first:
-        c.wait()
-    own = state[:, own_cols]
-    own_decay = decay[0:1, own_cols]
-    other = sib_state[...]
-    other_decay = sib_decay[0:1, :]
-    later = rank == 1
-    late_decay = jnp.where(later, own_decay, other_decay)
-    early_decay = jnp.where(later, other_decay, own_decay)
-    early = jnp.where(later, other, own)
-    late = jnp.where(later, own, other)
-    mine[...] = (late_decay * early + late).astype(bf16)
-    total[...] = jnp.broadcast_to(own_decay * other_decay, total.shape)
-    second = []
-    for k in range(1, chips):
-        to = lax.rem(chip + k, chips)
-        piece = pl.ds(pl.multiple_of(to * rows, rows), rows)
-        second.append(copy(mine.at[piece], got.at[k], 2 * k, peer(k)))
-        second.append(copy(total, got_decay.at[k], 2 * k + 1, peer(k)))
-    for c in second:
-        c.start()
-    got[0] = mine[pl.ds(pl.multiple_of(chip * rows, rows), rows), :]
-    got_decay[0] = total[...]
-    for c in second:
-        c.wait()
-
-    def scan(i, carry):
-        source = chips - 1 - i if reverse else i
-        slot = lax.rem(chip - source + chips, chips)
-        to = lax.rem(source - chip + chips, chips)
-        back[pl.ds(to, 1)] = carry.astype(bf16)[None]
-        return got_decay[pl.ds(slot, 1)][0, 0:1, :] * carry + got[pl.ds(slot, 1)][0].astype(f32)
-
-    lax.fori_loop(0, chips, scan, jnp.zeros((rows, half), f32))
-    third = []
-    here = pl.ds(pl.multiple_of(chip * rows, rows), rows)
-    base = 2 * chips
-    for k in range(1, chips):
-        third.append(copy(back.at[k], back_got.at[here], base + k, peer(k)))
-    for c in third:
-        c.start()
-    back_got[here, :] = back[0]
-    for c in third:
-        c.wait()
-    enter = back_got[...].astype(f32)
-    second_enter = early_decay * enter + early
-    for_own = jnp.where(later, second_enter, enter).astype(bf16)
-    for_sib = jnp.where(later, enter, second_enter).astype(bf16)
-    out[:, own_cols] = for_own
-    mine[...] = for_sib
-    last = copy(mine, out.at[:, own_cols], base, sibling)
-    last.start()
-    last.wait()
-
-
-def exchange(state, decay, reverse):
-    half = INNER // 2
-    chips = lax.axis_size("seq") // SEQS
-    rows = STATE // chips
-    n = 3 * chips
-    scratch = [
-        pltpu.VMEM((STATE, half), f32),
-        pltpu.VMEM((8, half), f32),
-        pltpu.VMEM((STATE, half), bf16),
-        pltpu.VMEM((8, half), f32),
-        pltpu.VMEM((chips, rows, half), bf16),
-        pltpu.VMEM((chips, 8, half), f32),
-        pltpu.VMEM((chips, rows, half), bf16),
-        pltpu.VMEM((STATE, half), bf16),
-        pltpu.SemaphoreType.DMA((n,)),
-        pltpu.SemaphoreType.DMA((n,)),
-    ]
-    return call(
-        partial(exchange_kernel, reverse),
-        [((STATE, INNER), bf16)],
-        (state, decay),
-        scratch,
-        collective_id=1 if reverse else 0,
-        has_side_effects=True,
-    )[0]
 
 
 def exchange_plain(state, decay, reverse):
@@ -408,7 +299,7 @@
         return carry
 
     lax.fori_loop(0, rows // step, gating, 0)
-    keep = valid_rows(lengths_ref, None, rows, D)
+    keep = valid_rows(lengths_ref, rows, D)
     db_s[...] = (gout[...].astype(f32) * keep).astype(bf16)
     dgn_s[...] = dot(db_s[...], w_out[...], NT)
     block_out[...] = (blk[...].astype(f32) + keep * dot(gn_s[...], w_out[...])).astype(bf16)
@@ -503,7 +394,7 @@
     q_s[...] = jnp.zeros_like(q_s)
     ry_s[...] = jnp.zeros_like(ry_s)
     lane = iota((rows, 128), 1)
-    keep = valid_rows(lengths_ref, None, rows, 128)
+    keep = valid_rows(lengths_ref, rows, 128)
     left = one_hot(iota((1, 128), 1) < HEAD_DIM)
     right = one_hot(iota((1, 128), 1) >= HEAD_DIM)
     pick_lane = iota((128, 128), 0)
@@ -581,10 +472,6 @@
     return call(back_kernel, outs, args, scratch, smem=(0,))
 
 
-VEC_ROW = XBC + 128
-REST_ROWS = 2048
-
-
 def last_kernel(
     blk,
     gout,
@@ -659,37 +546,154 @@
     return call(last_kernel, outs, args, scratch)
 
 
+class Refs:
+    def __init__(self, names, refs):
+        self.__dict__.update(zip(names, refs, strict=True))
+
+
+def remote(src, dst, ssem, rsem, to):
+    return pltpu.make_async_remote_copy(
+        src_ref=src, dst_ref=dst, send_sem=ssem, recv_sem=rsem, device_id=to, device_id_type=MESH
+    )
+
+
+class Exchange:
+    def __init__(self, reverse, state, decay, out, bufs, ssem, rsem):
+        self.sib_state, self.sib_decay, self.mine, self.total, self.got, self.got_decay, self.back, self.back_got = bufs
+        self.state, self.decay, self.out, self.reverse = state, decay, out, reverse
+        self.ssem, self.rsem = ssem, rsem
+        self.half = INNER // 2
+        self.chips = lax.axis_size("seq") // SEQS
+        self.rows = STATE // self.chips
+        self.place, self.core = lax.axis_index("seq"), lax.axis_index("head")
+        self.chip, self.which = self.place // SEQS, self.place % SEQS
+        self.sibling = (self.place, 1 - self.core)
+        self.later = (1 - self.core if reverse else self.core) == 1
+        self.own_cols = lanes(self.core * self.half, self.half)
+        self.sib_cols = lanes((1 - self.core) * self.half, self.half)
+        self.flying = []
+
+    def peer(self, k):
+        return (lax.rem(self.chip + k, self.chips) * SEQS + self.which, self.core)
+
+    def send(self, copies):
+        self.flying = [remote(src, dst, self.ssem.at[n], self.rsem.at[n], to) for src, dst, n, to in copies]
+        for c in self.flying:
+            c.start()
+
+    def arrive(self):
+        for c in self.flying:
+            c.wait()
+
+    def begin(self):
+        self.send(
+            [
+                (self.state.at[:, self.sib_cols], self.sib_state, 0, self.sibling),
+                (self.decay.at[0:8, self.sib_cols], self.sib_decay, 1, self.sibling),
+            ]
+        )
+
+    def ordered(self):
+        own, other = self.state[:, self.own_cols], self.sib_state[...]
+        own_decay, other_decay = self.decay[0:1, self.own_cols], self.sib_decay[0:1, :]
+        later = self.later
+        return (
+            jnp.where(later, other, own),
+            jnp.where(later, own, other),
+            jnp.where(later, other_decay, own_decay),
+            jnp.where(later, own_decay, other_decay),
+        )
+
+    def deal(self):
+        self.arrive()
+        early, late, early_decay, late_decay = self.ordered()
+        self.mine[...] = (late_decay * early + late).astype(bf16)
+        self.total[...] = jnp.broadcast_to(early_decay * late_decay, self.total.shape)
+        copies = []
+        for k in range(1, self.chips):
+            to = lax.rem(self.chip + k, self.chips)
+            piece = pl.ds(pl.multiple_of(to * self.rows, self.rows), self.rows)
+            copies.append((self.mine.at[piece], self.got.at[k], 2 * k, self.peer(k)))
+            copies.append((self.total, self.got_decay.at[k], 2 * k + 1, self.peer(k)))
+        self.send(copies)
+        self.got[0] = self.mine[pl.ds(pl.multiple_of(self.chip * self.rows, self.rows), self.rows), :]
+        self.got_decay[0] = self.total[...]
+
+    def scan(self):
+        self.arrive()
+        chips, chip = self.chips, self.chip
+
+        def one(i, carry):
+            source = chips - 1 - i if self.reverse else i
+            slot = lax.rem(chip - source + chips, chips)
+            to = lax.rem(source - chip + chips, chips)
+            self.back[pl.ds(to, 1)] = carry.astype(bf16)[None]
+            return self.got_decay[pl.ds(slot, 1)][0, 0:1, :] * carry + self.got[pl.ds(slot, 1)][0].astype(f32)
+
+        lax.fori_loop(0, chips, one, jnp.zeros((self.rows, self.half), f32))
+        here = pl.ds(pl.multiple_of(chip * self.rows, self.rows), self.rows)
+        self.send([(self.back.at[k], self.back_got.at[here], 2 * chips + k, self.peer(k)) for k in range(1, chips)])
+        self.back_got[here, :] = self.back[0]
+
+    def hand(self):
+        self.arrive()
+        early, _, early_decay, _ = self.ordered()
+        enter = self.back_got[...].astype(f32)
+        second = early_decay * enter + early
+        self.out[:, self.own_cols] = jnp.where(self.later, second, enter).astype(bf16)
+        self.mine[...] = jnp.where(self.later, enter, second).astype(bf16)
+        self.send([(self.mine, self.out.at[:, self.own_cols], 2 * self.chips, self.sibling)])
+
+
+def exchange_scratch(chips):
+    half, rows, n = INNER // 2, STATE // chips, 3 * chips
+    return [
+        pltpu.VMEM((STATE, half), f32),
+        pltpu.VMEM((8, half), f32),
+        pltpu.VMEM((STATE, half), bf16),
+        pltpu.VMEM((8, half), f32),
+        pltpu.VMEM((chips, rows, half), bf16),
+        pltpu.VMEM((chips, 8, half), f32),
+        pltpu.VMEM((chips, rows, half), bf16),
+        pltpu.VMEM((STATE, half), bf16),
+        pltpu.SemaphoreType.DMA((n,)),
+        pltpu.SemaphoreType.DMA((n,)),
+    ]
+
+
 ORDERS = (("x", "y", "z1", "z2"), ("y", "x", "z1", "z2"), ("z1", "z2", "x", "y"))
+STEPS = {"x": 1, "y": 2, "z1": 4, "z2": 8}
 STAGES = 9
 
 
-def sum_kernel(waves, *refs):
-    n = len(waves)
-    count = 1 + max(array for array, _, _ in waves)
-    ins = [refs[array].at[start : start + rows] for array, start, rows in waves]
-    outs = [refs[count + array].at[start : start + rows] for array, start, rows in waves]
-    acc, got = refs[2 * count : 2 * count + n], refs[2 * count + n : 2 * count + 2 * n]
-    ssem, rsem = refs[2 * count + 2 * n :]
+def bits_of():
     place = lax.axis_index("seq")
-    core = lax.axis_index("head")
-    bits = {"c": core, "x": place % 2, "y": place // 2 % 2, "z1": place // 4 % 2, "z2": place // 8}
-    steps = {"x": 1, "y": 2, "z1": 4, "z2": 8}
-
-    def partner(d):
-        if d == "c":
-            return (place, 1 - core)
-        return (place + steps[d] * (1 - 2 * bits[d]), core)
-
-    barrier = pltpu.get_barrier_semaphore()
-    for d in bits:
-        pl.semaphore_signal(barrier, inc=1, device_id=partner(d), device_id_type=MESH)
-    pl.semaphore_wait(barrier, len(bits))
-
-    def stream(w, s):
-        rows = waves[w][2]
+    return {
+        "c": lax.axis_index("head"),
+        "x": place % 2,
+        "y": place // 2 % 2,
+        "z1": place // 4 % 2,
+        "z2": place // 8,
+    }
+
+
+def partner(d):
+    place, core = lax.axis_index("seq"), lax.axis_index("head")
+    if d == "c":
+        return (place, 1 - core)
+    return (place + STEPS[d] * (1 - 2 * bits_of()[d]), core)
+
+
+class Sum:
+    def __init__(self, held, got, out, ssem, rsem, lsem):
+        self.streams = [self.stream(held, got, out, ssem, rsem, lsem, s) for s in range(3)]
+        self.stage = -1
+
+    def stream(self, held, got, out, ssem, rsem, lsem, s):
+        rows = held.shape[0]
+        bits = bits_of()
         cols = slice(s * 256, (s + 1) * 256)
         order = ("c",) + ORDERS[s]
-        index = w * 3 + s
         keeps, sends = [], []
         off, size = 0, rows
         for d in order[:4]:
@@ -698,7 +702,6 @@
             sends.append(off + (1 - bits[d]) * size)
             off = keeps[-1]
         unit = rows // 16
-        base = core * (rows // 2)
         sizes = [rows // 2, rows // 4, rows // 8, unit, unit]
         slots = [0, rows // 2, rows // 2 + rows // 4, rows - 2 * unit, rows - unit]
 
@@ -708,70 +711,475 @@
         def copy(stage):
             if stage < 5:
                 d = order[stage]
-                where = sends[stage] if stage < 4 else off
-                size = sizes[stage]
-                src = ins[w].at[at(where, size), cols] if stage == 0 else acc[w].at[at(where - base, size), cols]
-                dst = got[w].at[slice(slots[stage], slots[stage] + size), cols]
+                where = at(sends[stage] if stage < 4 else off, sizes[stage])
+                src, dst = held.at[where, cols], got.at[slice(slots[stage], slots[stage] + sizes[stage]), cols]
             else:
-                level = 8 - stage
-                d = order[level]
-                rows_here = at(keeps[level], sizes[level])
-                src = outs[w].at[rows_here, cols]
-                dst = outs[w].at[rows_here, cols]
-            return pltpu.make_async_remote_copy(
-                src_ref=src,
-                dst_ref=dst,
-                send_sem=ssem.at[index, stage],
-                recv_sem=rsem.at[index, stage],
-                device_id=partner(d),
-                device_id_type=MESH,
-            )
+                d = order[8 - stage]
+                where = at(keeps[8 - stage], sizes[8 - stage])
+                src, dst = (held if stage == 5 else out).at[where, cols], out.at[where, cols]
+            return remote(src, dst, ssem.at[s, stage], rsem.at[s, stage], partner(d))
 
         def add(stage):
             where = keeps[stage] if stage < 4 else off
-            size = sizes[stage]
-
-            @pl.loop(0, size // unit)
+
+            @pl.loop(0, sizes[stage] // unit)
             def _(i):
                 here = at(where + i * unit, unit)
-                local = at(where - base + i * unit, unit)
-                term = got[w][slice(slots[stage], slots[stage] + size), cols] if size == unit else got[w][at(slots[stage] + i * unit, unit), cols]
-                if stage == 0:
-                    acc[w][local, cols] = ins[w][here, cols] + term
-                elif stage < 4:
-                    acc[w][local, cols] = acc[w][local, cols] + term
-                else:
-                    outs[w][here, cols] = acc[w][local, cols] + term
-
-        return copy, add
-
-    streams = {(w, s): stream(w, s) for w in range(n) for s in range(3)}
-    for tick in range(STAGES + n):
-        for w in range(n):
-            stage = tick - w
-            for s in range(3):
-                copy, add = streams[w, s]
-                if 0 < stage <= STAGES:
-                    copy(stage - 1).wait()
-                    if stage - 1 < 5:
-                        add(stage - 1)
-                if 0 <= stage < STAGES:
-                    copy(stage).start()
-
-
-def sum_over_devices(*arrays):
-    waves = [(k, start, a.shape[0] // 2) for k, a in enumerate(arrays) for start in (0, a.shape[0] // 2)]
-    n = len(waves)
-    scratch = [pltpu.VMEM((r // 2, D), bf16) for _, _, r in waves] + [pltpu.VMEM((r, D), bf16) for _, _, r in waves]
-    scratch += [pltpu.SemaphoreType.DMA((n * 3, STAGES)), pltpu.SemaphoreType.DMA((n * 3, STAGES))]
-    return call(
-        partial(sum_kernel, waves),
-        [(a.shape, bf16) for a in arrays],
-        arrays,
-        scratch,
-        collective_id=2,
-        has_side_effects=True,
+                held[here, cols] = held[here, cols] + got[at(slots[stage] + i * unit, unit), cols]
+
+        def place():
+            return pltpu.make_async_copy(held.at[at(off, unit), cols], out.at[at(off, unit), cols], lsem.at[s])
+
+        return copy, add, place
+
+    def tick(self):
+        for copy, add, place in self.streams:
+            if 0 <= self.stage < STAGES:
+                copy(self.stage).wait()
+                if self.stage < 5:
+                    add(self.stage)
+            if self.stage == 4:
+                place().start()
+            if self.stage == 5:
+                place().wait()
+            if self.stage + 1 < STAGES:
+                copy(self.stage + 1).start()
+        self.stage += 1
+
+
+def greet():
+    place, core = lax.axis_index("seq"), lax.axis_index("head")
+    pieces = lax.axis_size("seq")
+    chips = pieces // SEQS
+    barrier = pltpu.get_barrier_semaphore()
+    peers = [partner(d) for d in ("c", "x", "y", "z1", "z2")]
+    peers += [((place // SEQS + k) % chips * SEQS + place % SEQS, core) for k in range(1, chips)]
+    peers += [block_at(1), block_at(-1)]
+    for to in peers:
+        pl.semaphore_signal(barrier, inc=1, device_id=to, device_id_type=MESH)
+    pl.semaphore_wait(barrier, len(peers))
+
+
+def block_at(ahead):
+    place, core = lax.axis_index("seq"), lax.axis_index("head")
+    pieces = lax.axis_size("seq")
+    block = (place // SEQS * 2 + core + ahead + pieces) % pieces
+    return (block // 2 * SEQS + place % SEQS, block % 2)
+
+
+def whole_kernel(names, *refs):
+    r = Refs(names, refs)
+    rows = r.blk.shape[0]
+    place, core = lax.axis_index("seq"), lax.axis_index("head")
+    chips = lax.axis_size("seq") // SEQS
+    block = place // SEQS * 2 + core
+    loads = [
+        pltpu.make_async_copy(r.w_in_hbm.at[INNER:], r.w_in.at[INNER:], r.load_sem.at[0]),
+        pltpu.make_async_copy(r.w_in_hbm.at[:INNER], r.w_in.at[:INNER], r.load_sem.at[1]),
+        pltpu.make_async_copy(r.w_out_hbm, r.w_out, r.load_sem.at[2]),
+    ]
+    for c in loads:
+        c.start()
+    greet()
+    edge = remote(r.blk.at[rows - 16 :], r.edge, r.edge_sem.at[0], r.edge_sem.at[1], block_at(1))
+    edge.start()
+
+    def norm(v):
+        v = v.astype(f32)
+        scale = lax.rsqrt(jnp.mean(v * v, axis=-1, keepdims=True) + EPS)
+        return (v * scale * r.gain[...]).astype(bf16)
+
+    r.normed[16:, :] = norm(r.blk[...])
+    lane = iota((rows, 128), 1)
+    keep = valid_rows(r.lengths, rows, 128)
+    pick_lane = iota((128, 256), 1)
+    pick_head = iota((128, 256), 0)
+    left = one_hot(iota((1, 128), 1) < HEAD_DIM)
+    right = one_hot(iota((1, 128), 1) >= HEAD_DIM)
+    own_rows = slice(16, 16 + rows)
+
+    loads[0].wait()
+    r.head[3] = jnp.zeros((rows, 128), f32)
+    r.head[3, :, 0:HEADS] = dot(r.normed[own_rows, :], r.w_in[INNER + XBC :, :], NT).astype(bf16).astype(f32)
+    moved = r.head[3] + r.heads[0:1, :]
+    soft = jnp.maximum(moved, 0.0) + jnp.log1p(jnp.exp(-jnp.abs(moved)))
+    dt = jnp.where(lane < HEADS, soft * keep, 0.0)
+    rates = -jnp.exp(r.heads[1:2, :])
+    below = one_hot(iota((rows, rows), 0) >= iota((rows, rows), 1))
+    cum = split_dot_left(below, dt) * rates
+    cum2 = cum * LOG2E
+    r.head[0] = dt
+    r.head[1] = cum
+    r.head[2] = sigmoid(moved) * keep
+    r.head[3] = cum2
+    r.cumt[...] = cum2.T
+
+    def spread(i, carry):
+        r.cumb[:, lanes(i * 256, 256)] = split_dot(r.head[3], one_hot((pick_lane >> 7) + 2 * i == pick_head))
+        return carry
+
+    lax.fori_loop(0, PAIRS, spread, 0)
+
+    edge.wait()
+    r.normed[0:16, :] = jnp.where(block == 0, 0.0, norm(r.edge[...]).astype(f32)).astype(bf16)
+
+    def convolve(i):
+        cols = lanes(i * 256, 256)
+        part = dot(r.normed[...], r.w_in[pl.ds(pl.multiple_of(INNER + i * 256, 256), 256), :], NT)
+        r.pad[:, cols] = part.astype(bf16).astype(f32)
+        running = r.conv_b[:, cols] + r.pad[13 : 13 + rows, cols] * r.conv_w[0:1, cols]
+        for tap in range(1, CONV):
+            running = running + r.pad[13 + tap : 13 + tap + rows, cols] * r.conv_w[tap : tap + 1, cols]
+        r.run[:, cols] = running
+        return running * sigmoid(running)
+
+    act = convolve(INNER // 256)
+    r.b[...] = act[:, :STATE].astype(bf16)
+    r.c[...] = act[:, STATE:].astype(bf16)
+    keep2 = valid_rows(r.lengths, rows, 256)
+
+    def channels(i, carry):
+        cols = lanes(i * 256, 256)
+        pick = one_hot((pick_lane >> 6) + 4 * i == pick_head)
+        x = convolve(i) * keep2
+        r.x[:, cols] = x
+        xd = x * split_dot(r.head[0], pick)
+        r.xd[:, cols] = xd.astype(bf16)
+        wide = split_dot(r.head[3], pick)
+        last = wide[rows - 1 : rows, :]
+        r.xde[:, cols] = (xd * jnp.exp2(last - wide)).astype(bf16)
+        r.spread[0:8, cols] = jnp.broadcast_to(jnp.exp2(last), (8, 256))
+        r.spread[8:16, cols] = split_dot(jnp.broadcast_to(r.heads[2:3, :], (8, 128)), pick)
+        return carry
+
+    lax.fori_loop(0, INNER // 256, channels, 0)
+    r.own[...] = dot(r.b[...], r.xde[...], TN)
+    bufs = 8
+    enter = Exchange(False, r.own, r.spread, r.enter, [getattr(r, f"f{k}") for k in range(bufs)], r.fs, r.fr)
+    leave = Exchange(True, r.adj, r.spread, r.leave, [getattr(r, f"g{k}") for k in range(bufs)], r.gs, r.gr)
+    enter.begin()
+
+    causal = iota((rows, rows), 0) >= iota((rows, rows), 1)
+    r.scores[...] = jnp.where(causal, dot(r.c[...], r.b[...], NT), 0.0)
+    r.scores_t[...] = jnp.where(
+        iota((rows, rows), 1) >= iota((rows, rows), 0), dot(r.b[...], r.c[...], NT), 0.0
     )
+    loads[1].wait()
+    enter.deal()
+
+    def gates(i, carry):
+        part = dot(r.normed[own_rows, :], r.w_in[pl.ds(pl.multiple_of(i * 256, 256), 256), :], NT)
+        r.gate[:, lanes(i * 256, 256)] = part.astype(bf16)
+        return carry
+
+    def columns(i):
+        c0 = r.cumb[:, lanes(i * 256, 128)]
+        c1 = r.cumb[:, lanes(i * 256 + 128, 128)]
+        return c0, c1
+
+    def pair(i, carry):
+        cols = lanes(i * 128, 128)
+        xd = r.xd[:, cols]
+        y = None
+        for cc, part, mask in zip(columns(i), (0, 1), (left, right), strict=True):
+            row = r.cumt[pl.ds(2 * i + part, 1), :]
+            decay = jnp.exp2(jnp.minimum(jnp.concatenate([cc] * (rows // 128), axis=1) - row, 0.0))
+            term = dot((decay * r.scores[...]).astype(bf16), xd * mask)
+            y = term if y is None else y + term
+        r.y[:, cols] = y
+        return carry
+
+    lax.fori_loop(0, INNER // 256, gates, 0)
+    lax.fori_loop(0, PAIRS // 2, pair, 0)
+    enter.scan()
+    lax.fori_loop(PAIRS // 2, PAIRS, pair, 0)
+    enter.hand()
+    keep_d = valid_rows(r.lengths, rows, D)
+    r.db[...] = (r.gout[...].astype(f32) * keep_d).astype(bf16)
+    loads[2].wait()
+    r.wide[...] = dot(r.db[...], r.w_out[...], NT)
+    enter.arrive()
+
+    def carried(i, carry):
+        cols = lanes(i * 128, 128)
+        c0, c1 = columns(i)
+        y = r.y[:, cols] + jnp.exp2(jnp.where(lane < HEAD_DIM, c0, c1)) * dot(r.c[...], r.enter[:, cols])
+        r.y[:, cols] = y
+        r.mixed[:, cols] = (y + r.spread[8:9, cols] * r.x[:, cols]).astype(bf16)
+        return carry
+
+    lax.fori_loop(0, PAIRS, carried, 0)
+
+    r.ggain[...] = jnp.zeros_like(r.ggain)
+    step = 32
+
+    def gating(i, carry):
+        at = pl.ds(pl.multiple_of(i * step, step), step)
+        g = r.gate[at, :].astype(f32)
+        sg = sigmoid(g)
+        mixed = r.mixed[at, :].astype(f32)
+        gated = mixed * g * sg
+        scale = lax.rsqrt(jnp.mean(gated * gated, axis=-1, keepdims=True) + EPS)
+        r.gn[at, :] = (gated * scale * r.gate_gain[...]).astype(bf16)
+        dgn = r.wide[at, :]
+        r.ggain[...] += jnp.sum((dgn * gated * scale).reshape(step // 8, 8, INNER), axis=0)
+        weighted = dgn * r.gate_gain[...]
+        average = jnp.mean(weighted * gated, axis=-1, keepdims=True)
+        d_gated = scale * weighted - gated * (scale * scale * scale) * average
+        r.dy[at, :] = (d_gated * g * sg).astype(bf16)
+        r.dgate[at, :] = (d_gated * mixed * sg * (1.0 + g * (1.0 - sg))).astype(bf16)
+        return carry
+
+    lax.fori_loop(0, rows // step, gating, 0)
+
+    def weigh(i, carry):
+        cols = lanes(i * 128, 128)
+        c0, c1 = columns(i)
+        grow = jnp.exp2(jnp.where(lane < HEAD_DIM, c0, c1))
+        r.dye[:, cols] = (r.dy[:, cols].astype(f32) * grow).astype(bf16)
+        return carry
+
+    lax.fori_loop(0, PAIRS, weigh, 0)
+    r.adj[...] = dot(r.c[...], r.dye[...], TN)
+    leave.begin()
+
+    def gate_grads(i, carry):
+        at = pl.ds(pl.multiple_of(i * 256, 256), 256)
+        r.first[at, :] = dot(r.dgate[:, lanes(i * 256, 256)], r.normed[own_rows, :], TN).astype(bf16)
+        return carry
+
+    def out_grads(i, carry):
+        at = pl.ds(pl.multiple_of(INNER + i * 256, 256), 256)
+        r.first[at, :] = dot(r.gn[:, lanes(i * 256, 256)], r.db[...], TN).astype(bf16)
+        return carry
+
+    def part(k, held, got, out, at):
+        return Sum(held.at[at], got.at[at], out.at[at], r.ss.at[k], r.rs.at[k], r.ls.at[k])
+
+    half = REST_ROWS // 2
+    sums = [
+        part(0, r.first, r.got_first, r.first_out, slice(0, INNER)),
+        part(1, r.first, r.got_first, r.first_out, slice(INNER, FIRST_ROWS)),
+        part(2, r.rest, r.got_rest, r.rest_out, slice(0, half)),
+        part(3, r.rest, r.got_rest, r.rest_out, slice(half, REST_ROWS)),
+    ]
+    lax.fori_loop(0, INNER // 256, gate_grads, 0)
+    leave.deal()
+    sums[0].tick()
+    lax.fori_loop(0, INNER // 256, out_grads, 0)
+    r.block_out[...] = (r.blk[...].astype(f32) + keep_d * dot(r.gn[...], r.w_out[...])).astype(bf16)
+    sums[1].tick()
+
+    r.dscores[...] = jnp.zeros_like(r.dscores)
+    r.q[...] = jnp.zeros_like(r.q)
+    r.ry[...] = jnp.zeros_like(r.ry)
+    row_head = iota((128, 128), 0)
+    col_head = iota((128, 128), 1)
+
+    def dsilu(cols):
+        running = r.run[:, cols]
+        sg = sigmoid(running)
+        return sg * (1.0 + running * (1.0 - sg))
+
+    def pair_back(i, carry):
+        cols = lanes(i * 128, 128)
+        xd, dy = r.xd[:, cols], r.dy[:, cols]
+        v = None
+        for cc, part, mask in zip(columns(i), (0, 1), (left, right), strict=True):
+            row = r.cumt[pl.ds(2 * i + part, 1), :]
+            decay = jnp.exp2(jnp.minimum(row - jnp.concatenate([cc] * (rows // 128), axis=1), 0.0))
+            masked = dy * mask
+            term = dot((decay * r.scores_t[...]).astype(bf16), masked)
+            v = term if v is None else v + term
+            r.dscores[...] += decay * dot(xd, masked, NT)
+        r.wide[:, cols] = v
+        r.ry[...] += split_dot(dy.astype(f32) * r.y[:, cols], one_hot((row_head >> 6) + 2 * i == col_head))
+        return carry
+
+    lax.fori_loop(0, PAIRS // 2, pair_back, 0)
+    leave.scan()
+    sums[0].tick()
+    lax.fori_loop(PAIRS // 2, PAIRS, pair_back, 0)
+    leave.hand()
+    sums[1].tick()
+    dsc = jnp.where(iota((rows, rows), 1) >= iota((rows, rows), 0), r.dscores[...], 0.0).astype(bf16)
+    d_b = dot(dsc, r.c[...])
+    d_c = dot(dsc, r.b[...], TN) + dot(r.dye[...], r.enter[...], NT)
+    leave.arrive()
+
+    def channels_back(i, carry):
+        cols = lanes(i * 128, 128)
+        c0, c1 = columns(i)
+        c01 = jnp.where(lane < HEAD_DIM, c0, c1)
+        v = r.wide[:, cols] + jnp.exp2(c01[rows - 1 : rows, :] - c01) * dot(r.b[...], r.leave[:, cols])
+        dtw = split_dot(r.head[0], one_hot((col_head >> 6) + 2 * i == row_head))
+        x = r.x[:, cols]
+        dy = r.dy[:, cols].astype(f32)
+        r.q[...] += split_dot(x * v, one_hot((row_head >> 6) + 2 * i == col_head))
+        r.skip[:, cols] = jnp.sum((dy * x).reshape(rows // 8, 8, 128), axis=0)
+        r.ext[0:rows, cols] = (dtw * v + r.spread[8:9, cols] * dy) * keep * dsilu(cols)
+        return carry
+
+    lax.fori_loop(0, PAIRS, channels_back, 0)
+    d_b = d_b + dot(r.xde[...], r.leave[...], NT)
+    r.ext[0:rows, INNER : INNER + STATE] = d_b * dsilu(slice(INNER, INNER + STATE))
+    r.ext[0:rows, INNER + STATE :] = d_c * dsilu(slice(INNER + STATE, XBC))
+    edge_back = remote(r.ext.at[0:8], r.edge_grad, r.edge_sem.at[2], r.edge_sem.at[3], block_at(-1))
+    edge_back.start()
+    sums[0].tick()
+    full_pick = one_hot((iota((INNER, 128), 0) >> 6) == iota((INNER, 128), 1))
+    out_state = r.spread[0:1, :] * r.enter[...].astype(f32) + r.own[...]
+    d_last = split_dot(
+        jnp.sum((r.leave[...].astype(f32) * out_state).reshape(STATE // 8, 8, INNER), axis=0), full_pick
+    )
+    d_last = jnp.sum(d_last, axis=0, keepdims=True)
+    q = r.q[...]
+    d_cum = r.ry[...] - r.head[0] * q + jnp.where(iota((rows, 128), 0) == rows - 1, d_last, 0.0)
+    above = one_hot(iota((rows, rows), 0) <= iota((rows, rows), 1))
+    dz = (q + split_dot_left(above, d_cum * -jnp.exp(r.heads[1:2, :]))) * r.head[2]
+    r.vec[...] = jnp.zeros_like(r.vec)
+    r.vec[18:19, 0:128] = jnp.sum(dz, axis=0, keepdims=True)
+    r.vec[19:20, 0:128] = jnp.sum(d_cum * r.head[1], axis=0, keepdims=True)
+    r.vec[20:21, 0:128] = jnp.sum(split_dot(r.skip[...], full_pick), axis=0, keepdims=True)
+    dz = dz.astype(bf16)
+    d_normed = dot(r.dgate[...], r.w_in[:INNER, :])
+    d_normed = d_normed + dot(dz[:, :HEADS], r.w_in[INNER + XBC :, :])
+    edge_back.wait()
+    r.ext[rows : rows + 8, :] = jnp.where(block == chips * 2 - 1, 0.0, r.edge_grad[...])
+    sums[1].tick()
+
+    def conv_back(i, carry):
+        cols = lanes(i * 128, 128)
+        drun = r.ext[0:rows, cols]
+        total = drun * r.conv_w[CONV - 1 : CONV, cols]
+        for tap in range(CONV - 1):
+            ahead = CONV - 1 - tap
+            total = total + r.ext[ahead : ahead + rows, cols] * r.conv_w[tap : tap + 1, cols]
+        r.dproj[:, cols] = total.astype(bf16)
+        for tap in range(CONV):
+            r.tap_sums[tap : tap + 1, cols] = jnp.sum(
+                drun * r.pad[13 + tap : 13 + tap + rows, cols], axis=0, keepdims=True
+            )
+        r.tap_sums[CONV : CONV + 1, cols] = jnp.sum(drun, axis=0, keepdims=True)
+        return carry
+
+    lax.fori_loop(0, XBC // 128, conv_back, 0)
+
+    def rest_grads(i, carry):
+        at = pl.ds(pl.multiple_of(i * 256, 256), 256)
+        r.rest[at, :] = dot(r.dproj[:, lanes(i * 256, 256)], r.normed[own_rows, :], TN).astype(bf16)
+        return carry
+
+    lax.fori_loop(0, 4, rest_grads, 0)
+    sums[2].tick()
+    sums[0].tick()
+    lax.fori_loop(4, XBC // 256, rest_grads, 0)
+    for v in range(CONV + 1):
+        for part in range(3):
+            width = min(D, XBC - part * D)
+            r.vec[3 * v + part : 3 * v + part + 1, 0:width] = r.tap_sums[v : v + 1, part * D : part * D + width]
+    d_normed = d_normed + dot(r.dproj[...], r.w_in[INNER : INNER + XBC, :])
+    src = r.blk[...].astype(f32)
+    scale = lax.rsqrt(jnp.mean(src * src, axis=-1, keepdims=True) + EPS)
+    r.vec[15:16, :] = jnp.sum(d_normed * src * scale, axis=0, keepdims=True)
+    gate_gain = jnp.sum(r.ggain[...], axis=0, keepdims=True)
+    r.vec[16:17, :] = gate_gain[:, :D]
+    r.vec[17:18, :] = gate_gain[:, D:]
+    r.rest[XBC:VEC_ROW, :] = dot(dz, r.normed[own_rows, :], TN).astype(bf16)
+    r.rest[VEC_ROW : VEC_ROW + 32, :] = r.vec[...].astype(bf16)
+    r.rest[VEC_ROW + 32 :, :] = jnp.zeros((REST_ROWS - VEC_ROW - 32, D), bf16)
+    sums[3].tick()
+    sums[1].tick()
+    weighted = d_normed * r.gain[...]
+    average = jnp.mean(weighted * src, axis=-1, keepdims=True)
+    r.grad_in[...] = r.gout[...].astype(f32) + scale * weighted - src * (scale * scale * scale) * average
+    for _ in range(STAGES + 1):
+        for total in (sums[2], sums[0], sums[3], sums[1]):
+            if total.stage < STAGES:
+                total.tick()
+
+
+def whole(lengths, blk, gout, gain, w_in, conv_w, conv_b, heads, gate_gain, w_out):
+    t = blk.shape[0]
+    chips = lax.axis_size("seq") // SEQS
+    ins = ["lengths", "blk", "gout", "gain", "w_in_hbm", "conv_w", "conv_b", "heads", "gate_gain", "w_out_hbm"]
+    outs = {
+        "block_out": ((t, D), bf16),
+        "grad_in": ((t, D), f32),
+        "first_out": ((FIRST_ROWS, D), bf16),
+        "rest_out": ((REST_ROWS, D), bf16),
+    }
+    held = {
+        "first": ((FIRST_ROWS, D), bf16),
+        "rest": ((REST_ROWS, D), bf16),
+        "w_in": ((PROJ, D), bf16),
+        "w_out": ((INNER, D), bf16),
+        "edge": ((16, D), bf16),
+        "edge_grad": ((8, XBC), f32),
+        "normed": ((t + 16, D), bf16),
+        "gate": ((t, INNER), bf16),
+        "pad": ((t + 16, XBC), f32),
+        "run": ((t, XBC), f32),
+        "x": ((t, INNER), f32),
+        "xd": ((t, INNER), bf16),
+        "xde": ((t, INNER), bf16),
+        "b": ((t, STATE), bf16),
+        "c": ((t, STATE), bf16),
+        "head": ((4, t, 128), f32),
+        "cumt": ((128, t), f32),
+        "cumb": ((t, HEADS * 128), f32),
+        "spread": ((16, INNER), f32),
+        "own": ((STATE, INNER), f32),
+        "enter": ((STATE, INNER), bf16),
+        "y": ((t, INNER), f32),
+        "mixed": ((t, INNER), bf16),
+        "gn": ((t, INNER), bf16),
+        "wide": ((t, INNER), f32),
+        "db": ((t, D), bf16),
+        "dy": ((t, INNER), bf16),
+        "dye": ((t, INNER), bf16),
+        "dgate": ((t, INNER), bf16),
+        "ggain": ((8, INNER), f32),
+        "adj": ((STATE, INNER), f32),
+        "leave": ((STATE, INNER), bf16),
+        "scores": ((t, t), f32),
+        "scores_t": ((t, t), f32),
+        "dscores": ((t, t), f32),
+        "skip": ((8, INNER), f32),
+        "q": ((t, 128), f32),
+        "ry": ((t, 128), f32),
+        "ext": ((t + 8, XBC), f32),
+        "dproj": ((t, XBC), bf16),
+        "vec": ((32, D), f32),
+        "tap_sums": ((8, XBC), f32),
+        "got_first": ((FIRST_ROWS, D), bf16),
+        "got_rest": ((REST_ROWS, D), bf16),
+    }
+    names = ins + list(outs) + list(held)
+    scratch = [pltpu.VMEM(s, d) for s, d in held.values()]
+    for tag in ("f", "g"):
+        scratch += exchange_scratch(chips)
+        names += [f"{tag}{k}" for k in range(8)] + [f"{tag}s", f"{tag}r"]
+    semaphores = {
+        "ss": (WAVES, 3, STAGES),
+        "rs": (WAVES, 3, STAGES),
+        "ls": (WAVES, 3),
+        "edge_sem": (4,),
+        "load_sem": (3,),
+    }
+    for name, shape in semaphores.items():
+        scratch.append(pltpu.SemaphoreType.DMA(shape))
+        names.append(name)
+    any_space = pl.BlockSpec(memory_space=pl.ANY)
+    specs = {"lengths": SMEM, "w_in_hbm": any_space, "w_out_hbm": any_space, "first_out": any_space, "rest_out": any_space}
+    return pl.pallas_call(
+        partial(whole_kernel, names),
+        out_shape=[jax.ShapeDtypeStruct(s, d) for s, d in outs.values()],
+        in_specs=[specs.get(n, VMEM) for n in ins],
+        out_specs=[specs.get(n, VMEM) for n in outs],
+        scratch_shapes=scratch,
+        compiler_params=pltpu.CompilerParams(vmem_limit_bytes=60 << 20, collective_id=0, has_side_effects=True),
+    )(lengths, blk, gout, gain, w_in, conv_w, conv_b, heads, gate_gain, w_out)
 
 
 def shifted(value, ahead):
@@ -790,22 +1198,16 @@
     return lax.ppermute(value, ("seq", "head"), moves)
 
 
-def local(block_in, grad_out, lengths, norm_gain, w_in, conv_w, conv_b, dt_bias, a_log, d_skip, gate_gain, w_out):
-    fast = lax.axis_size("seq") == 16 and lax.axis_size("head") == 2
-    swap = exchange if fast else exchange_plain
-    total = sum_over_devices if fast else lambda *a: lax.psum(a, ("seq", "head"))
-    w_in = w_in.T
-    heads = jnp.pad(jnp.stack([dt_bias, a_log, d_skip]), ((0, 5), (0, 128 - HEADS)))
-    gain = norm_gain.reshape(1, D)
+def by_parts(lengths, block_in, grad_out, gain, w_in, conv_w, conv_b, heads, gate_gain, w_out):
     edge = shifted(block_in[-16:], 1)
     (normed, gate, pad, run, x, xd, xde, b, c, head, cumt, cumb, rows, own) = front(
-        lengths, block_in, edge, gain, w_in, conv_w, conv_b.reshape(1, XBC), heads
+        lengths, block_in, edge, gain, w_in, conv_w, conv_b, heads
     )
-    enter = swap(own, rows[0:8], False)
+    enter = exchange_plain(own, rows[0:8], False)
     (y, block_out, dy, dye, dgate, ggain, adj, grads_a) = middle(
-        lengths, block_in, grad_out, normed, gate, x, xd, b, c, cumt, cumb, rows, enter, gate_gain.reshape(1, INNER), w_out
+        lengths, block_in, grad_out, normed, gate, x, xd, b, c, cumt, cumb, rows, enter, gate_gain, w_out
     )
-    leave = swap(adj, rows[0:8], True)
+    leave = exchange_plain(adj, rows[0:8], True)
     drun, dz, small = back(
         lengths, y, dy, dye, x, xd, xde, b, c, run, cumt, cumb, head, rows, heads, enter, own, leave
     )
@@ -813,7 +1215,25 @@
     grad_in, grads_b = last(
         block_in, grad_out, normed, gain, w_in, conv_w, pad, drun, edge_back, dz, dgate, ggain, small
     )
-    grads_a, grads_b = total(grads_a, grads_b)
+    grads_a, grads_b = lax.psum((grads_a, grads_b), ("seq", "head"))
+    return block_out, grad_in, grads_a, grads_b
+
+
+def local(block_in, grad_out, lengths, norm_gain, w_in, conv_w, conv_b, dt_bias, a_log, d_skip, gate_gain, w_out):
+    run = whole if lax.axis_size("seq") == 16 and lax.axis_size("head") == 2 else by_parts
+    heads = jnp.pad(jnp.stack([dt_bias, a_log, d_skip]), ((0, 5), (0, 128 - HEADS)))
+    block_out, grad_in, grads_a, grads_b = run(
+        lengths,
+        block_in,
+        grad_out,
+        norm_gain.reshape(1, D),
+        w_in.T,
+        conv_w,
+        conv_b.reshape(1, XBC),
+        heads,
+        gate_gain.reshape(1, INNER),
+        w_out,
+    )
     grad_w_in = jnp.concatenate([grads_a[:INNER], grads_b[: PROJ - INNER]], axis=0).astype(f32).T
     grad_w_out = grads_a[INNER:].astype(f32)
     vec = grads_b[VEC_ROW : VEC_ROW + 32].astype(f32)

time: 227 us -> 162 us (0.71)
  Pallas kernels: 196 us -> 138 us
  starting transfers between devices: 3.81 us -> 0 us
  local copies, waits for them, and re-layouts: 13 us -> 10.5 us
    pallas_call x7 -> x1, Pallas kernels: 196 us -> 138 us  [whole(): pl.pallas_call(partial(whole_kernel, names), out_shape=[jax.ShapeDtypeStr...]
    ppermute x2 -> x0, starting transfers between devices: 3.81 us -> none  [shifted(): return lax.ppermute(value, ('seq', 'head'), moves)]
    slice x3 -> x0, local copies, waits for them, and re-layouts: 2.97 us -> none  [the longest x1 1.41 us: local(): enter = swap(own, rows[0:8], False)]
  transfers between devices with their start and end apart: 2 -> 0, of which waited for: 1 -> 0; matrix products, arithmetic and copies ran while one was open for 2% -> 0% of each run, Pallas kernels for 0% -> 0%
where the time goes in v2:
time: 162 us; the launch traced here: 161 us
  Pallas kernels  138 us (85%)
  other arithmetic  12 us (7%)
  local copies, waits for them, and re-layouts  10.5 us (6%)
    pallas_call x1, Pallas kernels, whole(): pl.pallas_call(partial(whole_kernel, names), out_shape=[jax.ShapeDtypeStr...  138 us
    convert_element_type x1, other arithmetic, local(): grad_w_out = grads_a[INNER:].astype(f32)  5.06 us
    transpose x1, other arithmetic, local(): jnp.concatenate([grads_a[:INNER], grads_b[:PROJ - INNER]], axis=0)  4.83 us

profile of v2, /device:TPU:0, one launch (start us, length us, event | category | flops | bytes accessed | tf_op | source)
XLA Modules:
  0.0 161.4 jit_solution(12462023840660044626)
XLA Ops:
  0.6 1.3 reshape.40.refs_3_
  1.9 1.3 select_maximum_fusion.refs_7_
  3.2 1.3 reshape.42.refs_8_
  4.5 1.3 reshape.41.refs_6_
  5.8 138.2 %shard_map.203 = (bf16[256,768]{1,0:T(8,128)(2,1)}, f32[256,768]{1,0:T(8,128)}, bf16[3072,768]{1,0:T(8,128)(2,1)}, bf16[2048,768]{1,0:T(8,128)(2,1)}) custom-call(s32[2]{0:T(128)} %refs_0_.1, bf16[256,768]{1,0:T(8,128)(2,1)} %refs_1_.1, bf16[256,768]{1,0:T(8,128)(2,1)} %refs_2_.1, f32[1,768]{1,0:T(1,128)} %reshape.40.refs_3_, bf16[3352,768]{1,0:T(8,128)(2,1)} %bitcast.12, ...), custom_call_target="tpu_custom_call" | custom-call | tf_op jit(solution)/shard_map/pallas_call | solution.py:1175
  144.0 0.8 slice_convert_fusion.1
  144.8 2.0 %slice.42 = bf16[1816,768]{1,0:T(8,128)(2,1)S(1)} slice(bf16[2048,768]{1,0:T(8,128)(2,1)} %get-tuple-element.17), slice={[0:1816], [0:768]} | slice | bytes 5578752 | tf_op jit(solution)/shard_map/slice | solution.py:1237
  146.8 0.5 slice_bitcast_fusion
  147.3 0.6 slice_reduce_fusion
  148.0 0.6 reshape.45
  148.6 0.6 slice.54
  149.2 0.6 slice.56
  149.8 5.1 %slice_convert_fusion = (f32[1536,768]{1,0:T(8,128)}, bf16[1536,768]{1,0:T(8,128)(2,1)S(1)}) fusion(bf16[3072,768]{1,0:T(8,128)(2,1)} %get-tuple-element.18), kind=kLoop, calls=%fused_computation.1 | loop fusion | flops 1179648 | bytes 11796480 | tf_op jit(solution)/shard_map/convert_element_type | solution.py:1238
  154.9 0.0 copy-start.1
  154.9 0.0 copy-start
  154.9 4.8 %convert_bitcast_fusion = f32[768,3352]{0,1:T(8,128)} fusion(bf16[1816,768]{1,0:T(8,128)(2,1)S(1)} %slice.42, bf16[1536,768]{1,0:T(8,128)(2,1)S(1)} %get-tuple-element.20), kind=kLoop, calls=%fused_computation | loop fusion | flops 10297344 | bytes 15446016 | tf_op jit(solution)/shard_map/transpose | solution.py:1237
  159.7 0.0 copy-done.1
  159.7 0.7 copy.25
  160.5 0.0 copy-done
  160.5 0.9 copy.26
  (5 shorter events, 0.0 us)
Async XLA Ops:
  154.9 4.8 %copy-start.1 = (bf16[256,768]{1,0:T(8,128)(2,1)S(1)}, bf16[256,768]{1,0:T(8,128)(2,1)}, u32[]{:S(2)}) copy-start(bf16[256,768]{1,0:T(8,128)(2,1)} %get-tuple-element.35) | copy-start | bytes 1179652
  154.9 5.6 %copy-start = (f32[256,768]{1,0:T(8,128)S(1)}, f32[256,768]{1,0:T(8,128)}, u32[]{:S(2)}) copy-start(f32[256,768]{1,0:T(8,128)} %get-tuple-element.36) | copy-start | bytes 2359300

commit v3 on v2

--- a/solution.py
+++ b/solution.py
@@ -92,6 +92,7 @@
 REST_ROWS = 2048
 FIRST_ROWS = 2 * INNER
 WAVES = 4
+SPLITS = 2
 
 
 def front_kernel(
@@ -558,19 +559,21 @@
 
 
 class Exchange:
-    def __init__(self, reverse, state, decay, out, bufs, ssem, rsem):
-        self.sib_state, self.sib_decay, self.mine, self.total, self.got, self.got_decay, self.back, self.back_got = bufs
+    def __init__(self, reverse, state, decay, out, bufs, decays, ssem, rsem, start, width):
+        self.sib_state, self.mine, self.got, self.back, self.back_got = bufs
+        self.sib_decay, self.total, self.got_decay = decays
         self.state, self.decay, self.out, self.reverse = state, decay, out, reverse
         self.ssem, self.rsem = ssem, rsem
-        self.half = INNER // 2
         self.chips = lax.axis_size("seq") // SEQS
         self.rows = STATE // self.chips
-        self.place, self.core = lax.axis_index("seq"), lax.axis_index("head")
-        self.chip, self.which = self.place // SEQS, self.place % SEQS
-        self.sibling = (self.place, 1 - self.core)
-        self.later = (1 - self.core if reverse else self.core) == 1
-        self.own_cols = lanes(self.core * self.half, self.half)
-        self.sib_cols = lanes((1 - self.core) * self.half, self.half)
+        self.width = width
+        place, core = lax.axis_index("seq"), lax.axis_index("head")
+        self.core = core
+        self.chip, self.which = place // SEQS, place % SEQS
+        self.sibling = (place, 1 - core)
+        self.later = (1 - core if reverse else core) == 1
+        self.own_cols = lanes(core * (INNER // 2) + start, width)
+        self.sib_cols = lanes((1 - core) * (INNER // 2) + start, width)
         self.flying = []
 
     def peer(self, k):
@@ -586,12 +589,10 @@
             c.wait()
 
     def begin(self):
-        self.send(
-            [
-                (self.state.at[:, self.sib_cols], self.sib_state, 0, self.sibling),
-                (self.decay.at[0:8, self.sib_cols], self.sib_decay, 1, self.sibling),
-            ]
-        )
+        copies = [(self.state.at[:, self.sib_cols], self.sib_state, 0, self.sibling)]
+        if not self.reverse:
+            copies.append((self.decay.at[0:8, self.sib_cols], self.sib_decay, 1, self.sibling))
+        self.send(copies)
 
     def ordered(self):
         own, other = self.state[:, self.own_cols], self.sib_state[...]
@@ -608,16 +609,19 @@
         self.arrive()
         early, late, early_decay, late_decay = self.ordered()
         self.mine[...] = (late_decay * early + late).astype(bf16)
-        self.total[...] = jnp.broadcast_to(early_decay * late_decay, self.total.shape)
+        if not self.reverse:
+            self.total[...] = jnp.broadcast_to(early_decay * late_decay, self.total.shape)
         copies = []
         for k in range(1, self.chips):
             to = lax.rem(self.chip + k, self.chips)
             piece = pl.ds(pl.multiple_of(to * self.rows, self.rows), self.rows)
             copies.append((self.mine.at[piece], self.got.at[k], 2 * k, self.peer(k)))
-            copies.append((self.total, self.got_decay.at[k], 2 * k + 1, self.peer(k)))
+            if not self.reverse:
+                copies.append((self.total, self.got_decay.at[k], 2 * k + 1, self.peer(k)))
         self.send(copies)
         self.got[0] = self.mine[pl.ds(pl.multiple_of(self.chip * self.rows, self.rows), self.rows), :]
-        self.got_decay[0] = self.total[...]
+        if not self.reverse:
+            self.got_decay[0] = self.total[...]
 
     def scan(self):
         self.arrive()
@@ -630,7 +634,7 @@
             self.back[pl.ds(to, 1)] = carry.astype(bf16)[None]
             return self.got_decay[pl.ds(slot, 1)][0, 0:1, :] * carry + self.got[pl.ds(slot, 1)][0].astype(f32)
 
-        lax.fori_loop(0, chips, one, jnp.zeros((self.rows, self.half), f32))
+        lax.fori_loop(0, chips, one, jnp.zeros((self.rows, self.width), f32))
         here = pl.ds(pl.multiple_of(chip * self.rows, self.rows), self.rows)
         self.send([(self.back.at[k], self.back_got.at[here], 2 * chips + k, self.peer(k)) for k in range(1, chips)])
         self.back_got[here, :] = self.back[0]
@@ -645,20 +649,12 @@
         self.send([(self.mine, self.out.at[:, self.own_cols], 2 * self.chips, self.sibling)])
 
 
-def exchange_scratch(chips):
-    half, rows, n = INNER // 2, STATE // chips, 3 * chips
-    return [
-        pltpu.VMEM((STATE, half), f32),
-        pltpu.VMEM((8, half), f32),
-        pltpu.VMEM((STATE, half), bf16),
-        pltpu.VMEM((8, half), f32),
-        pltpu.VMEM((chips, rows, half), bf16),
-        pltpu.VMEM((chips, 8, half), f32),
-        pltpu.VMEM((chips, rows, half), bf16),
-        pltpu.VMEM((STATE, half), bf16),
-        pltpu.SemaphoreType.DMA((n,)),
-        pltpu.SemaphoreType.DMA((n,)),
-    ]
+def exchange_scratch(chips, width):
+    rows = STATE // chips
+    states = [((STATE, width), f32), ((STATE, width), bf16), ((chips, rows, width), bf16)]
+    states += [((chips, rows, width), bf16), ((STATE, width), bf16)]
+    decays = [((8, width), f32), ((8, width), f32), ((chips, 8, width), f32)]
+    return states, decays
 
 
 ORDERS = (("x", "y", "z1", "z2"), ("y", "x", "z1", "z2"), ("z1", "z2", "x", "y"))
@@ -770,6 +766,12 @@
 def whole_kernel(names, *refs):
     r = Refs(names, refs)
     rows = r.blk.shape[0]
+    r.gain[...] = r.norm_gain[...].reshape(1, D)
+    r.conv_b[...] = r.conv_bias[...].reshape(1, XBC)
+    r.gate_gain[...] = r.gated_gain[...].reshape(1, INNER)
+    r.heads[...] = jnp.zeros((8, 128), f32)
+    for k, one in enumerate((r.dt_bias, r.a_log, r.d_skip)):
+        r.heads[k : k + 1, 0:HEADS] = one[...].reshape(1, HEADS)
     place, core = lax.axis_index("seq"), lax.axis_index("head")
     chips = lax.axis_size("seq") // SEQS
     block = place // SEQS * 2 + core
@@ -814,50 +816,74 @@
     r.head[3] = cum2
     r.cumt[...] = cum2.T
 
-    def spread(i, carry):
-        r.cumb[:, lanes(i * 256, 256)] = split_dot(r.head[3], one_hot((pick_lane >> 7) + 2 * i == pick_head))
-        return carry
-
-    lax.fori_loop(0, PAIRS, spread, 0)
-
     edge.wait()
     r.normed[0:16, :] = jnp.where(block == 0, 0.0, norm(r.edge[...]).astype(f32)).astype(bf16)
 
-    def convolve(i):
-        cols = lanes(i * 256, 256)
-        part = dot(r.normed[...], r.w_in[pl.ds(pl.multiple_of(INNER + i * 256, 256), 256), :], NT)
-        r.pad[:, cols] = part.astype(bf16).astype(f32)
+    def project(start, width):
+        part = dot(r.normed[...], r.w_in[pl.ds(pl.multiple_of(INNER + start, 128), width), :], NT)
+        r.pad[:, lanes(start, width)] = part.astype(bf16).astype(f32)
+
+    def convolve(start, width):
+        cols = lanes(start, width)
         running = r.conv_b[:, cols] + r.pad[13 : 13 + rows, cols] * r.conv_w[0:1, cols]
         for tap in range(1, CONV):
             running = running + r.pad[13 + tap : 13 + tap + rows, cols] * r.conv_w[tap : tap + 1, cols]
         r.run[:, cols] = running
         return running * sigmoid(running)
 
-    act = convolve(INNER // 256)
+    project(INNER, 2 * STATE)
+    act = convolve(INNER, 2 * STATE)
     r.b[...] = act[:, :STATE].astype(bf16)
     r.c[...] = act[:, STATE:].astype(bf16)
-    keep2 = valid_rows(r.lengths, rows, 256)
-
-    def channels(i, carry):
-        cols = lanes(i * 256, 256)
-        pick = one_hot((pick_lane >> 6) + 4 * i == pick_head)
-        x = convolve(i) * keep2
-        r.x[:, cols] = x
-        xd = x * split_dot(r.head[0], pick)
-        r.xd[:, cols] = xd.astype(bf16)
-        wide = split_dot(r.head[3], pick)
-        last = wide[rows - 1 : rows, :]
-        r.xde[:, cols] = (xd * jnp.exp2(last - wide)).astype(bf16)
-        r.spread[0:8, cols] = jnp.broadcast_to(jnp.exp2(last), (8, 256))
-        r.spread[8:16, cols] = split_dot(jnp.broadcast_to(r.heads[2:3, :], (8, 128)), pick)
-        return carry
-
-    lax.fori_loop(0, INNER // 256, channels, 0)
-    r.own[...] = dot(r.b[...], r.xde[...], TN)
-    bufs = 8
-    enter = Exchange(False, r.own, r.spread, r.enter, [getattr(r, f"f{k}") for k in range(bufs)], r.fs, r.fr)
-    leave = Exchange(True, r.adj, r.spread, r.leave, [getattr(r, f"g{k}") for k in range(bufs)], r.gs, r.gr)
-    enter.begin()
+    third = 3 * 128
+
+    def channels(start):
+        project(start, third)
+
+        def one(i, carry):
+            at = start + i * 128
+            cols = lanes(at, 128)
+            pick = one_hot((iota((128, 128), 1) >> 6) + at // HEAD_DIM == iota((128, 128), 0))
+            x = convolve(at, 128) * keep
+            r.x[:, cols] = x
+            xd = x * split_dot(r.head[0], pick)
+            r.xd[:, cols] = xd.astype(bf16)
+            wide = split_dot(r.head[3], pick)
+            last = wide[rows - 1 : rows, :]
+            xde = (xd * jnp.exp2(last - wide)).astype(bf16)
+            r.xde[:, cols] = xde
+            r.spread[0:8, cols] = jnp.broadcast_to(jnp.exp2(last), (8, 128))
+            r.spread[8:16, cols] = split_dot(jnp.broadcast_to(r.heads[2:3, :], (8, 128)), pick)
+            return carry
+
+        lax.fori_loop(0, third // 128, one, 0, unroll=3)
+        r.own[:, start : start + third] = dot(r.b[...], r.xde[:, start : start + third], TN)
+
+    def exchanges(reverse, state, out, tag):
+        made = []
+        for k in range(SPLITS):
+            bufs = [getattr(r, f"{tag}{k}_{n}") for n in range(5)]
+            decays = [getattr(r, f"d{k}_{n}") for n in range(3)]
+            sems = getattr(r, f"{tag}s").at[k], getattr(r, f"{tag}r").at[k]
+            width = INNER // 2 // SPLITS
+            made.append(Exchange(reverse, state, r.spread, out, bufs, decays, *sems, k * width, width))
+        return made
+
+    enters = exchanges(False, r.own, r.enter, "f")
+    leaves = exchanges(True, r.adj, r.leave, "g")
+    channels(0)
+    channels(INNER // 2)
+    enters[0].begin()
+    channels(third)
+    enters[0].deal()
+    channels(INNER // 2 + third)
+    enters[1].begin()
+
+    def spread(i, carry):
+        r.cumb[:, lanes(i * 256, 256)] = split_dot(r.head[3], one_hot((pick_lane >> 7) + 2 * i == pick_head))
+        return carry
+
+    lax.fori_loop(0, PAIRS, spread, 0, unroll=2)
 
     causal = iota((rows, rows), 0) >= iota((rows, rows), 1)
     r.scores[...] = jnp.where(causal, dot(r.c[...], r.b[...], NT), 0.0)
@@ -865,7 +891,7 @@
         iota((rows, rows), 1) >= iota((rows, rows), 0), dot(r.b[...], r.c[...], NT), 0.0
     )
     loads[1].wait()
-    enter.deal()
+    enters[1].deal()
 
     def gates(i, carry):
         part = dot(r.normed[own_rows, :], r.w_in[pl.ds(pl.multiple_of(i * 256, 256), 256), :], NT)
@@ -889,16 +915,20 @@
         r.y[:, cols] = y
         return carry
 
-    lax.fori_loop(0, INNER // 256, gates, 0)
-    lax.fori_loop(0, PAIRS // 2, pair, 0)
-    enter.scan()
-    lax.fori_loop(PAIRS // 2, PAIRS, pair, 0)
-    enter.hand()
+    lax.fori_loop(0, INNER // 256, gates, 0, unroll=2)
+    lax.fori_loop(0, 4, pair, 0, unroll=2)
+    enters[0].scan()
+    lax.fori_loop(4, 8, pair, 0, unroll=2)
+    enters[1].scan()
+    lax.fori_loop(8, PAIRS, pair, 0, unroll=2)
+    enters[0].hand()
     keep_d = valid_rows(r.lengths, rows, D)
     r.db[...] = (r.gout[...].astype(f32) * keep_d).astype(bf16)
     loads[2].wait()
     r.wide[...] = dot(r.db[...], r.w_out[...], NT)
-    enter.arrive()
+    enters[1].hand()
+    for one in enters:
+        one.arrive()
 
     def carried(i, carry):
         cols = lanes(i * 128, 128)
@@ -908,7 +938,7 @@
         r.mixed[:, cols] = (y + r.spread[8:9, cols] * r.x[:, cols]).astype(bf16)
         return carry
 
-    lax.fori_loop(0, PAIRS, carried, 0)
+    lax.fori_loop(0, PAIRS, carried, 0, unroll=2)
 
     r.ggain[...] = jnp.zeros_like(r.ggain)
     step = 32
@@ -939,9 +969,10 @@
         r.dye[:, cols] = (r.dy[:, cols].astype(f32) * grow).astype(bf16)
         return carry
 
-    lax.fori_loop(0, PAIRS, weigh, 0)
+    lax.fori_loop(0, PAIRS, weigh, 0, unroll=2)
     r.adj[...] = dot(r.c[...], r.dye[...], TN)
-    leave.begin()
+    for one in leaves:
+        one.begin()
 
     def gate_grads(i, carry):
         at = pl.ds(pl.multiple_of(i * 256, 256), 256)
@@ -963,10 +994,11 @@
         part(2, r.rest, r.got_rest, r.rest_out, slice(0, half)),
         part(3, r.rest, r.got_rest, r.rest_out, slice(half, REST_ROWS)),
     ]
-    lax.fori_loop(0, INNER // 256, gate_grads, 0)
-    leave.deal()
+    lax.fori_loop(0, INNER // 256, gate_grads, 0, unroll=2)
+    for one in leaves:
+        one.deal()
     sums[0].tick()
-    lax.fori_loop(0, INNER // 256, out_grads, 0)
+    lax.fori_loop(0, INNER // 256, out_grads, 0, unroll=2)
     r.block_out[...] = (r.blk[...].astype(f32) + keep_d * dot(r.gn[...], r.w_out[...])).astype(bf16)
     sums[1].tick()
 
@@ -996,16 +1028,19 @@
         r.ry[...] += split_dot(dy.astype(f32) * r.y[:, cols], one_hot((row_head >> 6) + 2 * i == col_head))
         return carry
 
-    lax.fori_loop(0, PAIRS // 2, pair_back, 0)
-    leave.scan()
+    lax.fori_loop(0, PAIRS // 2, pair_back, 0, unroll=2)
+    for one in leaves:
+        one.scan()
     sums[0].tick()
-    lax.fori_loop(PAIRS // 2, PAIRS, pair_back, 0)
-    leave.hand()
+    lax.fori_loop(PAIRS // 2, PAIRS, pair_back, 0, unroll=2)
+    for one in leaves:
+        one.hand()
     sums[1].tick()
     dsc = jnp.where(iota((rows, rows), 1) >= iota((rows, rows), 0), r.dscores[...], 0.0).astype(bf16)
     d_b = dot(dsc, r.c[...])
     d_c = dot(dsc, r.b[...], TN) + dot(r.dye[...], r.enter[...], NT)
-    leave.arrive()
+    for one in leaves:
+        one.arrive()
 
     def channels_back(i, carry):
         cols = lanes(i * 128, 128)
@@ -1020,7 +1055,7 @@
         r.ext[0:rows, cols] = (dtw * v + r.spread[8:9, cols] * dy) * keep * dsilu(cols)
         return carry
 
-    lax.fori_loop(0, PAIRS, channels_back, 0)
+    lax.fori_loop(0, PAIRS, channels_back, 0, unroll=2)
     d_b = d_b + dot(r.xde[...], r.leave[...], NT)
     r.ext[0:rows, INNER : INNER + STATE] = d_b * dsilu(slice(INNER, INNER + STATE))
     r.ext[0:rows, INNER + STATE :] = d_c * dsilu(slice(INNER + STATE, XBC))
@@ -1063,14 +1098,14 @@
         r.tap_sums[CONV : CONV + 1, cols] = jnp.sum(drun, axis=0, keepdims=True)
         return carry
 
-    lax.fori_loop(0, XBC // 128, conv_back, 0)
+    lax.fori_loop(0, XBC // 128, conv_back, 0, unroll=2)
 
     def rest_grads(i, carry):
         at = pl.ds(pl.multiple_of(i * 256, 256), 256)
         r.rest[at, :] = dot(r.dproj[:, lanes(i * 256, 256)], r.normed[own_rows, :], TN).astype(bf16)
         return carry
 
-    lax.fori_loop(0, 4, rest_grads, 0)
+    lax.fori_loop(0, 4, rest_grads, 0, unroll=2)
     sums[2].tick()
     sums[0].tick()
     lax.fori_loop(4, XBC // 256, rest_grads, 0)
@@ -1099,10 +1134,11 @@
                 total.tick()
 
 
-def whole(lengths, blk, gout, gain, w_in, conv_w, conv_b, heads, gate_gain, w_out):
-    t = blk.shape[0]
+def whole(*args):
+    t = args[0].shape[0]
     chips = lax.axis_size("seq") // SEQS
-    ins = ["lengths", "blk", "gout", "gain", "w_in_hbm", "conv_w", "conv_b", "heads", "gate_gain", "w_out_hbm"]
+    ins = ["blk", "gout", "lengths", "norm_gain", "w_in_hbm", "conv_w", "conv_bias", "dt_bias", "a_log", "d_skip"]
+    ins += ["gated_gain", "w_out_hbm"]
     outs = {
         "block_out": ((t, D), bf16),
         "grad_in": ((t, D), f32),
@@ -1112,6 +1148,10 @@
     held = {
         "first": ((FIRST_ROWS, D), bf16),
         "rest": ((REST_ROWS, D), bf16),
+        "gain": ((1, D), f32),
+        "conv_b": ((1, XBC), f32),
+        "gate_gain": ((1, INNER), f32),
+        "heads": ((8, 128), f32),
         "w_in": ((PROJ, D), bf16),
         "w_out": ((INNER, D), bf16),
         "edge": ((16, D), bf16),
@@ -1157,13 +1197,19 @@
     }
     names = ins + list(outs) + list(held)
     scratch = [pltpu.VMEM(s, d) for s, d in held.values()]
-    for tag in ("f", "g"):
-        scratch += exchange_scratch(chips)
-        names += [f"{tag}{k}" for k in range(8)] + [f"{tag}s", f"{tag}r"]
+    states, decays = exchange_scratch(chips, INNER // 2 // SPLITS)
+    for tag, shapes in (("f", states), ("g", states), ("d", decays)):
+        for k in range(SPLITS):
+            scratch += [pltpu.VMEM(s, d) for s, d in shapes]
+            names += [f"{tag}{k}_{n}" for n in range(len(shapes))]
     semaphores = {
         "ss": (WAVES, 3, STAGES),
         "rs": (WAVES, 3, STAGES),
         "ls": (WAVES, 3),
+        "fs": (SPLITS, 3 * chips),
+        "fr": (SPLITS, 3 * chips),
+        "gs": (SPLITS, 3 * chips),
+        "gr": (SPLITS, 3 * chips),
         "edge_sem": (4,),
         "load_sem": (3,),
     }
@@ -1179,7 +1225,108 @@
         out_specs=[specs.get(n, VMEM) for n in outs],
         scratch_shapes=scratch,
         compiler_params=pltpu.CompilerParams(vmem_limit_bytes=60 << 20, collective_id=0, has_side_effects=True),
-    )(lengths, blk, gout, gain, w_in, conv_w, conv_b, heads, gate_gain, w_out)
+    )(*args)
+
+
+def finish_kernel(
+    block_in,
+    grad_in,
+    first,
+    rest,
+    block_out,
+    grad_out,
+    norm_out,
+    w_in_out,
+    conv_out,
+    bias_out,
+    dt_out,
+    alog_out,
+    skip_out,
+    gate_out,
+    w_out_out,
+    held_first,
+    held_rest,
+    held_block,
+    held_grad,
+    wide_in,
+    wide_out,
+    in_sem,
+    out_sem,
+    pass_sem,
+):
+    passed = [
+        (pltpu.make_async_copy(src, by, pass_sem.at[n, 0]), pltpu.make_async_copy(by, dst, pass_sem.at[n, 1]))
+        for n, (src, by, dst) in enumerate(((block_in, held_block, block_out), (grad_in, held_grad, grad_out)))
+    ]
+    chunks = [(first, held_first, k * 256, 256) for k in range(FIRST_ROWS // 256)]
+    chunks += [(rest, held_rest, k * 256, 256) for k in range(REST_ROWS // 256)]
+    loads = [
+        pltpu.make_async_copy(src.at[start : start + size], dst.at[start : start + size], in_sem.at[n])
+        for n, (src, dst, start, size) in enumerate(chunks)
+    ]
+    ahead = 4
+    for c in loads[:ahead] + [load for load, _ in passed]:
+        c.start()
+    stores = [store for _, store in passed]
+    for n, (src, held, start, size) in enumerate(chunks):
+        loads[n].wait()
+        if n == ahead:
+            for load, store in passed:
+                load.wait()
+                store.start()
+        if n + ahead < len(loads):
+            loads[n + ahead].start()
+        if src is first and start >= INNER:
+            wide, out, at = wide_out, w_out_out, start - INNER
+        else:
+            wide, out, at = wide_in, w_in_out, start if src is first else INNER + start
+        kept = min(size, out.shape[0] - at)
+        if kept <= 0:
+            continue
+        wide[at : at + kept, :] = held[start : start + kept, :].astype(f32)
+        c = pltpu.make_async_copy(wide.at[at : at + kept], out.at[at : at + kept], out_sem.at[n])
+        c.start()
+        stores.append(c)
+    vec = held_rest[VEC_ROW : VEC_ROW + 32, :].astype(f32)
+
+    def row(v):
+        return jnp.concatenate([vec[3 * v + k : 3 * v + k + 1, : min(D, XBC - k * D)] for k in range(3)], axis=1)
+
+    for v in range(CONV):
+        conv_out[v : v + 1, :] = row(v)
+    bias_out[...] = row(CONV).reshape(XBC)
+    norm_out[...] = vec[15:16, :].reshape(D)
+    gate_out[...] = jnp.concatenate([vec[16:17, :], vec[17:18, :]], axis=1).reshape(INNER)
+    for k, out in enumerate((dt_out, alog_out, skip_out)):
+        out[...] = vec[18 + k : 19 + k, 0:HEADS].reshape(HEADS)
+    for c in stores:
+        c.wait()
+
+
+def finish(block_out, grad_in, first, rest):
+    shapes = [block_out.shape, grad_in.shape, (D,), (PROJ, D), (CONV, XBC), (XBC,), (HEADS,), (HEADS,), (HEADS,), (INNER,)]
+    shapes += [(INNER, D)]
+    any_space = pl.BlockSpec(memory_space=pltpu.HBM)
+    away = (0, 1, 3, 10)
+    chunks = (FIRST_ROWS + REST_ROWS) // 256
+    return pl.pallas_call(
+        finish_kernel,
+        out_shape=[jax.ShapeDtypeStruct(s, bf16 if k == 0 else f32) for k, s in enumerate(shapes)],
+        in_specs=[any_space] * 4,
+        out_specs=[any_space if k in away else VMEM for k in range(len(shapes))],
+        scratch_shapes=[
+            pltpu.VMEM((FIRST_ROWS, D), bf16),
+            pltpu.VMEM((REST_ROWS, D), bf16),
+            pltpu.VMEM(block_out.shape, bf16),
+            pltpu.VMEM(grad_in.shape, f32),
+            pltpu.VMEM((PROJ, D), f32),
+            pltpu.VMEM((INNER, D), f32),
+            pltpu.SemaphoreType.DMA((chunks,)),
+            pltpu.SemaphoreType.DMA((chunks,)),
+            pltpu.SemaphoreType.DMA((2, 2)),
+        ],
+        compiler_params=pltpu.CompilerParams(vmem_limit_bytes=60 << 20),
+    )(block_out, grad_in, first, rest)
 
 
 def shifted(value, ahead):
@@ -1198,7 +1345,9 @@
     return lax.ppermute(value, ("seq", "head"), moves)
 
 
-def by_parts(lengths, block_in, grad_out, gain, w_in, conv_w, conv_b, heads, gate_gain, w_out):
+def by_parts(block_in, grad_out, lengths, norm_gain, w_in, conv_w, conv_b, dt_bias, a_log, d_skip, gate_gain, w_out):
+    heads = jnp.pad(jnp.stack([dt_bias, a_log, d_skip]), ((0, 5), (0, 128 - HEADS)))
+    gain, conv_b, gate_gain = norm_gain.reshape(1, D), conv_b.reshape(1, XBC), gate_gain.reshape(1, INNER)
     edge = shifted(block_in[-16:], 1)
     (normed, gate, pad, run, x, xd, xde, b, c, head, cumt, cumb, rows, own) = front(
         lengths, block_in, edge, gain, w_in, conv_w, conv_b, heads
@@ -1219,44 +1368,10 @@
     return block_out, grad_in, grads_a, grads_b
 
 
-def local(block_in, grad_out, lengths, norm_gain, w_in, conv_w, conv_b, dt_bias, a_log, d_skip, gate_gain, w_out):
+def local(block_in, grad_out, lengths, norm_gain, w_in, *others):
     run = whole if lax.axis_size("seq") == 16 and lax.axis_size("head") == 2 else by_parts
-    heads = jnp.pad(jnp.stack([dt_bias, a_log, d_skip]), ((0, 5), (0, 128 - HEADS)))
-    block_out, grad_in, grads_a, grads_b = run(
-        lengths,
-        block_in,
-        grad_out,
-        norm_gain.reshape(1, D),
-        w_in.T,
-        conv_w,
-        conv_b.reshape(1, XBC),
-        heads,
-        gate_gain.reshape(1, INNER),
-        w_out,
-    )
-    grad_w_in = jnp.concatenate([grads_a[:INNER], grads_b[: PROJ - INNER]], axis=0).astype(f32).T
-    grad_w_out = grads_a[INNER:].astype(f32)
-    vec = grads_b[VEC_ROW : VEC_ROW + 32].astype(f32)
-    grad_conv = vec[0:12].reshape(CONV, 3 * D)[:, :XBC]
-    grad_bias = vec[12:15].reshape(3 * D)[:XBC]
-    grad_norm = vec[15]
-    grad_gate = vec[16:18].reshape(INNER)
-    grad_dt = vec[18, :HEADS]
-    grad_alog = vec[19, :HEADS]
-    grad_skip = vec[20, :HEADS]
-    return (
-        block_out,
-        grad_in,
-        grad_norm,
-        grad_w_in,
-        grad_conv,
-        grad_bias,
-        grad_dt,
-        grad_alog,
-        grad_skip,
-        grad_gate,
-        grad_w_out,
-    )
+    outs = finish(*run(block_in, grad_out, lengths, norm_gain, w_in.T, *others))
+    return (*outs[:3], outs[3].T, *outs[4:])
 
 
 def solution(mesh):

time: 162 us -> 139 us (0.86)
  other arithmetic: 12 us -> 0 us
  local copies, waits for them, and re-layouts: 10.5 us -> 0 us
    pallas_call x1, Pallas kernels: 138 us -> 128 us  [whole(): pl.pallas_call(partial(whole_kernel, names), out_shape=[jax.ShapeDtypeStr...]
    pallas_call x0 -> x1, Pallas kernels: none -> 9.82 us  [finish(): pl.pallas_call(finish_kernel, out_shape=[jax.ShapeDtypeStruct(s, bf16 if...]
    convert_element_type x2 -> x0, other arithmetic: 5.87 us -> none  [the longest x1 5.06 us: local(): grad_w_out = grads_a[INNER:].astype(f32)]
    transpose x1 -> x0, other arithmetic: 4.83 us -> none  [local(): jnp.concatenate([grads_a[:INNER], grads_b[:PROJ - INNER]], axis=0)]
    reshape x6 -> x0, local copies, waits for them, and re-layouts: 4.5 us -> none  [the longest x1 1.29 us: local(): conv_b.reshape(1, XBC)]
    slice x7 -> x0, local copies, waits for them, and re-layouts: 3.8 us -> none  [the longest x1 1.97 us: local(): grads_b[:PROJ - INNER]]
    unnamed x6 -> x0, local copies, waits for them, and re-layouts: 1.63 us -> none
where the time goes in v3:
time: 139 us; the launch traced here: 138 us
  Pallas kernels  137 us (99%)
    pallas_call x1, Pallas kernels, whole(): pl.pallas_call(partial(whole_kernel, names), out_shape=[jax.ShapeDtypeStr...  128 us
    pallas_call x1, Pallas kernels, finish(): pl.pallas_call(finish_kernel, out_shape=[jax.ShapeDtypeStruct(s, bf16 if...  9.82 us

profile of v3, /device:TPU:0, one launch (start us, length us, event | category | flops | bytes accessed | tf_op | source)
XLA Modules:
  0.0 138.3 jit_solution(5648808472248112242)
XLA Ops:
  0.6 127.6 %shard_map.203 = (bf16[256,768]{1,0:T(8,128)(2,1)}, f32[256,768]{1,0:T(8,128)}, bf16[3072,768]{1,0:T(8,128)(2,1)}, bf16[2048,768]{1,0:T(8,128)(2,1)}) custom-call(bf16[256,768]{1,0:T(8,128)(2,1)} %refs_0_.1, bf16[256,768]{1,0:T(8,128)(2,1)} %refs_1_.1, s32[2]{0:T(128)} %refs_2_.1, f32[768]{0:T(1024)} %refs_3_.1, bf16[3352,768]{1,0:T(8,128)(2,1)} %bitcast.2, ...), custom_call_target="tpu_custom_call" | custom-call | tf_op jit(solution)/shard_map/pallas_call | solution.py:1221
  128.3 9.8 %shard_map.204 = (bf16[256,768]{1,0:T(8,128)(2,1)}, f32[256,768]{1,0:T(8,128)}, f32[768]{0:T(1024)}, f32[3352,768]{1,0:T(8,128)}, f32[4,1792]{1,0:T(4,128)}, /*i...) custom-call(bf16[256,768]{1,0:T(8,128)(2,1)} %get-tuple-element.26.b, ...), custom_call_target="tpu_custom_call" | custom-call | tf_op jit(solution)/shard_map/pallas_call | solution.py:1312

commit v4 on v3

--- a/solution.py
+++ b/solution.py
@@ -91,7 +91,7 @@
 VEC_ROW = XBC + 128
 REST_ROWS = 2048
 FIRST_ROWS = 2 * INNER
-WAVES = 4
+WAVES = 5
 SPLITS = 2
 
 
@@ -574,19 +574,17 @@
         self.later = (1 - core if reverse else core) == 1
         self.own_cols = lanes(core * (INNER // 2) + start, width)
         self.sib_cols = lanes((1 - core) * (INNER // 2) + start, width)
-        self.flying = []
 
     def peer(self, k):
         return (lax.rem(self.chip + k, self.chips) * SEQS + self.which, self.core)
 
     def send(self, copies):
-        self.flying = [remote(src, dst, self.ssem.at[n], self.rsem.at[n], to) for src, dst, n, to in copies]
-        for c in self.flying:
-            c.start()
-
-    def arrive(self):
-        for c in self.flying:
-            c.wait()
+        for src, dst, n, to in copies:
+            remote(src, dst, self.ssem.at[n % 2], self.rsem.at[n], to).start()
+
+    def arrive(self, *whole):
+        for src, dst, n in whole:
+            remote(src, dst, self.ssem.at[n % 2], self.rsem.at[n], self.sibling).wait()
 
     def begin(self):
         copies = [(self.state.at[:, self.sib_cols], self.sib_state, 0, self.sibling)]
@@ -606,7 +604,10 @@
         )
 
     def deal(self):
-        self.arrive()
+        whole = [(self.state.at[:, self.sib_cols], self.sib_state, 0)]
+        if not self.reverse:
+            whole.append((self.decay.at[0:8, self.sib_cols], self.sib_decay, 1))
+        self.arrive(*whole)
         early, late, early_decay, late_decay = self.ordered()
         self.mine[...] = (late_decay * early + late).astype(bf16)
         if not self.reverse:
@@ -615,16 +616,20 @@
         for k in range(1, self.chips):
             to = lax.rem(self.chip + k, self.chips)
             piece = pl.ds(pl.multiple_of(to * self.rows, self.rows), self.rows)
-            copies.append((self.mine.at[piece], self.got.at[k], 2 * k, self.peer(k)))
+            copies.append((self.mine.at[piece], self.got.at[k], 2, self.peer(k)))
             if not self.reverse:
-                copies.append((self.total, self.got_decay.at[k], 2 * k + 1, self.peer(k)))
+                copies.append((self.total, self.got_decay.at[k], 3, self.peer(k)))
         self.send(copies)
         self.got[0] = self.mine[pl.ds(pl.multiple_of(self.chip * self.rows, self.rows), self.rows), :]
         if not self.reverse:
             self.got_decay[0] = self.total[...]
 
     def scan(self):
-        self.arrive()
+        others = slice(1, self.chips)
+        whole = [(self.got.at[others], self.got.at[others], 2)]
+        if not self.reverse:
+            whole.append((self.got_decay.at[others], self.got_decay.at[others], 3))
+        self.arrive(*whole)
         chips, chip = self.chips, self.chip
 
         def one(i, carry):
@@ -636,17 +641,20 @@
 
         lax.fori_loop(0, chips, one, jnp.zeros((self.rows, self.width), f32))
         here = pl.ds(pl.multiple_of(chip * self.rows, self.rows), self.rows)
-        self.send([(self.back.at[k], self.back_got.at[here], 2 * chips + k, self.peer(k)) for k in range(1, chips)])
+        self.send([(self.back.at[k], self.back_got.at[here], 4, self.peer(k)) for k in range(1, chips)])
         self.back_got[here, :] = self.back[0]
 
     def hand(self):
-        self.arrive()
+        self.arrive((self.back.at[1 : self.chips], self.back.at[1 : self.chips], 4))
         early, _, early_decay, _ = self.ordered()
         enter = self.back_got[...].astype(f32)
         second = early_decay * enter + early
         self.out[:, self.own_cols] = jnp.where(self.later, second, enter).astype(bf16)
         self.mine[...] = jnp.where(self.later, enter, second).astype(bf16)
-        self.send([(self.mine, self.out.at[:, self.own_cols], 2 * self.chips, self.sibling)])
+        self.send([(self.mine, self.out.at[:, self.own_cols], 6, self.sibling)])
+
+    def end(self):
+        self.arrive((self.mine, self.mine, 6))
 
 
 def exchange_scratch(chips, width):
@@ -657,7 +665,81 @@
     return states, decays
 
 
-ORDERS = (("x", "y", "z1", "z2"), ("y", "x", "z1", "z2"), ("z1", "z2", "x", "y"))
+ORDERS = (
+    ("x", "z1", "y", "z2"),
+    ("x", "y", "z2", "z1"),
+    ("z1", "x", "y", "z2"),
+    ("y", "x", "z1", "z2"),
+    ("x", "z1", "y", "z2"),
+    ("y", "x", "z1", "z2"),
+    ("z1", "z2", "y", "x"),
+    ("y", "x", "z2", "z1"),
+    ("x", "y", "z1", "z2"),
+    ("y", "x", "z1", "z2"),
+    ("x", "y", "z2", "z1"),
+    ("z1", "x", "y", "z2"),
+    ("y", "x", "z1", "z2"),
+    ("z1", "x", "y", "z2"),
+    ("x", "y", "z2", "z1"),
+)
+SCHEDULE = {
+    "g2": (
+        2, 0,
+    ),
+    "o2": (
+        0, 5, 2,
+    ),
+    "b0": (
+        1,
+    ),
+    "b1": (
+        5,
+    ),
+    "b2": (
+        1, 4, 3,
+    ),
+    "s": (
+        2, 5, 4,
+    ),
+    "e": (
+        1, 2, 3, 0,
+    ),
+    "h": (
+        1, 5,
+    ),
+    "c1": (
+        2, 4, 0,
+    ),
+    "c3": (
+        1, 5,
+    ),
+    "r1": (
+        8, 7, 6, 0, 4,
+    ),
+    "v2": (
+        3, 2,
+    ),
+    "v3": (
+        6, 8, 1,
+    ),
+    "r2": (
+        11, 9, 7, 2, 11, 5,
+    ),
+    "e1": (
+        8, 3, 6, 9, 1, 0, 10, 7, 4, 11, 8,
+    ),
+    "e2": (
+        10, 7, 2, 11,
+    ),
+    "r3": (
+        12, 9, 1, 12, 11, 13, 7, 3, 0, 6, 10, 4, 14, 14,
+    ),
+    "z": (
+        12, 6, 10, 7, 5, 11, 13, 14, 2, 9, 1, 8, 0, 12, 10, 11, 14, 4, 3, 6, 5, 10, 13, 9, 14, 12, 7, 6, 4,
+        13, 8, 2, 10, 7, 14, 3, 13, 9, 12, 8, 6, 5, 10, 14, 11, 13, 0, 1, 3, 12, 4, 9, 13, 14, 8, 12, 11, 10,
+        6, 9, 7, 13, 3, 14, 14, 11, 12, 10, 8, 0, 5, 13, 9, 6, 7, 8, 4, 13, 12, 3, 9,
+    ),
+}
 STEPS = {"x": 1, "y": 2, "z1": 4, "z2": 8}
 STAGES = 9
 
@@ -681,15 +763,15 @@
 
 
 class Sum:
-    def __init__(self, held, got, out, ssem, rsem, lsem):
-        self.streams = [self.stream(held, got, out, ssem, rsem, lsem, s) for s in range(3)]
-        self.stage = -1
-
-    def stream(self, held, got, out, ssem, rsem, lsem, s):
+    def __init__(self, held, got, out, ssem, rsem, lsem, orders):
+        self.streams = [self.stream(held, got, out, ssem, rsem, lsem, s, order) for s, order in enumerate(orders)]
+        self.stages = [-1] * len(orders)
+
+    def stream(self, held, got, out, ssem, rsem, lsem, s, order):
         rows = held.shape[0]
         bits = bits_of()
         cols = slice(s * 256, (s + 1) * 256)
-        order = ("c",) + ORDERS[s]
+        order = ("c",) + order
         keeps, sends = [], []
         off, size = 0, rows
         for d in order[:4]:
@@ -713,7 +795,7 @@
                 d = order[8 - stage]
                 where = at(keeps[8 - stage], sizes[8 - stage])
                 src, dst = (held if stage == 5 else out).at[where, cols], out.at[where, cols]
-            return remote(src, dst, ssem.at[s, stage], rsem.at[s, stage], partner(d))
+            return remote(src, dst, ssem.at[s], rsem.at[s, stage], partner(d))
 
         def add(stage):
             where = keeps[stage] if stage < 4 else off
@@ -728,19 +810,20 @@
 
         return copy, add, place
 
-    def tick(self):
-        for copy, add, place in self.streams:
-            if 0 <= self.stage < STAGES:
-                copy(self.stage).wait()
-                if self.stage < 5:
-                    add(self.stage)
-            if self.stage == 4:
-                place().start()
-            if self.stage == 5:
-                place().wait()
-            if self.stage + 1 < STAGES:
-                copy(self.stage + 1).start()
-        self.stage += 1
+    def tick(self, s):
+        copy, add, place = self.streams[s]
+        stage = self.stages[s]
+        if 0 <= stage < STAGES:
+            copy(stage).wait()
+            if stage < 5:
+                add(stage)
+        if stage == 4:
+            place().start()
+        if stage == 5:
+            place().wait()
+        if stage + 1 < STAGES:
+            copy(stage + 1).start()
+        self.stages[s] = stage + 1
 
 
 def greet():
@@ -753,7 +836,7 @@
     peers += [block_at(1), block_at(-1)]
     for to in peers:
         pl.semaphore_signal(barrier, inc=1, device_id=to, device_id_type=MESH)
-    pl.semaphore_wait(barrier, len(peers))
+    return barrier, len(peers)
 
 
 def block_at(ahead):
@@ -766,6 +849,14 @@
 def whole_kernel(names, *refs):
     r = Refs(names, refs)
     rows = r.blk.shape[0]
+    greeted = greet()
+    loads = [
+        pltpu.make_async_copy(r.w_in_hbm.at[INNER:], r.w_in.at[INNER:], r.load_sem.at[0]),
+        pltpu.make_async_copy(r.w_in_hbm.at[:INNER], r.w_in.at[:INNER], r.load_sem.at[1]),
+        pltpu.make_async_copy(r.w_out_hbm, r.w_out, r.load_sem.at[2]),
+    ]
+    for c in loads:
+        c.start()
     r.gain[...] = r.norm_gain[...].reshape(1, D)
     r.conv_b[...] = r.conv_bias[...].reshape(1, XBC)
     r.gate_gain[...] = r.gated_gain[...].reshape(1, INNER)
@@ -775,34 +866,34 @@
     place, core = lax.axis_index("seq"), lax.axis_index("head")
     chips = lax.axis_size("seq") // SEQS
     block = place // SEQS * 2 + core
-    loads = [
-        pltpu.make_async_copy(r.w_in_hbm.at[INNER:], r.w_in.at[INNER:], r.load_sem.at[0]),
-        pltpu.make_async_copy(r.w_in_hbm.at[:INNER], r.w_in.at[:INNER], r.load_sem.at[1]),
-        pltpu.make_async_copy(r.w_out_hbm, r.w_out, r.load_sem.at[2]),
-    ]
-    for c in loads:
-        c.start()
-    greet()
-    edge = remote(r.blk.at[rows - 16 :], r.edge, r.edge_sem.at[0], r.edge_sem.at[1], block_at(1))
-    edge.start()
 
     def norm(v):
         v = v.astype(f32)
         scale = lax.rsqrt(jnp.mean(v * v, axis=-1, keepdims=True) + EPS)
         return (v * scale * r.gain[...]).astype(bf16)
 
-    r.normed[16:, :] = norm(r.blk[...])
+    r.normed[...] = norm(r.blk[...])
     lane = iota((rows, 128), 1)
     keep = valid_rows(r.lengths, rows, 128)
     pick_lane = iota((128, 256), 1)
     pick_head = iota((128, 256), 0)
     left = one_hot(iota((1, 128), 1) < HEAD_DIM)
     right = one_hot(iota((1, 128), 1) >= HEAD_DIM)
-    own_rows = slice(16, 16 + rows)
 
     loads[0].wait()
+
+    def project(i, carry):
+        part = dot(r.normed[...], r.w_in[pl.ds(pl.multiple_of(INNER + i * 256, 256), 256), :], NT)
+        r.pad[16:, lanes(i * 256, 256)] = part.astype(bf16).astype(f32)
+        return carry
+
+    lax.fori_loop(0, XBC // 256, project, 0, unroll=7)
+    pl.semaphore_wait(*greeted)
+    edge = remote(r.pad.at[rows + 8 :], r.pad.at[8:16], r.edge_sem.at[0], r.edge_sem.at[1], block_at(1))
+    edge.start()
+
     r.head[3] = jnp.zeros((rows, 128), f32)
-    r.head[3, :, 0:HEADS] = dot(r.normed[own_rows, :], r.w_in[INNER + XBC :, :], NT).astype(bf16).astype(f32)
+    r.head[3, :, 0:HEADS] = dot(r.normed[...], r.w_in[INNER + XBC :, :], NT).astype(bf16).astype(f32)
     moved = r.head[3] + r.heads[0:1, :]
     soft = jnp.maximum(moved, 0.0) + jnp.log1p(jnp.exp(-jnp.abs(moved)))
     dt = jnp.where(lane < HEADS, soft * keep, 0.0)
@@ -817,11 +908,7 @@
     r.cumt[...] = cum2.T
 
     edge.wait()
-    r.normed[0:16, :] = jnp.where(block == 0, 0.0, norm(r.edge[...]).astype(f32)).astype(bf16)
-
-    def project(start, width):
-        part = dot(r.normed[...], r.w_in[pl.ds(pl.multiple_of(INNER + start, 128), width), :], NT)
-        r.pad[:, lanes(start, width)] = part.astype(bf16).astype(f32)
+    r.pad[8:16, :] = jnp.where(block == 0, 0.0, r.pad[8:16, :])
 
     def convolve(start, width):
         cols = lanes(start, width)
@@ -831,15 +918,12 @@
         r.run[:, cols] = running
         return running * sigmoid(running)
 
-    project(INNER, 2 * STATE)
     act = convolve(INNER, 2 * STATE)
     r.b[...] = act[:, :STATE].astype(bf16)
     r.c[...] = act[:, STATE:].astype(bf16)
     third = 3 * 128
 
     def channels(start):
-        project(start, third)
-
         def one(i, carry):
             at = start + i * 128
             cols = lanes(at, 128)
@@ -887,14 +971,11 @@
 
     causal = iota((rows, rows), 0) >= iota((rows, rows), 1)
     r.scores[...] = jnp.where(causal, dot(r.c[...], r.b[...], NT), 0.0)
-    r.scores_t[...] = jnp.where(
-        iota((rows, rows), 1) >= iota((rows, rows), 0), dot(r.b[...], r.c[...], NT), 0.0
-    )
     loads[1].wait()
     enters[1].deal()
 
     def gates(i, carry):
-        part = dot(r.normed[own_rows, :], r.w_in[pl.ds(pl.multiple_of(i * 256, 256), 256), :], NT)
+        part = dot(r.normed[...], r.w_in[pl.ds(pl.multiple_of(i * 256, 256), 256), :], NT)
         r.gate[:, lanes(i * 256, 256)] = part.astype(bf16)
         return carry
 
@@ -928,7 +1009,7 @@
     r.wide[...] = dot(r.db[...], r.w_out[...], NT)
     enters[1].hand()
     for one in enters:
-        one.arrive()
+        one.end()
 
     def carried(i, carry):
         cols = lanes(i * 128, 128)
@@ -976,7 +1057,7 @@
 
     def gate_grads(i, carry):
         at = pl.ds(pl.multiple_of(i * 256, 256), 256)
-        r.first[at, :] = dot(r.dgate[:, lanes(i * 256, 256)], r.normed[own_rows, :], TN).astype(bf16)
+        r.first[at, :] = dot(r.dgate[:, lanes(i * 256, 256)], r.normed[...], TN).astype(bf16)
         return carry
 
     def out_grads(i, carry):
@@ -985,22 +1066,37 @@
         return carry
 
     def part(k, held, got, out, at):
-        return Sum(held.at[at], got.at[at], out.at[at], r.ss.at[k], r.rs.at[k], r.ls.at[k])
-
-    half = REST_ROWS // 2
+        return Sum(held.at[at], got.at[at], out.at[at], r.ss.at[k], r.rs.at[k], r.ls.at[k], ORDERS[3 * k : 3 * k + 3])
+
     sums = [
         part(0, r.first, r.got_first, r.first_out, slice(0, INNER)),
         part(1, r.first, r.got_first, r.first_out, slice(INNER, FIRST_ROWS)),
-        part(2, r.rest, r.got_rest, r.rest_out, slice(0, half)),
-        part(3, r.rest, r.got_rest, r.rest_out, slice(half, REST_ROWS)),
+        part(2, r.rest, r.got_rest, r.rest_out, slice(0, D)),
+        part(3, r.rest, r.got_rest, r.rest_out, slice(D, INNER)),
+        part(4, r.rest, r.got_rest, r.rest_out, slice(INNER, REST_ROWS)),
     ]
+    def slot(name):
+        for n in SCHEDULE.get(name, ()):
+            sums[n // 3].tick(n % 3)
+
     lax.fori_loop(0, INNER // 256, gate_grads, 0, unroll=2)
+    slot("g2")
     for one in leaves:
         one.deal()
-    sums[0].tick()
+    slot("d")
     lax.fori_loop(0, INNER // 256, out_grads, 0, unroll=2)
+    slot("o2")
     r.block_out[...] = (r.blk[...].astype(f32) + keep_d * dot(r.gn[...], r.w_out[...])).astype(bf16)
-    sums[1].tick()
+    stores = [
+        pltpu.make_async_copy(r.block_out, r.block_out_hbm, r.store_sem.at[0]),
+        pltpu.make_async_copy(r.grad_in, r.grad_in_hbm, r.store_sem.at[1]),
+    ]
+    stores[0].start()
+    slot("b0")
+
+    r.scores_t[...] = jnp.where(
+        iota((rows, rows), 1) >= iota((rows, rows), 0), dot(r.b[...], r.c[...], NT), 0.0
+    )
 
     r.dscores[...] = jnp.zeros_like(r.dscores)
     r.q[...] = jnp.zeros_like(r.q)
@@ -1028,19 +1124,25 @@
         r.ry[...] += split_dot(dy.astype(f32) * r.y[:, cols], one_hot((row_head >> 6) + 2 * i == col_head))
         return carry
 
-    lax.fori_loop(0, PAIRS // 2, pair_back, 0, unroll=2)
+    lax.fori_loop(0, 4, pair_back, 0, unroll=2)
+    slot("b1")
+    lax.fori_loop(4, 8, pair_back, 0, unroll=2)
+    slot("b2")
+    lax.fori_loop(8, PAIRS, pair_back, 0, unroll=2)
+    slot("b3")
     for one in leaves:
         one.scan()
-    sums[0].tick()
-    lax.fori_loop(PAIRS // 2, PAIRS, pair_back, 0, unroll=2)
-    for one in leaves:
-        one.hand()
-    sums[1].tick()
+    slot("s")
     dsc = jnp.where(iota((rows, rows), 1) >= iota((rows, rows), 0), r.dscores[...], 0.0).astype(bf16)
     d_b = dot(dsc, r.c[...])
     d_c = dot(dsc, r.b[...], TN) + dot(r.dye[...], r.enter[...], NT)
+    slot("e")
     for one in leaves:
-        one.arrive()
+        one.hand()
+    slot("h")
+    for one in leaves:
+        one.end()
+    slot("l")
 
     def channels_back(i, carry):
         cols = lanes(i * 128, 128)
@@ -1055,13 +1157,59 @@
         r.ext[0:rows, cols] = (dtw * v + r.spread[8:9, cols] * dy) * keep * dsilu(cols)
         return carry
 
-    lax.fori_loop(0, PAIRS, channels_back, 0, unroll=2)
+    def conv_back(i, carry):
+        cols = lanes(i * 128, 128)
+        drun = r.ext[0:rows, cols]
+        total = drun * r.conv_w[CONV - 1 : CONV, cols]
+        for tap in range(CONV - 1):
+            ahead = CONV - 1 - tap
+            total = total + r.ext[ahead : ahead + rows, cols] * r.conv_w[tap : tap + 1, cols]
+        r.dproj[:, cols] = total.astype(bf16)
+        for tap in range(CONV):
+            r.tap_sums[tap : tap + 1, cols] = jnp.sum(
+                drun * r.pad[13 + tap : 13 + tap + rows, cols], axis=0, keepdims=True
+            )
+        r.tap_sums[CONV : CONV + 1, cols] = jnp.sum(drun, axis=0, keepdims=True)
+        return carry
+
+    def rest_grads(i, carry):
+        at = pl.ds(pl.multiple_of(i * 256, 256), 256)
+        r.rest[at, :] = dot(r.dproj[:, lanes(i * 256, 256)], r.normed[...], TN).astype(bf16)
+        return carry
+
+    halves = (slice(0, INNER // 2), slice(INNER // 2, XBC))
+
+    def edges(k):
+        cols = halves[k]
+        sems = r.edge_sem.at[2 + 2 * k], r.edge_sem.at[3 + 2 * k]
+        return remote(r.ext.at[0:8, cols], r.edge_grad.at[:, cols], *sems, block_at(-1))
+
+    def edge_in(k):
+        edges(k).wait()
+        r.ext[rows : rows + 8, halves[k]] = jnp.where(block == chips * 2 - 1, 0.0, r.edge_grad[:, halves[k]])
+
+    lax.fori_loop(0, PAIRS // 2, channels_back, 0, unroll=2)
+    edges(0).start()
+    slot("c1")
+    lax.fori_loop(PAIRS // 2, PAIRS, channels_back, 0, unroll=2)
     d_b = d_b + dot(r.xde[...], r.leave[...], NT)
     r.ext[0:rows, INNER : INNER + STATE] = d_b * dsilu(slice(INNER, INNER + STATE))
     r.ext[0:rows, INNER + STATE :] = d_c * dsilu(slice(INNER + STATE, XBC))
-    edge_back = remote(r.ext.at[0:8], r.edge_grad, r.edge_sem.at[2], r.edge_sem.at[3], block_at(-1))
-    edge_back.start()
-    sums[0].tick()
+    edges(1).start()
+    slot("c2")
+
+    edge_in(0)
+    slot("c3")
+    lax.fori_loop(0, 6, conv_back, 0, unroll=2)
+    slot("v1")
+    lax.fori_loop(0, 3, rest_grads, 0, unroll=3)
+    slot("r1")
+    edge_in(1)
+    slot("v2")
+    lax.fori_loop(6, XBC // 128, conv_back, 0, unroll=2)
+    slot("v3")
+    lax.fori_loop(3, XBC // 256, rest_grads, 0, unroll=2)
+    slot("r2")
     full_pick = one_hot((iota((INNER, 128), 0) >> 6) == iota((INNER, 128), 1))
     out_state = r.spread[0:1, :] * r.enter[...].astype(f32) + r.own[...]
     d_last = split_dot(
@@ -1077,61 +1225,32 @@
     r.vec[19:20, 0:128] = jnp.sum(d_cum * r.head[1], axis=0, keepdims=True)
     r.vec[20:21, 0:128] = jnp.sum(split_dot(r.skip[...], full_pick), axis=0, keepdims=True)
     dz = dz.astype(bf16)
+    slot("e1")
     d_normed = dot(r.dgate[...], r.w_in[:INNER, :])
     d_normed = d_normed + dot(dz[:, :HEADS], r.w_in[INNER + XBC :, :])
-    edge_back.wait()
-    r.ext[rows : rows + 8, :] = jnp.where(block == chips * 2 - 1, 0.0, r.edge_grad[...])
-    sums[1].tick()
-
-    def conv_back(i, carry):
-        cols = lanes(i * 128, 128)
-        drun = r.ext[0:rows, cols]
-        total = drun * r.conv_w[CONV - 1 : CONV, cols]
-        for tap in range(CONV - 1):
-            ahead = CONV - 1 - tap
-            total = total + r.ext[ahead : ahead + rows, cols] * r.conv_w[tap : tap + 1, cols]
-        r.dproj[:, cols] = total.astype(bf16)
-        for tap in range(CONV):
-            r.tap_sums[tap : tap + 1, cols] = jnp.sum(
-                drun * r.pad[13 + tap : 13 + tap + rows, cols], axis=0, keepdims=True
-            )
-        r.tap_sums[CONV : CONV + 1, cols] = jnp.sum(drun, axis=0, keepdims=True)
-        return carry
-
-    lax.fori_loop(0, XBC // 128, conv_back, 0, unroll=2)
-
-    def rest_grads(i, carry):
-        at = pl.ds(pl.multiple_of(i * 256, 256), 256)
-        r.rest[at, :] = dot(r.dproj[:, lanes(i * 256, 256)], r.normed[own_rows, :], TN).astype(bf16)
-        return carry
-
-    lax.fori_loop(0, 4, rest_grads, 0, unroll=2)
-    sums[2].tick()
-    sums[0].tick()
-    lax.fori_loop(4, XBC // 256, rest_grads, 0)
+    d_normed = d_normed + dot(r.dproj[...], r.w_in[INNER : INNER + XBC, :])
+    slot("e2")
     for v in range(CONV + 1):
         for part in range(3):
             width = min(D, XBC - part * D)
             r.vec[3 * v + part : 3 * v + part + 1, 0:width] = r.tap_sums[v : v + 1, part * D : part * D + width]
-    d_normed = d_normed + dot(r.dproj[...], r.w_in[INNER : INNER + XBC, :])
     src = r.blk[...].astype(f32)
     scale = lax.rsqrt(jnp.mean(src * src, axis=-1, keepdims=True) + EPS)
     r.vec[15:16, :] = jnp.sum(d_normed * src * scale, axis=0, keepdims=True)
     gate_gain = jnp.sum(r.ggain[...], axis=0, keepdims=True)
     r.vec[16:17, :] = gate_gain[:, :D]
     r.vec[17:18, :] = gate_gain[:, D:]
-    r.rest[XBC:VEC_ROW, :] = dot(dz, r.normed[own_rows, :], TN).astype(bf16)
+    r.rest[XBC:VEC_ROW, :] = dot(dz, r.normed[...], TN).astype(bf16)
     r.rest[VEC_ROW : VEC_ROW + 32, :] = r.vec[...].astype(bf16)
     r.rest[VEC_ROW + 32 :, :] = jnp.zeros((REST_ROWS - VEC_ROW - 32, D), bf16)
-    sums[3].tick()
-    sums[1].tick()
+    slot("r3")
     weighted = d_normed * r.gain[...]
     average = jnp.mean(weighted * src, axis=-1, keepdims=True)
     r.grad_in[...] = r.gout[...].astype(f32) + scale * weighted - src * (scale * scale * scale) * average
-    for _ in range(STAGES + 1):
-        for total in (sums[2], sums[0], sums[3], sums[1]):
-            if total.stage < STAGES:
-                total.tick()
+    stores[1].start()
+    slot("z")
+    for c in stores:
+        c.wait()
 
 
 def whole(*args):
@@ -1140,12 +1259,14 @@
     ins = ["blk", "gout", "lengths", "norm_gain", "w_in_hbm", "conv_w", "conv_bias", "dt_bias", "a_log", "d_skip"]
     ins += ["gated_gain", "w_out_hbm"]
     outs = {
-        "block_out": ((t, D), bf16),
-        "grad_in": ((t, D), f32),
+        "block_out_hbm": ((t, D), bf16),
+        "grad_in_hbm": ((t, D), f32),
         "first_out": ((FIRST_ROWS, D), bf16),
         "rest_out": ((REST_ROWS, D), bf16),
     }
     held = {
+        "block_out": ((t, D), bf16),
+        "grad_in": ((t, D), f32),
         "first": ((FIRST_ROWS, D), bf16),
         "rest": ((REST_ROWS, D), bf16),
         "gain": ((1, D), f32),
@@ -1154,9 +1275,8 @@
         "heads": ((8, 128), f32),
         "w_in": ((PROJ, D), bf16),
         "w_out": ((INNER, D), bf16),
-        "edge": ((16, D), bf16),
         "edge_grad": ((8, XBC), f32),
-        "normed": ((t + 16, D), bf16),
+        "normed": ((t, D), bf16),
         "gate": ((t, INNER), bf16),
         "pad": ((t + 16, XBC), f32),
         "run": ((t, XBC), f32),
@@ -1203,21 +1323,22 @@
             scratch += [pltpu.VMEM(s, d) for s, d in shapes]
             names += [f"{tag}{k}_{n}" for n in range(len(shapes))]
     semaphores = {
-        "ss": (WAVES, 3, STAGES),
+        "ss": (WAVES, 3),
         "rs": (WAVES, 3, STAGES),
         "ls": (WAVES, 3),
-        "fs": (SPLITS, 3 * chips),
-        "fr": (SPLITS, 3 * chips),
-        "gs": (SPLITS, 3 * chips),
-        "gr": (SPLITS, 3 * chips),
-        "edge_sem": (4,),
+        "fs": (SPLITS, 2),
+        "fr": (SPLITS, 7),
+        "gs": (SPLITS, 2),
+        "gr": (SPLITS, 7),
+        "edge_sem": (6,),
         "load_sem": (3,),
+        "store_sem": (2,),
     }
     for name, shape in semaphores.items():
         scratch.append(pltpu.SemaphoreType.DMA(shape))
         names.append(name)
     any_space = pl.BlockSpec(memory_space=pl.ANY)
-    specs = {"lengths": SMEM, "w_in_hbm": any_space, "w_out_hbm": any_space, "first_out": any_space, "rest_out": any_space}
+    specs = {n: any_space for n in ("w_in_hbm", "w_out_hbm", *outs)} | {"lengths": SMEM}
     return pl.pallas_call(
         partial(whole_kernel, names),
         out_shape=[jax.ShapeDtypeStruct(s, d) for s, d in outs.values()],
@@ -1264,7 +1385,7 @@
         pltpu.make_async_copy(src.at[start : start + size], dst.at[start : start + size], in_sem.at[n])
         for n, (src, dst, start, size) in enumerate(chunks)
     ]
-    ahead = 4
+    ahead = 8
     for c in loads[:ahead] + [load for load, _ in passed]:
         c.start()
     stores = [store for _, store in passed]

time: 139 us -> 127 us (0.914)
  Pallas kernels: 137 us -> 126 us
    pallas_call x1, Pallas kernels: 128 us -> 117 us  [whole(): pl.pallas_call(partial(whole_kernel, names), out_shape=[jax.ShapeDtypeStr...]
where the time goes in v4:
time: 127 us
  Pallas kernels  126 us (99%)
    pallas_call x1, Pallas kernels, whole(): pl.pallas_call(partial(whole_kernel, names), out_shape=[jax.ShapeDtypeStr...  117 us
    pallas_call x1, Pallas kernels, finish(): pl.pallas_call(finish_kernel, out_shape=[jax.ShapeDtypeStruct(s, bf16 if...  9.27 us

profile of v4, /device:TPU:0, one launch (start us, length us, event | category | flops | bytes accessed | tf_op | source)
XLA Modules:
  0.0 126.8 jit_solution(4645954922185110495)
XLA Ops:
  0.6 116.7 %shard_map.203 = (bf16[256,768]{1,0:T(8,128)(2,1)}, f32[256,768]{1,0:T(8,128)}, bf16[3072,768]{1,0:T(8,128)(2,1)}, bf16[2048,768]{1,0:T(8,128)(2,1)}) custom-call(bf16[256,768]{1,0:T(8,128)(2,1)} %refs_0_.1, bf16[256,768]{1,0:T(8,128)(2,1)} %refs_1_.1, s32[2]{0:T(128)} %refs_2_.1, f32[768]{0:T(1024)} %refs_3_.1, bf16[3352,768]{1,0:T(8,128)(2,1)} %bitcast.2, ...), custom_call_target="tpu_custom_call" | custom-call | tf_op jit(solution)/shard_map/pallas_call | solution.py:1342
  117.4 9.3 %shard_map.204 = (bf16[256,768]{1,0:T(8,128)(2,1)}, f32[256,768]{1,0:T(8,128)}, f32[768]{0:T(1024)}, f32[3352,768]{1,0:T(8,128)}, f32[4,1792]{1,0:T(4,128)}, /*i...) custom-call(bf16[256,768]{1,0:T(8,128)(2,1)} %get-tuple-element.26.b, ...), custom_call_target="tpu_custom_call" | custom-call | tf_op jit(solution)/shard_map/pallas_call | solution.py:1433

commit v5 on v4

--- a/solution.py
+++ b/solution.py
@@ -88,10 +88,10 @@
     )(*args)
 
 
-VEC_ROW = XBC + 128
-REST_ROWS = 2048
+REST_ROWS = XBC
+VEC_ROWS = 48
 FIRST_ROWS = 2 * INNER
-WAVES = 5
+WAVES = 4
 SPLITS = 2
 
 
@@ -489,15 +489,15 @@
     small_in,
     gin_out,
     grads_out,
+    vec_out,
     ext,
     dproj,
-    vec,
     sums,
 ):
     rows = blk.shape[0]
     ext[0:rows, :] = drun_in[...]
     ext[rows : rows + 8, :] = edge[...]
-    vec[...] = jnp.zeros_like(vec)
+    vec_out[...] = jnp.zeros_like(vec_out)
 
     def channels(i, carry):
         cols = lanes(i * 128, 128)
@@ -518,31 +518,29 @@
     for v in range(CONV + 1):
         for part in range(3):
             width = min(D, XBC - part * D)
-            vec[3 * v + part : 3 * v + part + 1, 0:width] = sums[v : v + 1, part * D : part * D + width]
+            vec_out[HEADS + 3 * v + part : HEADS + 3 * v + part + 1, 0:width] = sums[v : v + 1, part * D : part * D + width]
     dz = dz_in[...].astype(bf16)
     d_normed = dot(dgate[...], w_in[:INNER, :])
     d_normed = d_normed + dot(dproj[...], w_in[INNER : INNER + XBC, :])
     d_normed = d_normed + dot(dz[:, :HEADS], w_in[INNER + XBC :, :])
     src = blk[...].astype(f32)
     scale = lax.rsqrt(jnp.mean(src * src, axis=-1, keepdims=True) + EPS)
-    vec[15:16, :] = jnp.sum(d_normed * src * scale, axis=0, keepdims=True)
+    vec_out[39:40, :] = jnp.sum(d_normed * src * scale, axis=0, keepdims=True)
     gate_gain = jnp.sum(ggain[...], axis=0, keepdims=True)
-    vec[16:17, :] = gate_gain[:, :D]
-    vec[17:18, :] = gate_gain[:, D:]
-    vec[18:21, 0:128] = small_in[0:3, :]
+    vec_out[40:41, :] = gate_gain[:, :D]
+    vec_out[41:42, :] = gate_gain[:, D:]
+    vec_out[42:45, 0:128] = small_in[0:3, :]
     weighted = d_normed * gain[...]
     average = jnp.mean(weighted * src, axis=-1, keepdims=True)
     gin_out[...] = gout[...].astype(f32) + scale * weighted - src * (scale * scale * scale) * average
-    grads_out[:XBC, :] = dot(dproj[...], normed[...], TN).astype(bf16)
-    grads_out[XBC:VEC_ROW, :] = dot(dz, normed[...], TN).astype(bf16)
-    grads_out[VEC_ROW : VEC_ROW + 32, :] = vec[...].astype(bf16)
-    grads_out[VEC_ROW + 32 :, :] = jnp.zeros((REST_ROWS - VEC_ROW - 32, D), bf16)
+    grads_out[...] = dot(dproj[...], normed[...], TN).astype(bf16)
+    vec_out[0:HEADS, :] = dot(dz, normed[...], TN)[0:HEADS, :]
 
 
 def last(blk, gout, normed, gain, w_in, conv_w, pad, drun, edge, dz, dgate, ggain, small):
     t = blk.shape[0]
-    outs = [((t, D), f32), ((REST_ROWS, D), bf16)]
-    scratch = [pltpu.VMEM((t + 8, XBC), f32), pltpu.VMEM((t, XBC), bf16), pltpu.VMEM((32, D), f32), pltpu.VMEM((8, XBC), f32)]
+    outs = [((t, D), f32), ((REST_ROWS, D), bf16), ((VEC_ROWS, D), f32)]
+    scratch = [pltpu.VMEM((t + 8, XBC), f32), pltpu.VMEM((t, XBC), bf16), pltpu.VMEM((8, XBC), f32)]
     args = (blk, gout, normed, gain, w_in, conv_w, pad, drun, edge, dz, dgate, ggain, small)
     return call(last_kernel, outs, args, scratch)
 
@@ -666,78 +664,78 @@
 
 
 ORDERS = (
+    ("x", "y", "z1", "z2"),
+    ("z1", "y", "x", "z2"),
     ("x", "z1", "y", "z2"),
     ("x", "y", "z2", "z1"),
-    ("z1", "x", "y", "z2"),
+    ("x", "y", "z1", "z2"),
+    ("y", "x", "z2", "z1"),
+    ("z1", "y", "x", "z2"),
     ("y", "x", "z1", "z2"),
-    ("x", "z1", "y", "z2"),
-    ("y", "x", "z1", "z2"),
-    ("z1", "z2", "y", "x"),
-    ("y", "x", "z2", "z1"),
     ("x", "y", "z1", "z2"),
-    ("y", "x", "z1", "z2"),
-    ("x", "y", "z2", "z1"),
-    ("z1", "x", "y", "z2"),
-    ("y", "x", "z1", "z2"),
-    ("z1", "x", "y", "z2"),
-    ("x", "y", "z2", "z1"),
+    ("z1", "y", "x", "z2"),
+    ("y", "z1", "x", "z2"),
+    ("x", "y", "z1", "z2"),
+    ("y", "z1", "z2", "x"),
+    ("x", "z2", "y", "z1"),
+    ("y", "z2", "x", "z1"),
 )
 SCHEDULE = {
     "g2": (
-        2, 0,
+        2, 1,
     ),
     "o2": (
-        0, 5, 2,
-    ),
-    "b0": (
-        1,
+        2, 5,
     ),
     "b1": (
+        1, 5, 0,
+    ),
+    "b2": (
+        3,
+    ),
+    "b3": (
+        4, 0,
+    ),
+    "s": (
+        2,
+    ),
+    "e": (
+        5, 1, 3, 0,
+    ),
+    "h": (
+        4, 2,
+    ),
+    "c1": (
+        5, 1, 0,
+    ),
+    "c2": (
+        2, 3,
+    ),
+    "r1": (
+        6, 8, 1, 5, 7, 4, 8, 7, 0,
+    ),
+    "v2": (
+        2, 6,
+    ),
+    "v3": (
         5,
     ),
-    "b2": (
-        1, 4, 3,
-    ),
-    "s": (
-        2, 5, 4,
-    ),
-    "e": (
-        1, 2, 3, 0,
-    ),
-    "h": (
-        1, 5,
-    ),
-    "c1": (
-        2, 4, 0,
-    ),
-    "c3": (
-        1, 5,
-    ),
-    "r1": (
-        8, 7, 6, 0, 4,
-    ),
-    "v2": (
-        3, 2,
-    ),
-    "v3": (
-        6, 8, 1,
-    ),
     "r2": (
-        11, 9, 7, 2, 11, 5,
+        9, 1, 11, 4, 10, 9, 11, 8, 6, 7, 2, 10, 3, 6, 8, 9, 7, 0, 11, 1, 5, 4, 10,
     ),
     "e1": (
-        8, 3, 6, 9, 1, 0, 10, 7, 4, 11, 8,
+        2, 7,
     ),
     "e2": (
-        10, 7, 2, 11,
+        0, 11, 6, 3, 9, 10, 8, 5, 4,
     ),
     "r3": (
-        12, 9, 1, 12, 11, 13, 7, 3, 0, 6, 10, 4, 14, 14,
+        11, 7, 0, 12, 2, 6, 3, 4, 13,
     ),
     "z": (
-        12, 6, 10, 7, 5, 11, 13, 14, 2, 9, 1, 8, 0, 12, 10, 11, 14, 4, 3, 6, 5, 10, 13, 9, 14, 12, 7, 6, 4,
-        13, 8, 2, 10, 7, 14, 3, 13, 9, 12, 8, 6, 5, 10, 14, 11, 13, 0, 1, 3, 12, 4, 9, 13, 14, 8, 12, 11, 10,
-        6, 9, 7, 13, 3, 14, 14, 11, 12, 10, 8, 0, 5, 13, 9, 6, 7, 8, 4, 13, 12, 3, 9,
+        14, 8, 10, 12, 9, 1, 13, 7, 14, 11, 4, 3, 10, 12, 6, 2, 13, 14, 9, 7, 5, 8, 3, 0, 11, 1, 10, 6, 9, 8,
+        0, 13, 12, 7, 4, 14, 10, 11, 9, 3, 13, 3, 5, 14, 12, 8, 10, 6, 11, 9, 1, 4, 13, 8, 6, 12, 7, 10, 11,
+        14, 9,
     ),
 }
 STEPS = {"x": 1, "y": 2, "z1": 4, "z2": 8}
@@ -822,6 +820,29 @@
         if stage == 5:
             place().wait()
         if stage + 1 < STAGES:
+            copy(stage + 1).start()
+        self.stages[s] = stage + 1
+
+
+class Swap:
+    def __init__(self, held, got, ssem, rsem, orders):
+        self.held, self.got, self.ssem, self.rsem = held, got, ssem, rsem
+        self.orders = [("c",) + order for order in orders]
+        self.stages = [-1] * len(orders)
+
+    def tick(self, s):
+        cols = slice(s * 256, (s + 1) * 256)
+        order, stage = self.orders[s], self.stages[s]
+
+        def copy(k):
+            return remote(
+                self.held.at[:, cols], self.got.at[k, :, cols], self.ssem.at[s], self.rsem.at[s, k], partner(order[k])
+            )
+
+        if 0 <= stage < len(order):
+            copy(stage).wait()
+            self.held[:, cols] = self.held[:, cols] + self.got[stage, :, cols]
+        if stage + 1 < len(order):
             copy(stage + 1).start()
         self.stages[s] = stage + 1
 
@@ -907,6 +928,20 @@
     r.head[3] = cum2
     r.cumt[...] = cum2.T
 
+    def widen(i, carry):
+        cols = lanes(i * 128, 128)
+        pick = one_hot((iota((128, 128), 1) >> 6) + 2 * i == iota((128, 128), 0))
+        r.dt_wide[:, cols] = split_dot(r.head[0], pick)
+        wide = split_dot(r.head[3], pick)
+        last = wide[rows - 1 : rows, :]
+        r.grow[:, cols] = jnp.exp2(wide)
+        r.fall[:, cols] = jnp.exp2(last - wide)
+        r.spread[0:8, cols] = jnp.broadcast_to(jnp.exp2(last), (8, 128))
+        r.spread[8:16, cols] = split_dot(jnp.broadcast_to(r.heads[2:3, :], (8, 128)), pick)
+        return carry
+
+    lax.fori_loop(0, PAIRS, widen, 0, unroll=2)
+
     edge.wait()
     r.pad[8:16, :] = jnp.where(block == 0, 0.0, r.pad[8:16, :])
 
@@ -927,17 +962,11 @@
         def one(i, carry):
             at = start + i * 128
             cols = lanes(at, 128)
-            pick = one_hot((iota((128, 128), 1) >> 6) + at // HEAD_DIM == iota((128, 128), 0))
             x = convolve(at, 128) * keep
             r.x[:, cols] = x
-            xd = x * split_dot(r.head[0], pick)
+            xd = x * r.dt_wide[:, cols]
             r.xd[:, cols] = xd.astype(bf16)
-            wide = split_dot(r.head[3], pick)
-            last = wide[rows - 1 : rows, :]
-            xde = (xd * jnp.exp2(last - wide)).astype(bf16)
-            r.xde[:, cols] = xde
-            r.spread[0:8, cols] = jnp.broadcast_to(jnp.exp2(last), (8, 128))
-            r.spread[8:16, cols] = split_dot(jnp.broadcast_to(r.heads[2:3, :], (8, 128)), pick)
+            r.xde[:, cols] = (xd * r.fall[:, cols]).astype(bf16)
             return carry
 
         lax.fori_loop(0, third // 128, one, 0, unroll=3)
@@ -967,12 +996,13 @@
         r.cumb[:, lanes(i * 256, 256)] = split_dot(r.head[3], one_hot((pick_lane >> 7) + 2 * i == pick_head))
         return carry
 
-    lax.fori_loop(0, PAIRS, spread, 0, unroll=2)
 
     causal = iota((rows, rows), 0) >= iota((rows, rows), 1)
     r.scores[...] = jnp.where(causal, dot(r.c[...], r.b[...], NT), 0.0)
+    lax.fori_loop(0, 4, spread, 0, unroll=2)
+    enters[1].deal()
+    lax.fori_loop(4, PAIRS, spread, 0, unroll=2)
     loads[1].wait()
-    enters[1].deal()
 
     def gates(i, carry):
         part = dot(r.normed[...], r.w_in[pl.ds(pl.multiple_of(i * 256, 256), 256), :], NT)
@@ -997,24 +1027,31 @@
         return carry
 
     lax.fori_loop(0, INNER // 256, gates, 0, unroll=2)
-    lax.fori_loop(0, 4, pair, 0, unroll=2)
     enters[0].scan()
-    lax.fori_loop(4, 8, pair, 0, unroll=2)
+    lax.fori_loop(0, 6, pair, 0, unroll=2)
     enters[1].scan()
-    lax.fori_loop(8, PAIRS, pair, 0, unroll=2)
-    enters[0].hand()
+    lax.fori_loop(6, PAIRS, pair, 0, unroll=2)
+
+    def slopes(i, carry):
+        cols = lanes(i * 128, 128)
+        running = r.run[:, cols]
+        sg = sigmoid(running)
+        r.run[:, cols] = sg * (1.0 + running * (1.0 - sg))
+        return carry
+
+    lax.fori_loop(0, XBC // 128, slopes, 0, unroll=2)
     keep_d = valid_rows(r.lengths, rows, D)
     r.db[...] = (r.gout[...].astype(f32) * keep_d).astype(bf16)
     loads[2].wait()
     r.wide[...] = dot(r.db[...], r.w_out[...], NT)
-    enters[1].hand()
+    for one in enters:
+        one.hand()
     for one in enters:
         one.end()
 
     def carried(i, carry):
         cols = lanes(i * 128, 128)
-        c0, c1 = columns(i)
-        y = r.y[:, cols] + jnp.exp2(jnp.where(lane < HEAD_DIM, c0, c1)) * dot(r.c[...], r.enter[:, cols])
+        y = r.y[:, cols] + r.grow[:, cols] * dot(r.c[...], r.enter[:, cols])
         r.y[:, cols] = y
         r.mixed[:, cols] = (y + r.spread[8:9, cols] * r.x[:, cols]).astype(bf16)
         return carry
@@ -1045,9 +1082,7 @@
 
     def weigh(i, carry):
         cols = lanes(i * 128, 128)
-        c0, c1 = columns(i)
-        grow = jnp.exp2(jnp.where(lane < HEAD_DIM, c0, c1))
-        r.dye[:, cols] = (r.dy[:, cols].astype(f32) * grow).astype(bf16)
+        r.dye[:, cols] = (r.dy[:, cols].astype(f32) * r.grow[:, cols]).astype(bf16)
         return carry
 
     lax.fori_loop(0, PAIRS, weigh, 0, unroll=2)
@@ -1072,8 +1107,8 @@
         part(0, r.first, r.got_first, r.first_out, slice(0, INNER)),
         part(1, r.first, r.got_first, r.first_out, slice(INNER, FIRST_ROWS)),
         part(2, r.rest, r.got_rest, r.rest_out, slice(0, D)),
-        part(3, r.rest, r.got_rest, r.rest_out, slice(D, INNER)),
-        part(4, r.rest, r.got_rest, r.rest_out, slice(INNER, REST_ROWS)),
+        part(3, r.rest, r.got_rest, r.rest_out, slice(D, REST_ROWS)),
+        Swap(r.vec, r.got_vec, r.vs, r.vr, ORDERS[12:15]),
     ]
     def slot(name):
         for n in SCHEDULE.get(name, ()):
@@ -1103,11 +1138,6 @@
     r.ry[...] = jnp.zeros_like(r.ry)
     row_head = iota((128, 128), 0)
     col_head = iota((128, 128), 1)
-
-    def dsilu(cols):
-        running = r.run[:, cols]
-        sg = sigmoid(running)
-        return sg * (1.0 + running * (1.0 - sg))
 
     def pair_back(i, carry):
         cols = lanes(i * 128, 128)
@@ -1146,15 +1176,12 @@
 
     def channels_back(i, carry):
         cols = lanes(i * 128, 128)
-        c0, c1 = columns(i)
-        c01 = jnp.where(lane < HEAD_DIM, c0, c1)
-        v = r.wide[:, cols] + jnp.exp2(c01[rows - 1 : rows, :] - c01) * dot(r.b[...], r.leave[:, cols])
-        dtw = split_dot(r.head[0], one_hot((col_head >> 6) + 2 * i == row_head))
+        v = r.wide[:, cols] + r.fall[:, cols] * dot(r.b[...], r.leave[:, cols])
         x = r.x[:, cols]
         dy = r.dy[:, cols].astype(f32)
         r.q[...] += split_dot(x * v, one_hot((row_head >> 6) + 2 * i == col_head))
         r.skip[:, cols] = jnp.sum((dy * x).reshape(rows // 8, 8, 128), axis=0)
-        r.ext[0:rows, cols] = (dtw * v + r.spread[8:9, cols] * dy) * keep * dsilu(cols)
+        r.ext[0:rows, cols] = (r.dt_wide[:, cols] * v + r.spread[8:9, cols] * dy) * keep * r.run[:, cols]
         return carry
 
     def conv_back(i, carry):
@@ -1193,8 +1220,8 @@
     slot("c1")
     lax.fori_loop(PAIRS // 2, PAIRS, channels_back, 0, unroll=2)
     d_b = d_b + dot(r.xde[...], r.leave[...], NT)
-    r.ext[0:rows, INNER : INNER + STATE] = d_b * dsilu(slice(INNER, INNER + STATE))
-    r.ext[0:rows, INNER + STATE :] = d_c * dsilu(slice(INNER + STATE, XBC))
+    r.ext[0:rows, INNER : INNER + STATE] = d_b * r.run[:, INNER : INNER + STATE]
+    r.ext[0:rows, INNER + STATE :] = d_c * r.run[:, INNER + STATE :]
     edges(1).start()
     slot("c2")
 
@@ -1221,9 +1248,9 @@
     above = one_hot(iota((rows, rows), 0) <= iota((rows, rows), 1))
     dz = (q + split_dot_left(above, d_cum * -jnp.exp(r.heads[1:2, :]))) * r.head[2]
     r.vec[...] = jnp.zeros_like(r.vec)
-    r.vec[18:19, 0:128] = jnp.sum(dz, axis=0, keepdims=True)
-    r.vec[19:20, 0:128] = jnp.sum(d_cum * r.head[1], axis=0, keepdims=True)
-    r.vec[20:21, 0:128] = jnp.sum(split_dot(r.skip[...], full_pick), axis=0, keepdims=True)
+    r.vec[42:43, 0:128] = jnp.sum(dz, axis=0, keepdims=True)
+    r.vec[43:44, 0:128] = jnp.sum(d_cum * r.head[1], axis=0, keepdims=True)
+    r.vec[44:45, 0:128] = jnp.sum(split_dot(r.skip[...], full_pick), axis=0, keepdims=True)
     dz = dz.astype(bf16)
     slot("e1")
     d_normed = dot(r.dgate[...], r.w_in[:INNER, :])
@@ -1233,23 +1260,23 @@
     for v in range(CONV + 1):
         for part in range(3):
             width = min(D, XBC - part * D)
-            r.vec[3 * v + part : 3 * v + part + 1, 0:width] = r.tap_sums[v : v + 1, part * D : part * D + width]
+            r.vec[HEADS + 3 * v + part : HEADS + 3 * v + part + 1, 0:width] = r.tap_sums[v : v + 1, part * D : part * D + width]
     src = r.blk[...].astype(f32)
     scale = lax.rsqrt(jnp.mean(src * src, axis=-1, keepdims=True) + EPS)
-    r.vec[15:16, :] = jnp.sum(d_normed * src * scale, axis=0, keepdims=True)
+    r.vec[39:40, :] = jnp.sum(d_normed * src * scale, axis=0, keepdims=True)
     gate_gain = jnp.sum(r.ggain[...], axis=0, keepdims=True)
-    r.vec[16:17, :] = gate_gain[:, :D]
-    r.vec[17:18, :] = gate_gain[:, D:]
-    r.rest[XBC:VEC_ROW, :] = dot(dz, r.normed[...], TN).astype(bf16)
-    r.rest[VEC_ROW : VEC_ROW + 32, :] = r.vec[...].astype(bf16)
-    r.rest[VEC_ROW + 32 :, :] = jnp.zeros((REST_ROWS - VEC_ROW - 32, D), bf16)
+    r.vec[40:41, :] = gate_gain[:, :D]
+    r.vec[41:42, :] = gate_gain[:, D:]
+    r.vec[0:HEADS, :] = dot(dz, r.normed[...], TN)[0:HEADS, :]
     slot("r3")
     weighted = d_normed * r.gain[...]
     average = jnp.mean(weighted * src, axis=-1, keepdims=True)
     r.grad_in[...] = r.gout[...].astype(f32) + scale * weighted - src * (scale * scale * scale) * average
     stores[1].start()
     slot("z")
-    for c in stores:
+    out = pltpu.make_async_copy(r.vec, r.vec_out, r.store_sem.at[2])
+    out.start()
+    for c in (*stores, out):
         c.wait()
 
 
@@ -1263,6 +1290,7 @@
         "grad_in_hbm": ((t, D), f32),
         "first_out": ((FIRST_ROWS, D), bf16),
         "rest_out": ((REST_ROWS, D), bf16),
+        "vec_out": ((VEC_ROWS, D), f32),
     }
     held = {
         "block_out": ((t, D), bf16),
@@ -1292,6 +1320,9 @@
         "own": ((STATE, INNER), f32),
         "enter": ((STATE, INNER), bf16),
         "y": ((t, INNER), f32),
+        "grow": ((t, INNER), f32),
+        "fall": ((t, INNER), f32),
+        "dt_wide": ((t, INNER), f32),
         "mixed": ((t, INNER), bf16),
         "gn": ((t, INNER), bf16),
         "wide": ((t, INNER), f32),
@@ -1310,7 +1341,8 @@
         "ry": ((t, 128), f32),
         "ext": ((t + 8, XBC), f32),
         "dproj": ((t, XBC), bf16),
-        "vec": ((32, D), f32),
+        "vec": ((VEC_ROWS, D), f32),
+        "got_vec": ((5, VEC_ROWS, D), f32),
         "tap_sums": ((8, XBC), f32),
         "got_first": ((FIRST_ROWS, D), bf16),
         "got_rest": ((REST_ROWS, D), bf16),
@@ -1332,7 +1364,9 @@
         "gr": (SPLITS, 7),
         "edge_sem": (6,),
         "load_sem": (3,),
-        "store_sem": (2,),
+        "store_sem": (3,),
+        "vs": (3,),
+        "vr": (3, 5),
     }
     for name, shape in semaphores.items():
         scratch.append(pltpu.SemaphoreType.DMA(shape))
@@ -1354,6 +1388,7 @@
     grad_in,
     first,
     rest,
+    vec_in,
     block_out,
     grad_out,
     norm_out,
@@ -1369,6 +1404,7 @@
     held_rest,
     held_block,
     held_grad,
+    vec,
     wide_in,
     wide_out,
     in_sem,
@@ -1386,7 +1422,8 @@
         for n, (src, dst, start, size) in enumerate(chunks)
     ]
     ahead = 8
-    for c in loads[:ahead] + [load for load, _ in passed]:
+    small = pltpu.make_async_copy(vec_in, vec, pass_sem.at[1, 2])
+    for c in loads[:ahead] + [small] + [load for load, _ in passed]:
         c.start()
     stores = [store for _, store in passed]
     for n, (src, held, start, size) in enumerate(chunks):
@@ -1401,30 +1438,31 @@
             wide, out, at = wide_out, w_out_out, start - INNER
         else:
             wide, out, at = wide_in, w_in_out, start if src is first else INNER + start
-        kept = min(size, out.shape[0] - at)
-        if kept <= 0:
-            continue
-        wide[at : at + kept, :] = held[start : start + kept, :].astype(f32)
-        c = pltpu.make_async_copy(wide.at[at : at + kept], out.at[at : at + kept], out_sem.at[n])
+        wide[at : at + size, :] = held[start : start + size, :].astype(f32)
+        c = pltpu.make_async_copy(wide.at[at : at + size], out.at[at : at + size], out_sem.at[n])
         c.start()
         stores.append(c)
-    vec = held_rest[VEC_ROW : VEC_ROW + 32, :].astype(f32)
+    small.wait()
+    wide_in[INNER + XBC :, :] = vec[0:HEADS, :]
+    c = pltpu.make_async_copy(wide_in.at[INNER + XBC :], w_in_out.at[INNER + XBC :], pass_sem.at[0, 2])
+    c.start()
+    stores.append(c)
 
     def row(v):
-        return jnp.concatenate([vec[3 * v + k : 3 * v + k + 1, : min(D, XBC - k * D)] for k in range(3)], axis=1)
+        return jnp.concatenate([vec[HEADS + 3 * v + k : HEADS + 3 * v + k + 1, : min(D, XBC - k * D)] for k in range(3)], axis=1)
 
     for v in range(CONV):
         conv_out[v : v + 1, :] = row(v)
     bias_out[...] = row(CONV).reshape(XBC)
-    norm_out[...] = vec[15:16, :].reshape(D)
-    gate_out[...] = jnp.concatenate([vec[16:17, :], vec[17:18, :]], axis=1).reshape(INNER)
+    norm_out[...] = vec[39:40, :].reshape(D)
+    gate_out[...] = jnp.concatenate([vec[40:41, :], vec[41:42, :]], axis=1).reshape(INNER)
     for k, out in enumerate((dt_out, alog_out, skip_out)):
-        out[...] = vec[18 + k : 19 + k, 0:HEADS].reshape(HEADS)
+        out[...] = vec[42 + k : 43 + k, 0:HEADS].reshape(HEADS)
     for c in stores:
         c.wait()
 
 
-def finish(block_out, grad_in, first, rest):
+def finish(block_out, grad_in, first, rest, vec):
     shapes = [block_out.shape, grad_in.shape, (D,), (PROJ, D), (CONV, XBC), (XBC,), (HEADS,), (HEADS,), (HEADS,), (INNER,)]
     shapes += [(INNER, D)]
     any_space = pl.BlockSpec(memory_space=pltpu.HBM)
@@ -1433,21 +1471,22 @@
     return pl.pallas_call(
         finish_kernel,
         out_shape=[jax.ShapeDtypeStruct(s, bf16 if k == 0 else f32) for k, s in enumerate(shapes)],
-        in_specs=[any_space] * 4,
+        in_specs=[any_space] * 5,
         out_specs=[any_space if k in away else VMEM for k in range(len(shapes))],
         scratch_shapes=[
             pltpu.VMEM((FIRST_ROWS, D), bf16),
             pltpu.VMEM((REST_ROWS, D), bf16),
             pltpu.VMEM(block_out.shape, bf16),
             pltpu.VMEM(grad_in.shape, f32),
+            pltpu.VMEM((VEC_ROWS, D), f32),
             pltpu.VMEM((PROJ, D), f32),
             pltpu.VMEM((INNER, D), f32),
             pltpu.SemaphoreType.DMA((chunks,)),
             pltpu.SemaphoreType.DMA((chunks,)),
-            pltpu.SemaphoreType.DMA((2, 2)),
+            pltpu.SemaphoreType.DMA((2, 3)),
         ],
         compiler_params=pltpu.CompilerParams(vmem_limit_bytes=60 << 20),
-    )(block_out, grad_in, first, rest)
+    )(block_out, grad_in, first, rest, vec)
 
 
 def shifted(value, ahead):
@@ -1482,11 +1521,11 @@
         lengths, y, dy, dye, x, xd, xde, b, c, run, cumt, cumb, head, rows, heads, enter, own, leave
     )
     edge_back = shifted(drun[0:8], -1)
-    grad_in, grads_b = last(
+    grad_in, grads_b, vec = last(
         block_in, grad_out, normed, gain, w_in, conv_w, pad, drun, edge_back, dz, dgate, ggain, small
     )
-    grads_a, grads_b = lax.psum((grads_a, grads_b), ("seq", "head"))
-    return block_out, grad_in, grads_a, grads_b
+    grads_a, grads_b, vec = lax.psum((grads_a, grads_b, vec), ("seq", "head"))
+    return block_out, grad_in, grads_a, grads_b, vec
 
 
 def local(block_in, grad_out, lengths, norm_gain, w_in, *others):

time: 127 us -> 123 us (0.969)
  Pallas kernels: 126 us -> 122 us
    pallas_call x1, Pallas kernels: 117 us -> 112 us  [whole(): pl.pallas_call(partial(whole_kernel, names), out_shape=[jax.ShapeDtypeStr...]
where the time goes in v5:
time: 123 us
  Pallas kernels  122 us (99%)
    pallas_call x1, Pallas kernels, whole(): pl.pallas_call(partial(whole_kernel, names), out_shape=[jax.ShapeDtypeStr...  112 us
    pallas_call x1, Pallas kernels, finish(): pl.pallas_call(finish_kernel, out_shape=[jax.ShapeDtypeStruct(s, bf16 if...  9.31 us

profile of v5, /device:TPU:0, one launch (start us, length us, event | category | flops | bytes accessed | tf_op | source)
XLA Modules:
  0.0 122.6 jit_solution(3106512887403444640)
XLA Ops:
  0.6 112.5 %shard_map.203 = (bf16[256,768]{1,0:T(8,128)(2,1)}, f32[256,768]{1,0:T(8,128)}, bf16[3072,768]{1,0:T(8,128)(2,1)}, bf16[1792,768]{1,0:T(8,128)(2,1)}, f32[48,768]{1,0:T(8,128)}) custom-call(bf16[256,768]{1,0:T(8,128)(2,1)} %refs_0_.1, bf16[256,768]{1,0:T(8,128)(2,1)} %refs_1_.1, s32[2]{0:T(128)} %refs_2_.1, f32[768]{0:T(1024)} %refs_3_.1, ...), custom_call_target="tpu_custom_call" | custom-call | tf_op jit(solution)/shard_map/pallas_call | solution.py:1376
  113.1 9.3 %shard_map.204 = (bf16[256,768]{1,0:T(8,128)(2,1)}, f32[256,768]{1,0:T(8,128)}, f32[768]{0:T(1024)}, f32[3352,768]{1,0:T(8,128)}, f32[4,1792]{1,0:T(4,128)}, /*i...) custom-call(bf16[256,768]{1,0:T(8,128)(2,1)} %get-tuple-element.27.b, ...), custom_call_target="tpu_custom_call" | custom-call | tf_op jit(solution)/shard_map/pallas_call | solution.py:1471

commit v6 on v5

--- a/solution.py
+++ b/solution.py
@@ -1059,7 +1059,7 @@
     lax.fori_loop(0, PAIRS, carried, 0, unroll=2)
 
     r.ggain[...] = jnp.zeros_like(r.ggain)
-    step = 32
+    step = 16
 
     def gating(i, carry):
         at = pl.ds(pl.multiple_of(i * step, step), step)
@@ -1074,18 +1074,14 @@
         weighted = dgn * r.gate_gain[...]
         average = jnp.mean(weighted * gated, axis=-1, keepdims=True)
         d_gated = scale * weighted - gated * (scale * scale * scale) * average
-        r.dy[at, :] = (d_gated * g * sg).astype(bf16)
+        dy = (d_gated * g * sg).astype(bf16)
+        r.dy[at, :] = dy
+        r.dye[at, :] = (dy.astype(f32) * r.grow[at, :]).astype(bf16)
         r.dgate[at, :] = (d_gated * mixed * sg * (1.0 + g * (1.0 - sg))).astype(bf16)
         return carry
 
-    lax.fori_loop(0, rows // step, gating, 0)
-
-    def weigh(i, carry):
-        cols = lanes(i * 128, 128)
-        r.dye[:, cols] = (r.dy[:, cols].astype(f32) * r.grow[:, cols]).astype(bf16)
-        return carry
-
-    lax.fori_loop(0, PAIRS, weigh, 0, unroll=2)
+    lax.fori_loop(0, rows // step, gating, 0, unroll=2)
+
     r.adj[...] = dot(r.c[...], r.dye[...], TN)
     for one in leaves:
         one.begin()

time: 123 us -> 123 us (level)
  no operation moved by 1% of the time
where the time goes in v6:
time: 123 us; the launch traced here: 122 us
  Pallas kernels  122 us (99%)
    pallas_call x1, Pallas kernels, whole(): pl.pallas_call(partial(whole_kernel, names), out_shape=[jax.ShapeDtypeStr...  112 us
    pallas_call x1, Pallas kernels, finish(): pl.pallas_call(finish_kernel, out_shape=[jax.ShapeDtypeStruct(s, bf16 if...  9.31 us

profile of v6, /device:TPU:0, one launch (start us, length us, event | category | flops | bytes accessed | tf_op | source)
XLA Modules:
  0.0 122.4 jit_solution(5894946487493418071)
XLA Ops:
  0.6 112.2 %shard_map.203 = (bf16[256,768]{1,0:T(8,128)(2,1)}, f32[256,768]{1,0:T(8,128)}, bf16[3072,768]{1,0:T(8,128)(2,1)}, bf16[1792,768]{1,0:T(8,128)(2,1)}, f32[48,768]{1,0:T(8,128)}) custom-call(bf16[256,768]{1,0:T(8,128)(2,1)} %refs_0_.1, bf16[256,768]{1,0:T(8,128)(2,1)} %refs_1_.1, s32[2]{0:T(128)} %refs_2_.1, f32[768]{0:T(1024)} %refs_3_.1, ...), custom_call_target="tpu_custom_call" | custom-call | tf_op jit(solution)/shard_map/pallas_call | solution.py:1372
  112.9 9.3 %shard_map.204 = (bf16[256,768]{1,0:T(8,128)(2,1)}, f32[256,768]{1,0:T(8,128)}, f32[768]{0:T(1024)}, f32[3352,768]{1,0:T(8,128)}, f32[4,1792]{1,0:T(4,128)}, /*i...) custom-call(bf16[256,768]{1,0:T(8,128)(2,1)} %get-tuple-element.27.b, ...), custom_call_target="tpu_custom_call" | custom-call | tf_op jit(solution)/shard_map/pallas_call | solution.py:1467

commit v7 on v5

--- a/solution.py
+++ b/solution.py
@@ -852,9 +852,9 @@
     pieces = lax.axis_size("seq")
     chips = pieces // SEQS
     barrier = pltpu.get_barrier_semaphore()
-    peers = [partner(d) for d in ("c", "x", "y", "z1", "z2")]
+    peers = [partner("c"), partner("x")]
     peers += [((place // SEQS + k) % chips * SEQS + place % SEQS, core) for k in range(1, chips)]
-    peers += [block_at(1), block_at(-1)]
+    peers += [block_at(2 * core - 1)]
     for to in peers:
         pl.semaphore_signal(barrier, inc=1, device_id=to, device_id_type=MESH)
     return barrier, len(peers)

time: 123 us -> 123 us (level)
  no operation moved by 1% of the time
where the time goes in v7:
time: 123 us
  Pallas kernels  122 us (99%)
    pallas_call x1, Pallas kernels, whole(): pl.pallas_call(partial(whole_kernel, names), out_shape=[jax.ShapeDtypeStr...  112 us
    pallas_call x1, Pallas kernels, finish(): pl.pallas_call(finish_kernel, out_shape=[jax.ShapeDtypeStruct(s, bf16 if...  9.31 us

profile of v7, /device:TPU:0, one launch (start us, length us, event | category | flops | bytes accessed | tf_op | source)
XLA Modules:
  0.0 122.6 jit_solution(310640472363443106)
XLA Ops:
  0.6 112.4 %shard_map.203 = (bf16[256,768]{1,0:T(8,128)(2,1)}, f32[256,768]{1,0:T(8,128)}, bf16[3072,768]{1,0:T(8,128)(2,1)}, bf16[1792,768]{1,0:T(8,128)(2,1)}, f32[48,768]{1,0:T(8,128)}) custom-call(bf16[256,768]{1,0:T(8,128)(2,1)} %refs_0_.1, bf16[256,768]{1,0:T(8,128)(2,1)} %refs_1_.1, s32[2]{0:T(128)} %refs_2_.1, f32[768]{0:T(1024)} %refs_3_.1, ...), custom_call_target="tpu_custom_call" | custom-call | tf_op jit(solution)/shard_map/pallas_call | solution.py:1376
  113.1 9.3 %shard_map.204 = (bf16[256,768]{1,0:T(8,128)(2,1)}, f32[256,768]{1,0:T(8,128)}, f32[768]{0:T(1024)}, f32[3352,768]{1,0:T(8,128)}, f32[4,1792]{1,0:T(4,128)}, /*i...) custom-call(bf16[256,768]{1,0:T(8,128)(2,1)} %get-tuple-element.27.b, ...), custom_call_target="tpu_custom_call" | custom-call | tf_op jit(solution)/shard_map/pallas_call | solution.py:1471
